TPU v7x, 512 devices: a whole 4x8x8 slice. The times are simulated.
512 devices in a mesh: gx: 16 (over y_lo, x), gy: 16 (over z, core), gz: 2 (over y_hi).
Axes of the slice: x: 4, y: 8 (y_hi: 2, y_lo: 4; y = y_hi * 4 + y_lo), z: 8, core: 2. Of those that a mesh axis runs over, the one named last changes fastest.
Arguments:
- droplets: float32 [2, 16, 16, 8, 8192], P('gz', 'gx', 'gy'), as said below
- cell_index: int32 [2, 16, 16, 8192], P('gz', 'gx', 'gy'), may hold values from 0 to 16383
- crossing: int32 [2, 16, 16, 4, 512], P('gz', 'gx', 'gy'), may hold values from 0 to 8191, as said below
- crossing_count: int32 [2, 16, 16, 4], P('gz', 'gx', 'gy'), may hold values from 128 to 512, as said below
- saturation: float32 [128, 16, 16, 256], P('gz', 'gx', 'gy'), may hold values from -4 to 4
- velocity: float32 [128, 16, 16, 256], P('gz', 'gx', 'gy'), may hold values from -6 to 6
- pressure: float32 [128, 16, 16, 256], P('gz', 'gx', 'gy'), may hold values from -6 to 6
- block_inverse: float32 [4, 128], replicated
- forward_map: float32 [4, 128], replicated
- backward_map: float32 [4, 128], replicated
Outputs:
- residents: float32 [2, 16, 16, 8, 8192], P('gz', 'gx', 'gy')
- arrivals: float32 [2, 16, 16, 4, 8, 512], P('gz', 'gx', 'gy')
- new_velocity: float32 [128, 16, 16, 256], P('gz', 'gx', 'gy')
- new_pressure: float32 [128, 16, 16, 256], P('gz', 'gx', 'gy')
Inputs may be any that keep to these rules, and one draw needn't show every extreme that they name: `droplets`: multiplicity (value 1) is positive and radius (value 0) at least 0.5 in every record. `crossing`: indices into the tile's droplets; no droplet appears twice among a tile's four faces, padding slots included. `crossing_count`: some face of every tile uses all 512 slots.
All inputs are finite; a program needn't handle non-finite values.
Results may differ from a plain program's by a relative error of at most 0.0003.
Values sent between devices are 32-bit elements; how exact they have to be, the bound alone decides.
No kernel may reach another device: no remote copies, remote signals or barrier semaphores. Data moves between devices by JAX's collectives and lax.ppermute only.
A program may use at most 64 MiB of HBM per device.

v0:
```python
import math

import jax
import jax.numpy as jnp
from jax import lax
from jax.sharding import PartitionSpec as P

CX = 8
CY = 32


GROW = 0.4
CURVATURE = 0.05
FLOOR_SQ = 0.09
BUOYANCY = 0.5
EXACT = lax.Precision.HIGHEST


def shifted(value, axis, steps):
    count = lax.axis_size(axis)
    pairs = [(source, (source + steps) % count) for source in range(count)]
    return lax.ppermute(value, axis, pairs)


def compose(latter, former):
    return jnp.stack(
        [
            latter[0] * former[0] + latter[1] * former[2],
            latter[0] * former[1] + latter[1] * former[3],
            latter[2] * former[0] + latter[3] * former[2],
            latter[2] * former[1] + latter[3] * former[3],
        ]
    )


def apply_pair(matrix, vector):
    return jnp.stack(
        [
            matrix[0] * vector[0] + matrix[1] * vector[1],
            matrix[2] * vector[0] + matrix[3] * vector[1],
        ]
    )


def linear_scan(matrices, vectors):

    def combine(former, latter):
        return (compose(latter[0], former[0]), apply_pair(latter[0], former[1]) + latter[1])

    return lax.associative_scan(combine, (matrices, vectors), axis=1)


def one_hot_of(index, width, dtype):
    return (index[:, None] == lax.broadcasted_iota(jnp.int32, (1, width), 1)).astype(dtype)


def read_cells(field, cell_ids):
    level_count, column_count = field.shape
    total = cell_ids.shape[0]
    block_rows = math.gcd(total, 2048)

    def read_one_block(ids_block):
        levels = one_hot_of(ids_block // column_count, level_count, jnp.float32)
        rows = jnp.dot(levels, field, precision=EXACT, preferred_element_type=jnp.float32)
        return jnp.sum(
            rows * one_hot_of(ids_block % column_count, column_count, jnp.float32), axis=1
        )

    return lax.map(read_one_block, cell_ids.reshape(-1, block_rows)).reshape(-1)


def add_cells(values, cell_ids, level_count, column_count):
    total = cell_ids.shape[0]
    block_rows = math.gcd(total, 2048)

    def add_one_block(carried, inputs):
        ids_block, value_block = inputs
        levels = (
            one_hot_of(ids_block // column_count, level_count, jnp.float32) * value_block[:, None]
        )
        columns = one_hot_of(ids_block % column_count, column_count, jnp.float32)
        return (
            carried
            + jnp.einsum(
                "nl,nc->lc", levels, columns, precision=EXACT, preferred_element_type=jnp.float32
            ),
            None,
        )

    start = jnp.zeros((level_count, column_count), jnp.float32)
    summed, _ = lax.scan(
        add_one_block, start, (cell_ids.reshape(-1, block_rows), values.reshape(-1, block_rows))
    )
    return summed


def condense(records, excess, occupied):
    radius = jnp.where(occupied, records[..., 0, :], 1.0)
    dry_radius = records[..., 2, :]
    solute = records[..., 3, :]
    radius_cubed = radius * radius * radius
    squared = jnp.maximum(
        radius * radius
        + GROW
        * (
            excess
            - CURVATURE / radius
            + solute * dry_radius * dry_radius * dry_radius / radius_cubed
        ),
        FLOOR_SQ,
    )
    grown_radius = jnp.sqrt(squared)
    condensed = jnp.where(
        occupied,
        records[..., 1, :] * (grown_radius * grown_radius * grown_radius - radius_cubed),
        0.0,
    )
    updated = jnp.concatenate([grown_radius[..., None, :], records[..., 1:, :]], axis=-2)
    updated = jnp.where(occupied[..., None, :], updated, 0.0)
    return (updated, condensed)


def emit_packets(records, cell_ids, leavers, live_count, width_x, width_y):
    record_width, drop_count = records.shape
    slot_count = leavers.shape[1]
    slot_ids = lax.broadcasted_iota(jnp.int32, (4, slot_count), 1)
    face_ids = lax.broadcasted_iota(jnp.int32, (4, slot_count), 0)
    in_use = slot_ids < live_count[:, None]
    inner = min(128, drop_count)
    outer = drop_count // inner
    table = jnp.concatenate([records, cell_ids.astype(jnp.float32)[None, :]], axis=0).reshape(
        record_width + 1, outer, inner
    )
    flat_leavers = leavers.reshape(-1)
    flat_use = in_use.reshape(-1).astype(jnp.bfloat16)
    block_rows = math.gcd(4 * slot_count, 1024)

    def pick_block(inputs):
        ids_block, use_block = inputs
        upper = one_hot_of(ids_block // inner, outer, jnp.float32)
        lower = one_hot_of(ids_block % inner, inner, jnp.float32)
        rows = jnp.einsum(
            "nh,rhl->nrl", upper, table, precision=EXACT, preferred_element_type=jnp.float32
        )
        picked_block = jnp.sum(rows * lower[:, None, :], axis=2)
        upper_used = upper.astype(jnp.bfloat16) * use_block[:, None]
        counts = jnp.einsum(
            "nh,nl->hl", upper_used, lower.astype(jnp.bfloat16), preferred_element_type=jnp.float32
        )
        return (picked_block, counts)

    picked_blocks, count_blocks = lax.map(
        pick_block, (flat_leavers.reshape(-1, block_rows), flat_use.reshape(-1, block_rows))
    )
    picked_all = picked_blocks.reshape(4, slot_count, record_width + 1)
    departed = jnp.sum(count_blocks, axis=0).reshape(-1)
    picked = jnp.moveaxis(picked_all[:, :, :record_width], 2, 1)
    source = (picked_all[:, :, record_width] + 0.5).astype(jnp.int32)
    height = source // (width_x * width_y)
    cell_x = source // width_y % width_x
    cell_y = source % width_y
    new_x = jnp.where(face_ids == 0, 0, jnp.where(face_ids == 1, width_x - 1, cell_x))
    new_y = jnp.where(face_ids == 2, 0, jnp.where(face_ids == 3, width_y - 1, cell_y))
    target = height * (width_x * width_y) + new_x * width_y + new_y
    packet = jnp.concatenate([picked, target.astype(records.dtype)[:, None, :]], axis=1)
    packet = jnp.where(in_use[:, None, :], packet, 0.0)
    return (packet, departed == 0.0)


def settle(records, cell_ids, staying, packet_in, sat_tile, vel_tile, pres_tile):
    level_count, column_count = sat_tile.shape
    record_width = records.shape[0]
    incoming = packet_in[:, :record_width]
    target = (packet_in[:, record_width] + 0.5).astype(jnp.int32)
    occupied = incoming[:, 1] > 0
    all_ids = jnp.concatenate([cell_ids, target.reshape(-1)])
    excess = read_cells(sat_tile, all_ids)
    drop_count = cell_ids.shape[0]
    resident, res_mass = condense(records, excess[:drop_count], staying)
    arrived, arr_mass = condense(incoming, excess[drop_count:].reshape(target.shape), occupied)
    heating = add_cells(
        jnp.concatenate([res_mass, arr_mass.reshape(-1)]), all_ids, level_count, column_count
    )
    forcing = jnp.stack([vel_tile + BUOYANCY * heating, pres_tile])
    return (resident, arrived, forcing)


def along_x(packet_face, offset):
    return shifted(packet_face, "gx", offset)


def along_y(packet_face, offset):
    return shifted(packet_face, "gy", offset)


def solve_whole(columns, block_inverse, forward_map, backward_map):
    driven = apply_pair(block_inverse[:, :, None], columns)
    _, upward = linear_scan(forward_map[:, :, None], driven)
    _, downward = linear_scan(backward_map[:, ::-1, None], upward[:, ::-1])
    return downward[:, ::-1]


def body(
    droplets,
    cell_index,
    crossing,
    crossing_count,
    saturation,
    velocity,
    pressure,
    block_inverse,
    forward_map,
    backward_map,
):
    records = droplets[0, 0, 0]
    cell_ids = cell_index[0, 0, 0]
    sat_tile = saturation[:, 0, 0, :]
    packet, staying = emit_packets(
        records, cell_ids, crossing[0, 0, 0], crossing_count[0, 0, 0], CX, CY
    )
    from_west = along_x(packet[0], 1)
    from_east = along_x(packet[1], -1)
    from_south = along_y(packet[2], 1)
    from_north = along_y(packet[3], -1)
    packet_in = jnp.stack([from_west, from_east, from_south, from_north])
    resident, arrived, forcing = settle(
        records, cell_ids, staying, packet_in, sat_tile, velocity[:, 0, 0, :], pressure[:, 0, 0, :]
    )
    columns = lax.all_to_all(forcing, "gz", split_axis=2, concat_axis=1, tiled=True)
    solved = solve_whole(columns, block_inverse, forward_map, backward_map)
    result = lax.all_to_all(solved, "gz", split_axis=1, concat_axis=2, tiled=True)
    new_velocity = result[0][:, None, None, :]
    new_pressure = result[1][:, None, None, :]
    return (resident[None, None, None], arrived[None, None, None], new_velocity, new_pressure)


def solution(mesh):
    return jax.shard_map(
        body,
        mesh=mesh,
        in_specs=(
            P("gz", "gx", "gy", None, None),
            P("gz", "gx", "gy", None),
            P("gz", "gx", "gy", None, None),
            P("gz", "gx", "gy", None),
            P("gz", "gx", "gy", None),
            P("gz", "gx", "gy", None),
            P("gz", "gx", "gy", None),
            P(),
            P(),
            P(),
        ),
        out_specs=(
            P("gz", "gx", "gy", None, None),
            P("gz", "gx", "gy", None, None, None),
            P("gz", "gx", "gy", None),
            P("gz", "gx", "gy", None),
        ),
        check_vma=False,
    )
```

profile of v0, /device:TPU:8, one launch (start us, length us, event | category | flops | bytes accessed | tf_op | source)
XLA Modules:
  0.0 108.3 jit_solution(13891839763500059318)
XLA Ops:
  0.7 1.0 copy.93
  1.8 0.5 broadcast.1150
  2.3 0.7 reduce.5
  3.2 6.9 %while.39 = (s32[]{:T(128)}, f32[2,1024,9]{1,0,2:T(2,128)S(1)}, f32[2,64,128]{2,1,0:T(8,128)S(1)}, s32[2,1024]{1,0:T(2,128)S(1)}, f32[9,64,128]{2,1,0:T(8,128)S(...) while((s32[]{:T(128)}, f32[2,1024,9]{1,0,2:T(2,128)S(1)}, f32[2,64,128]{2,1,0:T(8,128)S(1)}, ...), condition=%wide.region_2.3_spmd, body=%wide.region_0.2_spmd.sunk | while | flops 926296064 | bytes 1603685 | solution.py:152
  3.3 0.2 fusion.96
  3.6 2.3 %multiply_reduce_fusion.2 = f32[1024,9]{0,1:T(8,128)S(1)} fusion(f32[1024,128]{0,1:T(8,128)S(1)} %fusion.95, f32[9,64,128]{2,1,0:T(8,128)S(1)} %get-tuple-element.595, s32[1024]{0:T(1024)S(1)} %get-tuple-element.562), kind=kOutput, calls=%fused_computation.34.clone.1 | convolution fusion | flops 908385280 | bytes 860160 | tf_op jit(solution)/shard_map/while/body/eval_jaxpr/nh,rhl->nrl/dot_general | solution.py:142
  5.9 0.7 dynamic_update_slice.26
  6.7 0.2 fusion.96
  7.0 2.3 %multiply_reduce_fusion.2 = f32[1024,9]{0,1:T(8,128)S(1)} fusion(f32[1024,128]{0,1:T(8,128)S(1)} %fusion.95, f32[9,64,128]{2,1,0:T(8,128)S(1)} %get-tuple-element.595, s32[1024]{0:T(1024)S(1)} %get-tuple-element.562), kind=kOutput, calls=%fused_computation.34.clone.1 | convolution fusion | flops 908385280 | bytes 860160 | tf_op jit(solution)/shard_map/while/body/eval_jaxpr/nh,rhl->nrl/dot_general | solution.py:142
  9.3 0.7 dynamic_update_slice.26
  10.4 3.4 %collective-permute-start = (f32[9,512]{1,0:T(8,128)S(1)}, f32[9,512]{1,0:T(8,128)S(1)}, u32[]{:S(2)}, u32[]{:S(2)}) collective-permute-start(f32[9,512]{1,0:T(8,128)S(1)} %bitcast.379), channel_id=1, source_target_pairs={{0,32},{32,64},{64,96},{96,128},{128,160},{160,192},{192,224},{224... | collective-permute-start | bytes 55304 | tf_op jit(solution)/shard_map/ppermute | solution.py:22
  13.9 4.5 %collective-permute-start.1 = (f32[9,512]{1,0:T(8,128)S(1)}, f32[9,512]{1,0:T(8,128)S(1)}, u32[]{:S(2)}, u32[]{:S(2)}) collective-permute-start(f32[9,512]{1,0:T(8,128)S(1)} %bitcast.380), channel_id=1, source_target_pairs={{0,480},{32,0},{64,32},{96,64},{128,96},{160,128},{192,160},{224,1... | collective-permute-start | bytes 55304 | tf_op jit(solution)/shard_map/ppermute | solution.py:22
  18.5 7.9 %collective-permute-start.3 = (f32[9,512]{1,0:T(8,128)S(1)}, f32[9,512]{1,0:T(8,128)S(1)}, u32[]{:S(2)}, u32[]{:S(2)}) collective-permute-start(f32[9,512]{1,0:T(8,128)S(1)} %bitcast.382), channel_id=1, source_target_pairs={{0,30},{2,0},{4,2},{6,4},{8,6},{10,8},{12,10},{14,12},{16,14},{18,... | collective-permute-start | bytes 55304 | tf_op jit(solution)/shard_map/ppermute | solution.py:22
  31.1 0.6 slice.1400
  31.8 0.6 slice.1426
  32.4 0.6 slice.1428
  33.0 0.6 slice.1429
  33.6 0.6 slice.1548
  34.2 0.6 slice.1574
  34.8 0.6 slice.1576
  35.4 0.6 slice.1577
  36.3 0.6 slice.1416
  36.9 0.6 slice.1420
  37.5 0.6 slice.1422
  38.1 0.6 slice.1423
  38.7 0.6 slice.1564
  39.3 0.6 slice.1568
  39.9 0.6 slice.1570
  40.6 0.6 slice.1571
  41.3 9.7 %while.40 = (s32[]{:T(128)}, f32[5,2048]{1,0:T(8,128)S(1)}, s32[5,2048]{1,0:T(8,128)S(1)}, f32[64,256]{1,0:T(8,128)S(1)}, s32[]{:T(128)}, /*index=5*/s32[]{:T(128)}) while((s32[]{:T(128)}, f32[5,2048]{1,0:T(8,128)S(1)}, s32[5,2048]{1,0:T(8,128)S(1)}, f32[64,256]{1,0:T(8,128)S(1)}, s32[]{:T(128)}, /*index=5*/s32[]{:T(128)}) %tuple.250), condition=%wide.region_6.7_spmd, body=%wide.region_4.6_spmd.sunk | while | flops 404393984 | bytes 147533 | solution.py:69
  41.4 1.7 %fusion.98 = f32[2048]{0:T(1024)S(1)} fusion(f32[64,256]{1,0:T(8,128)S(1)} %get-tuple-element.614, s32[2048]{0:T(1024)S(1)} %get-tuple-element.567, s32[2048]{0:T(1024)S(1)} %get-tuple-element.568), kind=kOutput, calls=%fused_computation.2.clone.1 | convolution fusion | flops 404355072 | bytes 90112 | tf_op jit(solution)/shard_map/while/body/eval_jaxpr/dot_general | solution.py:64
  43.0 0.2 dynamic_update_slice.27
  43.3 1.7 %fusion.98 = f32[2048]{0:T(1024)S(1)} fusion(f32[64,256]{1,0:T(8,128)S(1)} %get-tuple-element.614, s32[2048]{0:T(1024)S(1)} %get-tuple-element.567, s32[2048]{0:T(1024)S(1)} %get-tuple-element.568), kind=kOutput, calls=%fused_computation.2.clone.1 | convolution fusion | flops 404355072 | bytes 90112 | tf_op jit(solution)/shard_map/while/body/eval_jaxpr/dot_general | solution.py:64
  45.0 0.2 dynamic_update_slice.27
  45.2 1.7 %fusion.98 = f32[2048]{0:T(1024)S(1)} fusion(f32[64,256]{1,0:T(8,128)S(1)} %get-tuple-element.614, s32[2048]{0:T(1024)S(1)} %get-tuple-element.567, s32[2048]{0:T(1024)S(1)} %get-tuple-element.568), kind=kOutput, calls=%fused_computation.2.clone.1 | convolution fusion | flops 404355072 | bytes 90112 | tf_op jit(solution)/shard_map/while/body/eval_jaxpr/dot_general | solution.py:64
  46.9 0.2 dynamic_update_slice.27
  47.2 1.7 %fusion.98 = f32[2048]{0:T(1024)S(1)} fusion(f32[64,256]{1,0:T(8,128)S(1)} %get-tuple-element.614, s32[2048]{0:T(1024)S(1)} %get-tuple-element.567, s32[2048]{0:T(1024)S(1)} %get-tuple-element.568), kind=kOutput, calls=%fused_computation.2.clone.1 | convolution fusion | flops 404355072 | bytes 90112 | tf_op jit(solution)/shard_map/while/body/eval_jaxpr/dot_general | solution.py:64
  48.8 0.2 dynamic_update_slice.27
  49.1 1.7 %fusion.98 = f32[2048]{0:T(1024)S(1)} fusion(f32[64,256]{1,0:T(8,128)S(1)} %get-tuple-element.614, s32[2048]{0:T(1024)S(1)} %get-tuple-element.567, s32[2048]{0:T(1024)S(1)} %get-tuple-element.568), kind=kOutput, calls=%fused_computation.2.clone.1 | convolution fusion | flops 404355072 | bytes 90112 | tf_op jit(solution)/shard_map/while/body/eval_jaxpr/dot_general | solution.py:64
  51.2 10.0 %while.41 = (s32[]{:T(128)}, f32[64,256]{1,0:T(8,128)S(1)}, s32[5,2048]{1,0:T(8,128)S(1)}, f32[5,2048]{1,0:T(8,128)S(1)}, s32[]{:T(128)}, /*index=5*/s32[]{:T(128)}) while((s32[]{:T(128)}, f32[64,256]{1,0:T(8,128)S(1)}, s32[5,2048]{1,0:T(8,128)S(1)}, f32[5,2048]{1,0:T(8,128)S(1)}, s32[]{:T(128)}, /*index=5*/s32[]{:T(128)}) %tuple.249), condition=%wide.region_8.9_spmd.clone, body=%wide.region_7.8_spmd.clone.sunk | while | flops 403511296 | bytes 213079 | solution.py:91
  51.3 1.9 %fusion.100 = f32[64,256]{1,0:T(8,128)S(1)} fusion(s32[2048]{0:T(1024)S(1)} %get-tuple-element.573, f32[2048]{0:T(1024)S(1)} %bitcast.362, s32[2048]{0:T(1024)S(1)} %get-tuple-element.574, f32[64,256]{1,0:T(8,128)S(1)} %get-tuple-element.624, pred[]{:T(512)S(6)} %compare.91), kind=kOutput, calls=%fused_computation.16.clone.1 | convolution fusion | flops 403472384 | bytes 155649 | tf_op jit(solution)/shard_map/while/body/eval_jaxpr/nl,nc->lc/dot_general | solution.py:84
  53.3 1.9 %fusion.100 = f32[64,256]{1,0:T(8,128)S(1)} fusion(s32[2048]{0:T(1024)S(1)} %get-tuple-element.573, f32[2048]{0:T(1024)S(1)} %bitcast.362, s32[2048]{0:T(1024)S(1)} %get-tuple-element.574, f32[64,256]{1,0:T(8,128)S(1)} %get-tuple-element.624, pred[]{:T(512)S(6)} %compare.91), kind=kOutput, calls=%fused_computation.16.clone.1 | convolution fusion | flops 403472384 | bytes 155649 | tf_op jit(solution)/shard_map/while/body/eval_jaxpr/nl,nc->lc/dot_general | solution.py:84
  55.3 1.9 %fusion.100 = f32[64,256]{1,0:T(8,128)S(1)} fusion(s32[2048]{0:T(1024)S(1)} %get-tuple-element.573, f32[2048]{0:T(1024)S(1)} %bitcast.362, s32[2048]{0:T(1024)S(1)} %get-tuple-element.574, f32[64,256]{1,0:T(8,128)S(1)} %get-tuple-element.624, pred[]{:T(512)S(6)} %compare.91), kind=kOutput, calls=%fused_computation.16.clone.1 | convolution fusion | flops 403472384 | bytes 155649 | tf_op jit(solution)/shard_map/while/body/eval_jaxpr/nl,nc->lc/dot_general | solution.py:84
  57.3 1.9 %fusion.100 = f32[64,256]{1,0:T(8,128)S(1)} fusion(s32[2048]{0:T(1024)S(1)} %get-tuple-element.573, f32[2048]{0:T(1024)S(1)} %bitcast.362, s32[2048]{0:T(1024)S(1)} %get-tuple-element.574, f32[64,256]{1,0:T(8,128)S(1)} %get-tuple-element.624, pred[]{:T(512)S(6)} %compare.91), kind=kOutput, calls=%fused_computation.16.clone.1 | convolution fusion | flops 403472384 | bytes 155649 | tf_op jit(solution)/shard_map/while/body/eval_jaxpr/nl,nc->lc/dot_general | solution.py:84
  59.3 1.9 %fusion.100 = f32[64,256]{1,0:T(8,128)S(1)} fusion(s32[2048]{0:T(1024)S(1)} %get-tuple-element.573, f32[2048]{0:T(1024)S(1)} %bitcast.362, s32[2048]{0:T(1024)S(1)} %get-tuple-element.574, f32[64,256]{1,0:T(8,128)S(1)} %get-tuple-element.624, pred[]{:T(512)S(6)} %compare.91), kind=kOutput, calls=%fused_computation.16.clone.1 | convolution fusion | flops 403472384 | bytes 155649 | tf_op jit(solution)/shard_map/while/body/eval_jaxpr/nl,nc->lc/dot_general | solution.py:84
  61.4 0.3 fusion.78
  61.7 0.9 reshape.2137
  62.6 6.2 %all-to-all-start = ((f32[2,1,16384]{2,1,0:T(1,128)}), f32[2,1,16384]{2,1,0:T(1,128)S(1)}, u32[]{:S(2)}, u32[]{:S(2)}) async-start(f32[2,1,16384]{2,1,0:T(1,128)} %reshape.2137), calls=%async_computation | async-start | bytes 262144 | tf_op jit(solution)/shard_map/all_to_all | solution.py:229
  68.9 0.2 fusion.40
  69.1 0.8 maximum_select_fusion
  69.9 7.9 %all-to-all-done = f32[2,1,16384]{2,1,0:T(1,128)S(1)} async-done(((f32[2,1,16384]{2,1,0:T(1,128)}), f32[2,1,16384]{2,1,0:T(1,128)S(1)}, u32[]{:S(2)}, u32[]{:S(2)}) %all-to-all-start) | async-done | bytes 131104 | tf_op jit(solution)/shard_map/all_to_all | solution.py:229
  77.9 0.5 broadcast.1151
  78.4 1.0 reduce.6
  79.4 0.3 reshape.2138
  80.9 2.5 %multiply_add_fusion.81 = (f32[1,1,128]{2,1,0:T(1,128)S(1)}, f32[1,1,128]{2,1,0:T(1,128)S(1)}) fusion(f32[2,2,128]{2,1,0:T(2,128)S(1)} %maximum_add_fusion.21, f32[]{:T(128)} %bitcast.76, f32[]{:T(128)} %bitcast.75, f32[]{:T(128)} %bitcast.78, f32[]{:T(128)} %bitcast.77), kind=kLoop, calls=%fused_computation.359 | loop fusion | flops 768 | bytes 2064 | tf_op jit(solution)/shard_map/add | solution.py:39
  83.4 2.5 %multiply_add_fusion.77 = (f32[1,1,128]{2,1,0:T(1,128)S(1)}, f32[1,1,128]{2,1,0:T(1,128)S(1)}) fusion(f32[]{:T(128)} %bitcast.79, f32[]{:T(128)} %bitcast.70, f32[2,1,128]{2,1,0:T(1,128)S(1)} %get-tuple-element.444, f32[2,1,128]{2,1,0:T(1,128)S(1)} %get-tuple-element.445, f32[]{:T(128)} %bitcast.81, f32[]{:T(128)} %bitcast.80), kind=kLoop, calls=%fused_computation.355 | loop fusion | flops 1280 | bytes 3088 | tf_op jit(solution)/shard_map/add | solution.py:39
  88.0 2.5 %multiply_add_fusion.53 = (f32[1,1,128]{2,1,0:T(1,128)S(1)}, f32[1,1,128]{2,1,0:T(1,128)S(1)}) fusion(f32[2,2,128]{2,1,0:T(2,128)S(1)} %maximum_add_fusion.22, f32[]{:T(128)} %bitcast.129, f32[]{:T(128)} %bitcast.128, f32[]{:T(128)} %bitcast.131, f32[]{:T(128)} %bitcast.130), kind=kLoop, calls=%fused_computation.311 | loop fusion | flops 768 | bytes 2064 | tf_op jit(solution)/shard_map/add | solution.py:39
  90.5 2.5 %multiply_add_fusion.49 = (f32[1,1,128]{2,1,0:T(1,128)S(1)}, f32[1,1,128]{2,1,0:T(1,128)S(1)}) fusion(f32[]{:T(128)} %bitcast.132, f32[]{:T(128)} %bitcast.123, f32[2,1,128]{2,1,0:T(1,128)S(1)} %get-tuple-element.398, f32[2,1,128]{2,1,0:T(1,128)S(1)} %get-tuple-element.399, f32[]{:T(128)} %bitcast.134, f32[]{:T(128)} %bitcast.133), kind=kLoop, calls=%fused_computation.307 | loop fusion | flops 1280 | bytes 3088 | tf_op jit(solution)/shard_map/add | solution.py:39
  94.2 0.8 copy.38
  94.9 3.4 %all-to-all-start.1 = ((f32[2,128,128]{2,0,1:T(2,128)}), f32[2,128,128]{2,0,1:T(2,128)S(1)}, u32[]{:S(2)}, u32[]{:S(2)}) async-start(f32[2,128,128]{2,0,1:T(2,128)} %copy.38), calls=%async_computation.1 | async-start | bytes 262144 | tf_op jit(solution)/shard_map/all_to_all | solution.py:231
  98.3 0.7 maximum_select_fusion.2
  99.0 7.9 %all-to-all-done.1 = f32[2,128,128]{2,0,1:T(2,128)S(1)} async-done(((f32[2,128,128]{2,0,1:T(2,128)}), f32[2,128,128]{2,0,1:T(2,128)S(1)}, u32[]{:S(2)}, u32[]{:S(2)}) %all-to-all-start.1) | async-done | bytes 131104 | tf_op jit(solution)/shard_map/all_to_all | solution.py:231
  106.9 0.7 copy.40
  107.6 0.7 copy.41
  (346 shorter events, 10.3 us)
Async XLA Ops:
  0.6 1.1 %copy-start.1 = (s32[1,1,1,8192]{3,2,1,0:T(1,128)S(1)}, s32[1,1,1,8192]{3,2,1,0:T(1,128)}, u32[]{:S(2)}) copy-start(s32[1,1,1,8192]{3,2,1,0:T(1,128)} %param.17) | copy-start | bytes 98308
  0.6 1.6 %copy-start.9 = (s32[1,1,1,4]{3,2,1,0:T(1,128)S(1)}, s32[1,1,1,4]{3,2,1,0:T(1,128)}, u32[]{:S(2)}) copy-start(s32[1,1,1,4]{3,2,1,0:T(1,128)} %param.19) | copy-start | bytes 52
  0.7 2.5 %copy-start.6 = (s32[1,1,1,4,512]{4,3,2,1,0:T(4,128)S(1)}, s32[1,1,1,4,512]{4,3,2,1,0:T(4,128)}, u32[]{:S(2)}) copy-start(s32[1,1,1,4,512]{4,3,2,1,0:T(4,128)} %param.18) | copy-start | bytes 24580
  10.1 16.4 %copy-start.7 = (f32[4,128]{1,0:T(4,128)S(1)}, f32[4,128]{1,0:T(4,128)}, u32[]{:S(2)}) copy-start(f32[4,128]{1,0:T(4,128)} %param.25) | copy-start | bytes 6148
  10.1 18.0 %copy-start.5 = (f32[4,128]{1,0:T(4,128)S(1)}, f32[4,128]{1,0:T(4,128)}, u32[]{:S(2)}) copy-start(f32[4,128]{1,0:T(4,128)} %param.24) | copy-start | bytes 6148
  10.2 19.4 %copy-start = (f32[1,1,1,8,8192]{4,3,2,1,0:T(8,128)S(1)}, f32[1,1,1,8,8192]{4,3,2,1,0:T(8,128)}, u32[]{:S(2)}) copy-start(f32[1,1,1,8,8192]{4,3,2,1,0:T(8,128)} %param.16) | copy-start | bytes 786436
  10.4 20.6 %copy-start.8 = (f32[4,128]{1,0:T(4,128)S(1)}, f32[4,128]{1,0:T(4,128)}, u32[]{:S(2)}) copy-start(f32[4,128]{1,0:T(4,128)} %param.23) | copy-start | bytes 6148
  10.4 30.7 %collective-permute-start = (f32[9,512]{1,0:T(8,128)S(1)}, f32[9,512]{1,0:T(8,128)S(1)}, u32[]{:S(2)}, u32[]{:S(2)}) collective-permute-start(f32[9,512]{1,0:T(8,128)S(1)} %bitcast.379), channel_id=1, source_target_pairs={{0,32},{32,64},{64,96},{96,128},{128,160},{160,192},{192,224},{224... | collective-permute-start | bytes 55304 | tf_op jit(solution)/shard_map/ppermute | solution.py:22
  13.9 27.3 %collective-permute-start.1 = (f32[9,512]{1,0:T(8,128)S(1)}, f32[9,512]{1,0:T(8,128)S(1)}, u32[]{:S(2)}, u32[]{:S(2)}) collective-permute-start(f32[9,512]{1,0:T(8,128)S(1)} %bitcast.380), channel_id=1, source_target_pairs={{0,480},{32,0},{64,32},{96,64},{128,96},{160,128},{192,160},{224,1... | collective-permute-start | bytes 55304 | tf_op jit(solution)/shard_map/ppermute | solution.py:22
  18.4 22.8 %collective-permute-start.2 = (f32[9,512]{1,0:T(8,128)S(1)}, f32[9,512]{1,0:T(8,128)S(1)}, u32[]{:S(2)}, u32[]{:S(2)}) collective-permute-start(f32[9,512]{1,0:T(8,128)S(1)} %bitcast.381), channel_id=1, source_target_pairs={{0,2},{2,4},{4,6},{6,8},{8,10},{10,12},{12,14},{14,16},{16,18},{18... | collective-permute-start | bytes 55304 | tf_op jit(solution)/shard_map/ppermute | solution.py:22
  18.5 22.7 %collective-permute-start.3 = (f32[9,512]{1,0:T(8,128)S(1)}, f32[9,512]{1,0:T(8,128)S(1)}, u32[]{:S(2)}, u32[]{:S(2)}) collective-permute-start(f32[9,512]{1,0:T(8,128)S(1)} %bitcast.382), channel_id=1, source_target_pairs={{0,30},{2,0},{4,2},{6,4},{8,6},{10,8},{12,10},{14,12},{16,14},{18,... | collective-permute-start | bytes 55304 | tf_op jit(solution)/shard_map/ppermute | solution.py:22
  28.5 7.5 %copy-start.4 = (f32[64,1,1,256]{3,2,1,0:T(1,128)S(1)}, f32[64,1,1,256]{3,2,1,0:T(1,128)}, u32[]{:S(2)}) copy-start(f32[64,1,1,256]{3,2,1,0:T(1,128)} %param.20) | copy-start | bytes 196612
  29.5 6.5 %copy-start.2 = (f32[64,1,1,256]{3,2,1,0:T(1,128)S(1)}, f32[64,1,1,256]{3,2,1,0:T(1,128)}, u32[]{:S(2)}) copy-start(f32[64,1,1,256]{3,2,1,0:T(1,128)} %param.21) | copy-start | bytes 196612
  29.6 6.5 %copy-start.3 = (f32[64,1,1,256]{3,2,1,0:T(1,128)S(1)}, f32[64,1,1,256]{3,2,1,0:T(1,128)}, u32[]{:S(2)}) copy-start(f32[64,1,1,256]{3,2,1,0:T(1,128)} %param.22) | copy-start | bytes 196612
  62.6 15.3 %all-to-all-start = ((f32[2,1,16384]{2,1,0:T(1,128)}), f32[2,1,16384]{2,1,0:T(1,128)S(1)}, u32[]{:S(2)}, u32[]{:S(2)}) async-start(f32[2,1,16384]{2,1,0:T(1,128)} %reshape.2137), calls=%async_computation | async-start | bytes 262144 | tf_op jit(solution)/shard_map/all_to_all | solution.py:229
  94.9 12.0 %all-to-all-start.1 = ((f32[2,128,128]{2,0,1:T(2,128)}), f32[2,128,128]{2,0,1:T(2,128)S(1)}, u32[]{:S(2)}, u32[]{:S(2)}) async-start(f32[2,128,128]{2,0,1:T(2,128)} %copy.38), calls=%async_computation.1 | async-start | bytes 262144 | tf_op jit(solution)/shard_map/all_to_all | solution.py:231
where the time goes:
time: 109 us; the launch traced here: 108 us
  starting transfers between devices  25.5 us (23%)
  local copies, waits for them, and re-layouts  24.2 us (22%)
  matrix products  22.9 us (21%)
  other arithmetic  17 us (16%)
  waiting for transfers between devices  15.9 us (15%)
  between operations  2.16 us (2%)
    ppermute x4, starting transfers between devices, shifted(): return lax.ppermute(value, axis, pairs)  15.9 us
    add x27, other arithmetic, apply_pair(): matrix[0] * vector[0] + matrix[1] * vector[1]  11.9 us
    dot_general x5, matrix products, add_one_block(): jnp.einsum('nl,nc->lc', levels, columns, precision=EXACT, preferred_eleme...  9.57 us
    dot_general x5, matrix products, read_one_block(): jnp.dot(levels, field, precision=EXACT, preferred_element_type=jnp.float32)  8.3 us
    all_to_all x1, waiting for transfers between devices, body(): lax.all_to_all(forcing, 'gz', split_axis=2, concat_axis=1, tiled=True)  7.94 us
    all_to_all x1, waiting for transfers between devices, body(): lax.all_to_all(solved, 'gz', split_axis=1, concat_axis=2, tiled=True)  7.92 us
    all_to_all x1, starting transfers between devices, body(): lax.all_to_all(forcing, 'gz', split_axis=2, concat_axis=1, tiled=True)  6.18 us
    dot_general x2, matrix products, pick_block(): jnp.einsum('nh,rhl->nrl', upper, table, precision=EXACT, preferred_elemen...  4.59 us
  transfers between devices with their start and end apart: 6, of which 2 were waited for; matrix products, arithmetic and copies ran while one was open for 15% of the time, Pallas kernels for 0%

commit v1 on v0

--- a/solution.py
+++ b/solution.py
@@ -4,6 +4,8 @@
 import jax.numpy as jnp
 from jax import lax
 from jax.sharding import PartitionSpec as P
+from jax.experimental import pallas as pl
+from jax.experimental.pallas import tpu as pltpu
 
 CX = 8
 CY = 32
@@ -193,11 +195,116 @@
     return shifted(packet_face, "gy", offset)
 
 
-def solve_whole(columns, block_inverse, forward_map, backward_map):
-    driven = apply_pair(block_inverse[:, :, None], columns)
-    _, upward = linear_scan(forward_map[:, :, None], driven)
-    _, downward = linear_scan(backward_map[:, ::-1, None], upward[:, ::-1])
-    return downward[:, ::-1]
+def solve_kernel(
+    off_ref, maps_ref, fv_ref, fp_ref, sv_ref, sp_ref, last_ref, first_ref, ex_ref, xv_ref, xp_ref
+):
+    levels = fv_ref.shape[0]
+    off = off_ref[0]
+    upper = jnp.where(off > 0, 1.0, 0.0).astype(jnp.float32)
+    lane = lax.broadcasted_iota(jnp.int32, (1, 128), 1)
+    e0 = jnp.where(lane == 0, 1.0, 0.0).astype(jnp.float32)
+    e1 = jnp.where(lane == 1, 1.0, 0.0).astype(jnp.float32)
+    zero = jnp.zeros(fv_ref.shape[1:], jnp.float32)[None, :]
+
+    def forward(k, carry):
+        uv, up, xv, xp = carry
+        level = off + k
+        b0 = maps_ref[0, level]
+        b1 = maps_ref[1, level]
+        b2 = maps_ref[2, level]
+        b3 = maps_ref[3, level]
+        f0 = maps_ref[4, level]
+        f1 = maps_ref[5, level]
+        f2 = maps_ref[6, level]
+        f3 = maps_ref[7, level]
+        gv = fv_ref[pl.ds(k, 1), :]
+        gp = fp_ref[pl.ds(k, 1), :]
+        nuv = (b0 * gv + b1 * gp) + (f0 * uv + f1 * up)
+        nup = (b2 * gv + b3 * gp) + (f2 * uv + f3 * up)
+        nxv = f0 * xv + f1 * xp
+        nxp = f2 * xv + f3 * xp
+        sv_ref[pl.ds(k, 1), :] = nuv
+        sp_ref[pl.ds(k, 1), :] = nup
+        xv_ref[pl.ds(k, 1), :] = nxv
+        xp_ref[pl.ds(k, 1), :] = nxp
+        return (nuv, nup, nxv, nxp)
+
+    uv, up, xv, xp = lax.fori_loop(
+        0, levels, forward, (zero, zero, upper * e0, upper * e1)
+    )
+    last_ref[0:1, :] = uv
+    last_ref[1:2, :] = up
+    last_ref[2:4, :] = jnp.zeros((2, uv.shape[1]), jnp.float32)
+    last_ref[2:3, 0:128] = xv
+    last_ref[3:4, 0:128] = xp
+
+    def backward(step, carry):
+        sv, sp, yv, yp = carry
+        k = levels - 1 - step
+        level = off + k
+        c0 = maps_ref[8, level]
+        c1 = maps_ref[9, level]
+        c2 = maps_ref[10, level]
+        c3 = maps_ref[11, level]
+        nsv = sv_ref[pl.ds(k, 1), :] + (c0 * sv + c1 * sp)
+        nsp = sp_ref[pl.ds(k, 1), :] + (c2 * sv + c3 * sp)
+        nyv = xv_ref[pl.ds(k, 1), :] + (c0 * yv + c1 * yp)
+        nyp = xp_ref[pl.ds(k, 1), :] + (c2 * yv + c3 * yp)
+        sv_ref[pl.ds(k, 1), :] = nsv
+        sp_ref[pl.ds(k, 1), :] = nsp
+        ex_ref[0, pl.ds(k, 1), :] = nyv
+        ex_ref[1, pl.ds(k, 1), :] = nyp
+        return (nsv, nsp, nyv, nyp)
+
+    lower = 1.0 - upper
+    sv, sp, yv, yp = lax.fori_loop(
+        0, levels, backward, (zero, zero, lower * e0, lower * e1)
+    )
+    first_ref[0:1, :] = sv
+    first_ref[1:2, :] = sp
+    first_ref[2:4, :] = jnp.zeros((2, sv.shape[1]), jnp.float32)
+    first_ref[2:3, 0:128] = yv
+    first_ref[3:4, 0:128] = yp
+
+
+def solve_local(forcing, block_inverse, forward_map, backward_map):
+    _, levels, columns = forcing.shape
+    offset = jnp.full((1,), lax.axis_index("gz") * levels, jnp.int32)
+    maps = jnp.concatenate([block_inverse, forward_map, backward_map], axis=0)
+    smem = pl.BlockSpec(memory_space=pltpu.SMEM)
+    vmem = pl.BlockSpec(memory_space=pltpu.VMEM)
+    return pl.pallas_call(
+        solve_kernel,
+        out_shape=(
+            jax.ShapeDtypeStruct((levels, columns), jnp.float32),
+            jax.ShapeDtypeStruct((levels, columns), jnp.float32),
+            jax.ShapeDtypeStruct((4, columns), jnp.float32),
+            jax.ShapeDtypeStruct((4, columns), jnp.float32),
+            jax.ShapeDtypeStruct((2, levels, 128), jnp.float32),
+        ),
+        in_specs=[smem, smem, vmem, vmem],
+        out_specs=(vmem, vmem, vmem, vmem, vmem),
+        scratch_shapes=[
+            pltpu.VMEM((levels, 128), jnp.float32),
+            pltpu.VMEM((levels, 128), jnp.float32),
+        ],
+        cost_estimate=pl.CostEstimate(
+            flops=40 * levels * columns, bytes_accessed=24 * levels * columns, transcendentals=0
+        ),
+    )(offset, maps, forcing[0], forcing[1])
+
+
+def solve_split(forcing, block_inverse, forward_map, backward_map):
+    assert lax.axis_size("gz") == 2
+    sv, sp, last, first, extra = solve_local(forcing, block_inverse, forward_map, backward_map)
+    lower = lax.axis_index("gz") == 0
+    message = jnp.where(lower, last, first)
+    received = lax.ppermute(message, "gz", [(0, 1), (1, 0)])
+    r0 = received[0] + received[2, 0] * last[0] + received[2, 1] * last[1]
+    r1 = received[1] + received[3, 0] * last[0] + received[3, 1] * last[1]
+    new_v = sv + extra[0, :, 0:1] * r0[None, :] + extra[0, :, 1:2] * r1[None, :]
+    new_p = sp + extra[1, :, 0:1] * r0[None, :] + extra[1, :, 1:2] * r1[None, :]
+    return new_v, new_p
 
 
 def body(
@@ -226,11 +333,9 @@
     resident, arrived, forcing = settle(
         records, cell_ids, staying, packet_in, sat_tile, velocity[:, 0, 0, :], pressure[:, 0, 0, :]
     )
-    columns = lax.all_to_all(forcing, "gz", split_axis=2, concat_axis=1, tiled=True)
-    solved = solve_whole(columns, block_inverse, forward_map, backward_map)
-    result = lax.all_to_all(solved, "gz", split_axis=1, concat_axis=2, tiled=True)
-    new_velocity = result[0][:, None, None, :]
-    new_pressure = result[1][:, None, None, :]
+    solved_v, solved_p = solve_split(forcing, block_inverse, forward_map, backward_map)
+    new_velocity = solved_v[:, None, None, :]
+    new_pressure = solved_p[:, None, None, :]
     return (resident[None, None, None], arrived[None, None, None], new_velocity, new_pressure)
 
 

time: 109 us -> 69.2 us (0.63)
  the two profiles are of different devices: /device:TPU:8 before, /device:TPU:32 now
where the time goes in v1:
time: 69.2 us; the launch traced here: 68.9 us
  matrix products  22.9 us (33%)
  starting transfers between devices  20 us (29%)
  local copies, waits for them, and re-layouts  7.84 us (11%)
  other arithmetic  7.69 us (11%)
  waiting for transfers between devices  5.15 us (7%)
  Pallas kernels  3.48 us (5%)
  between operations  1.17 us (2%)
    ppermute x4, starting transfers between devices, shifted(): return lax.ppermute(value, axis, pairs)  17.7 us
    dot_general x5, matrix products, add_one_block(): jnp.einsum('nl,nc->lc', levels, columns, precision=EXACT, preferred_eleme...  9.56 us
    dot_general x5, matrix products, read_one_block(): jnp.dot(levels, field, precision=EXACT, preferred_element_type=jnp.float32)  8.29 us
    ppermute x1, waiting for transfers between devices, solve_split(): received = lax.ppermute(message, 'gz', [(0, 1), (1, 0)])  5 us
    dot_general x2, matrix products, pick_block(): jnp.einsum('nh,rhl->nrl', upper, table, precision=EXACT, preferred_elemen...  4.59 us
    unnamed x45, local copies, waits for them, and re-layouts  3.76 us
    pallas_call x1, Pallas kernels, solve_local(): pl.pallas_call(solve_kernel, out_shape=(jax.ShapeDtypeStruct((levels, col...  3.48 us
    add x1, other arithmetic, solve_split(): r0 = received[0] + received[2, 0] * last[0] + received[2, 1] * last[1]  2.55 us
  transfers between devices with their start and end apart: 5, of which 2 were waited for; matrix products, arithmetic and copies ran while one was open for 5% of the time, Pallas kernels for 0%

profile of v1, /device:TPU:32, one launch (start us, length us, event | category | flops | bytes accessed | tf_op | source)
XLA Modules:
  0.0 68.9 jit_solution(188675496024828595)
XLA Ops:
  0.7 1.0 %copy.46 = f32[1,8,64,128]{3,2,1,0:T(8,128)S(1)} copy(f32[1,8,64,128]{3,1,2,0:T(8,128)} %bitcast.117) | data formatting | bytes 524288
  1.8 0.5 broadcast.698
  2.3 0.7 reduce.13
  2.9 0.1 lt.65
  3.0 0.1 broadcast_bitcast_fusion
  3.2 6.9 %while.39 = (s32[]{:T(128)}, f32[2,1024,9]{1,0,2:T(2,128)S(1)}, f32[2,64,128]{2,1,0:T(8,128)S(1)}, s32[2,1024]{1,0:T(2,128)S(1)}, f32[9,64,128]{2,1,0:T(8,128)S(...) while((s32[]{:T(128)}, f32[2,1024,9]{1,0,2:T(2,128)S(1)}, f32[2,64,128]{2,1,0:T(8,128)S(1)}, ...), condition=%wide.region_2.3_spmd, body=%wide.region_0.2_spmd.sunk | while | flops 926296064 | bytes 1603685 | solution.py:154
  3.3 0.2 fusion.86
  3.5 0.1 fusion.85
  3.6 2.3 %multiply_reduce_fusion.2 = f32[1024,9]{0,1:T(8,128)S(1)} fusion(f32[1024,128]{0,1:T(8,128)S(1)} %fusion.85, f32[9,64,128]{2,1,0:T(8,128)S(1)} %get-tuple-element.421, s32[1024]{0:T(1024)S(1)} %get-tuple-element.388), kind=kOutput, calls=%fused_computation.34.clone.1 | convolution fusion | flops 908385280 | bytes 860160 | tf_op jit(solution)/shard_map/while/body/eval_jaxpr/nh,rhl->nrl/dot_general | solution.py:144
  5.9 0.7 %dynamic_update_slice.26 = f32[2,1024,9]{1,0,2:T(2,128)S(1)} dynamic-update-slice(f32[2,1024,9]{1,0,2:T(2,128)S(1)} %get-tuple-element.410, f32[1,1024,9]{1,0,2:T(1,128)S(1)} %copy.55, s32[]{:T(128)} %get-tuple-element.409, s32[]{:T(128)} %constant.252.clone.1..sunk, s32[]{:T(128)} %constant.252.clone.1..sunk) | dynamic-update-slice | bytes 73732 | tf_op jit(solution)/shard_map/while/body/jit(dynamic_update_index_in_dim)/dynamic_update_slice | solution.py:154
  6.7 0.2 fusion.86
  6.9 0.1 fusion.85
  7.0 2.3 %multiply_reduce_fusion.2 = f32[1024,9]{0,1:T(8,128)S(1)} fusion(f32[1024,128]{0,1:T(8,128)S(1)} %fusion.85, f32[9,64,128]{2,1,0:T(8,128)S(1)} %get-tuple-element.421, s32[1024]{0:T(1024)S(1)} %get-tuple-element.388), kind=kOutput, calls=%fused_computation.34.clone.1 | convolution fusion | flops 908385280 | bytes 860160 | tf_op jit(solution)/shard_map/while/body/eval_jaxpr/nh,rhl->nrl/dot_general | solution.py:144
  9.3 0.7 %dynamic_update_slice.26 = f32[2,1024,9]{1,0,2:T(2,128)S(1)} dynamic-update-slice(f32[2,1024,9]{1,0,2:T(2,128)S(1)} %get-tuple-element.410, f32[1,1024,9]{1,0,2:T(1,128)S(1)} %copy.55, s32[]{:T(128)} %get-tuple-element.409, s32[]{:T(128)} %constant.252.clone.1..sunk, s32[]{:T(128)} %constant.252.clone.1..sunk) | dynamic-update-slice | bytes 73732 | tf_op jit(solution)/shard_map/while/body/jit(dynamic_update_index_in_dim)/dynamic_update_slice | solution.py:154
  10.1 0.0 copy-start.10
  10.1 0.0 copy-start.11
  10.1 0.1 reshape.627
  10.2 0.1 iota_compare_fusion.11
  10.3 0.1 fusion.47
  10.4 0.1 fusion.67
  10.4 0.0 copy-start.4
  10.5 3.4 %collective-permute-start = (f32[9,512]{1,0:T(8,128)S(1)}, f32[9,512]{1,0:T(8,128)S(1)}, u32[]{:S(2)}, u32[]{:S(2)}) collective-permute-start(f32[9,512]{1,0:T(8,128)S(1)} %bitcast.155), channel_id=1, source_target_pairs={{0,32},{32,64},{64,96},{96,128},{128,160},{160,192},{192,224},{224... | collective-permute-start | bytes 55304 | tf_op jit(solution)/shard_map/ppermute | solution.py:24
  13.9 6.4 %collective-permute-start.1 = (f32[9,512]{1,0:T(8,128)S(1)}, f32[9,512]{1,0:T(8,128)S(1)}, u32[]{:S(2)}, u32[]{:S(2)}) collective-permute-start(f32[9,512]{1,0:T(8,128)S(1)} %bitcast.156), channel_id=1, source_target_pairs={{0,480},{32,0},{64,32},{96,64},{128,96},{160,128},{192,160},{224,1... | collective-permute-start | bytes 55304 | tf_op jit(solution)/shard_map/ppermute | solution.py:24
  20.2 0.0 copy-start.5
  20.3 0.0 collective-permute-start.2
  20.3 7.9 %collective-permute-start.3 = (f32[9,512]{1,0:T(8,128)S(1)}, f32[9,512]{1,0:T(8,128)S(1)}, u32[]{:S(2)}, u32[]{:S(2)}) collective-permute-start(f32[9,512]{1,0:T(8,128)S(1)} %bitcast.158), channel_id=1, source_target_pairs={{0,30},{2,0},{4,2},{6,4},{8,6},{10,8},{12,10},{14,12},{16,14},{18,... | collective-permute-start | bytes 55304 | tf_op jit(solution)/shard_map/ppermute | solution.py:24
  28.2 0.1 fusion.66
  28.4 0.6 pad_maximum_fusion.9.maps_ref
  29.0 0.6 copy.47
  29.7 0.1 collective-permute-done.2
  29.8 0.0 collective-permute-done.3
  29.9 9.7 %while.40 = (s32[]{:T(128)}, f32[5,2048]{1,0:T(8,128)S(1)}, s32[5,2048]{1,0:T(8,128)S(1)}, f32[64,256]{1,0:T(8,128)S(1)}, s32[]{:T(128)}, /*index=5*/s32[]{:T(128)}) while((s32[]{:T(128)}, f32[5,2048]{1,0:T(8,128)S(1)}, s32[5,2048]{1,0:T(8,128)S(1)}, f32[64,256]{1,0:T(8,128)S(1)}, s32[]{:T(128)}, /*index=5*/s32[]{:T(128)}) %tuple.119), condition=%wide.region_6.7_spmd, body=%wide.region_4.6_spmd.sunk | while | flops 404393984 | bytes 147533 | solution.py:71
  30.0 1.7 %fusion.88 = f32[2048]{0:T(1024)S(1)} fusion(f32[64,256]{1,0:T(8,128)S(1)} %get-tuple-element.440, s32[2048]{0:T(1024)S(1)} %get-tuple-element.393, s32[2048]{0:T(1024)S(1)} %get-tuple-element.394), kind=kOutput, calls=%fused_computation.2.clone.1 | convolution fusion | flops 404355072 | bytes 90112 | tf_op jit(solution)/shard_map/while/body/eval_jaxpr/dot_general | solution.py:66
  31.6 0.2 dynamic_update_slice.27
  31.9 1.7 %fusion.88 = f32[2048]{0:T(1024)S(1)} fusion(f32[64,256]{1,0:T(8,128)S(1)} %get-tuple-element.440, s32[2048]{0:T(1024)S(1)} %get-tuple-element.393, s32[2048]{0:T(1024)S(1)} %get-tuple-element.394), kind=kOutput, calls=%fused_computation.2.clone.1 | convolution fusion | flops 404355072 | bytes 90112 | tf_op jit(solution)/shard_map/while/body/eval_jaxpr/dot_general | solution.py:66
  33.6 0.2 dynamic_update_slice.27
  33.8 1.7 %fusion.88 = f32[2048]{0:T(1024)S(1)} fusion(f32[64,256]{1,0:T(8,128)S(1)} %get-tuple-element.440, s32[2048]{0:T(1024)S(1)} %get-tuple-element.393, s32[2048]{0:T(1024)S(1)} %get-tuple-element.394), kind=kOutput, calls=%fused_computation.2.clone.1 | convolution fusion | flops 404355072 | bytes 90112 | tf_op jit(solution)/shard_map/while/body/eval_jaxpr/dot_general | solution.py:66
  35.5 0.2 dynamic_update_slice.27
  35.8 1.7 %fusion.88 = f32[2048]{0:T(1024)S(1)} fusion(f32[64,256]{1,0:T(8,128)S(1)} %get-tuple-element.440, s32[2048]{0:T(1024)S(1)} %get-tuple-element.393, s32[2048]{0:T(1024)S(1)} %get-tuple-element.394), kind=kOutput, calls=%fused_computation.2.clone.1 | convolution fusion | flops 404355072 | bytes 90112 | tf_op jit(solution)/shard_map/while/body/eval_jaxpr/dot_general | solution.py:66
  37.4 0.2 dynamic_update_slice.27
  37.7 1.7 %fusion.88 = f32[2048]{0:T(1024)S(1)} fusion(f32[64,256]{1,0:T(8,128)S(1)} %get-tuple-element.440, s32[2048]{0:T(1024)S(1)} %get-tuple-element.393, s32[2048]{0:T(1024)S(1)} %get-tuple-element.394), kind=kOutput, calls=%fused_computation.2.clone.1 | convolution fusion | flops 404355072 | bytes 90112 | tf_op jit(solution)/shard_map/while/body/eval_jaxpr/dot_general | solution.py:66
  39.4 0.2 dynamic_update_slice.27
  39.6 0.1 sqrt_bitcast_fusion
  39.9 10.0 %while.41 = (s32[]{:T(128)}, f32[64,256]{1,0:T(8,128)S(1)}, s32[5,2048]{1,0:T(8,128)S(1)}, f32[5,2048]{1,0:T(8,128)S(1)}, s32[]{:T(128)}, /*index=5*/s32[]{:T(128)}) while((s32[]{:T(128)}, f32[64,256]{1,0:T(8,128)S(1)}, s32[5,2048]{1,0:T(8,128)S(1)}, f32[5,2048]{1,0:T(8,128)S(1)}, s32[]{:T(128)}, /*index=5*/s32[]{:T(128)}) %tuple.118), condition=%wide.region_8.9_spmd.clone, body=%wide.region_7.8_spmd.clone.sunk | while | flops 403511296 | bytes 213079 | solution.py:93
  39.9 1.9 %fusion.90 = f32[64,256]{1,0:T(8,128)S(1)} fusion(s32[2048]{0:T(1024)S(1)} %get-tuple-element.399, f32[2048]{0:T(1024)S(1)} %bitcast.140, s32[2048]{0:T(1024)S(1)} %get-tuple-element.400, f32[64,256]{1,0:T(8,128)S(1)} %get-tuple-element.450, pred[]{:T(512)S(6)} %compare.63), kind=kOutput, calls=%fused_computation.16.clone.1 | convolution fusion | flops 403472384 | bytes 155649 | tf_op jit(solution)/shard_map/while/body/eval_jaxpr/nl,nc->lc/dot_general | solution.py:86
  41.9 1.9 %fusion.90 = f32[64,256]{1,0:T(8,128)S(1)} fusion(s32[2048]{0:T(1024)S(1)} %get-tuple-element.399, f32[2048]{0:T(1024)S(1)} %bitcast.140, s32[2048]{0:T(1024)S(1)} %get-tuple-element.400, f32[64,256]{1,0:T(8,128)S(1)} %get-tuple-element.450, pred[]{:T(512)S(6)} %compare.63), kind=kOutput, calls=%fused_computation.16.clone.1 | convolution fusion | flops 403472384 | bytes 155649 | tf_op jit(solution)/shard_map/while/body/eval_jaxpr/nl,nc->lc/dot_general | solution.py:86
  43.9 1.9 %fusion.90 = f32[64,256]{1,0:T(8,128)S(1)} fusion(s32[2048]{0:T(1024)S(1)} %get-tuple-element.399, f32[2048]{0:T(1024)S(1)} %bitcast.140, s32[2048]{0:T(1024)S(1)} %get-tuple-element.400, f32[64,256]{1,0:T(8,128)S(1)} %get-tuple-element.450, pred[]{:T(512)S(6)} %compare.63), kind=kOutput, calls=%fused_computation.16.clone.1 | convolution fusion | flops 403472384 | bytes 155649 | tf_op jit(solution)/shard_map/while/body/eval_jaxpr/nl,nc->lc/dot_general | solution.py:86
  45.9 1.9 %fusion.90 = f32[64,256]{1,0:T(8,128)S(1)} fusion(s32[2048]{0:T(1024)S(1)} %get-tuple-element.399, f32[2048]{0:T(1024)S(1)} %bitcast.140, s32[2048]{0:T(1024)S(1)} %get-tuple-element.400, f32[64,256]{1,0:T(8,128)S(1)} %get-tuple-element.450, pred[]{:T(512)S(6)} %compare.63), kind=kOutput, calls=%fused_computation.16.clone.1 | convolution fusion | flops 403472384 | bytes 155649 | tf_op jit(solution)/shard_map/while/body/eval_jaxpr/nl,nc->lc/dot_general | solution.py:86
  47.9 1.9 %fusion.90 = f32[64,256]{1,0:T(8,128)S(1)} fusion(s32[2048]{0:T(1024)S(1)} %get-tuple-element.399, f32[2048]{0:T(1024)S(1)} %bitcast.140, s32[2048]{0:T(1024)S(1)} %get-tuple-element.400, f32[64,256]{1,0:T(8,128)S(1)} %get-tuple-element.450, pred[]{:T(512)S(6)} %compare.63), kind=kOutput, calls=%fused_computation.16.clone.1 | convolution fusion | flops 403472384 | bytes 155649 | tf_op jit(solution)/shard_map/while/body/eval_jaxpr/nl,nc->lc/dot_general | solution.py:86
  49.9 0.6 bitcast_add_fusion.fv_ref
  50.5 3.5 %shard_map.129 = (f32[64,256]{1,0:T(8,128)}, f32[64,256]{1,0:T(8,128)}, f32[4,256]{1,0:T(4,128)}, f32[4,256]{1,0:T(4,128)}, f32[2,64,128]{2,1,0:T(8,128)}) custom-call(s32[1]{0:T(128)} %bitcast.24.off_ref, f32[12,128]{1,0:T(8,128)} %pad_maximum_fusion.9.maps_ref, f32[64,256]{1,0:T(8,128)} %bitcast_add_fusion.fv_ref, f32[64,256]{1,0:T(8,128)} %bitcast.139), custom_call_target="tpu_custom_call" | custom-call | flops 655360 | bytes 393216 | tf_op jit(solution)/shard_map/pallas_call | solution.py:276
  54.0 0.7 %broadcast_select_fusion = f32[4,256]{1,0:T(4,128)S(1)} fusion(f32[4,256]{1,0:T(4,128)} %get-tuple-element.208, f32[4,256]{1,0:T(4,128)} %get-tuple-element.209, pred[]{:T(512)S(6)} %eq.204), kind=kLoop, calls=%fused_computation.161 | loop fusion | flops 1024 | bytes 12289 | tf_op jit(solution)/shard_map/jit(_where)/select_n | solution.py:301
  54.7 2.3 %collective-permute-start.4 = (f32[4,256]{1,0:T(4,128)S(1)}, f32[4,256]{1,0:T(4,128)S(1)}, u32[]{:S(2)}, u32[]{:S(2)}) collective-permute-start(f32[4,256]{1,0:T(4,128)S(1)} %broadcast_select_fusion), channel_id=1, source_target_pairs={{0,1},{1,0},{2,3},{3,2},{4,5},{5,4},{6,7},{7,6},{8,9},{9,8},{10,11... | collective-permute-start | bytes 12296 | tf_op jit(solution)/shard_map/ppermute | solution.py:302
  57.1 0.1 slice.122
  57.2 0.2 fusion.38
  57.5 0.7 maximum_select_fusion.2
  58.1 0.8 %maximum_select_fusion = f32[1,1,1,8,8192]{4,3,2,1,0:T(8,128)} fusion(f32[1,1,1,7,8192]{4,3,2,1,0:T(8,128)S(1)} %slice.125, f32[1,1,1,1,8192]{4,3,2,1,0:T(1,128)S(1)} %fusion.38, pred[8192]{0:T(1024)(128)(4,1)S(1)} %bitcast.149), kind=kLoop, calls=%fused_computation.59 | loop fusion | flops 131072 | bytes 532480 | tf_op jit(solution)/shard_map/jit(_where)/select_n | solution.py:121
  58.9 0.2 slice_reduce_fusion.1
  59.1 5.0 %collective-permute-done.4 = f32[4,256]{1,0:T(4,128)S(1)} collective-permute-done((f32[4,256]{1,0:T(4,128)S(1)}, f32[4,256]{1,0:T(4,128)S(1)}, u32[]{:S(2)}, u32[]{:S(2)}) %collective-permute-start.4) | collective-permute-done | bytes 4128 | tf_op jit(solution)/shard_map/ppermute | solution.py:302
  64.1 0.7 fusion.68
  64.8 2.5 %fusion.65 = (f32[1,256]{1,0:T(1,128)S(1)}, f32[1,256]{1,0:T(1,128)S(1)}) fusion(f32[4,256]{1,0:T(4,128)S(1)} %collective-permute-done.4, f32[4,256]{1,0:T(4,128)S(1)} %copy-done.8, f32[]{:T(128)} %bitcast.35, f32[]{:T(128)} %bitcast.34, f32[]{:T(128)} %bitcast.38, f32[]{:T(128)} %bitcast.37), kind=kLoop, calls=%fused_computation.165 | loop fusion | flops 2048 | bytes 6160 | tf_op jit(solution)/shard_map/add | solution.py:303
  67.4 0.1 add_bitcast_fusion
  67.5 0.7 %copy.20 = f32[64,1,1,256]{3,2,1,0:T(1,128)} copy(f32[64,1,1,256]{3,0,2,1:T(8,128)S(1)} %get-tuple-element.297) | data formatting | bytes 131072
  68.2 0.7 %copy.21 = f32[64,1,1,256]{3,2,1,0:T(1,128)} copy(f32[64,1,1,256]{3,0,2,1:T(8,128)S(1)} %get-tuple-element.296) | data formatting | bytes 131072
  (95 shorter events, 0.9 us)
Async XLA Ops:
  0.6 1.1 %copy-start.2 = (s32[1,1,1,8192]{3,2,1,0:T(1,128)S(1)}, s32[1,1,1,8192]{3,2,1,0:T(1,128)}, u32[]{:S(2)}) copy-start(s32[1,1,1,8192]{3,2,1,0:T(1,128)} %param.17) | copy-start | bytes 98308
  0.6 1.6 %copy-start.13 = (s32[1,1,1,4]{3,2,1,0:T(1,128)S(1)}, s32[1,1,1,4]{3,2,1,0:T(1,128)}, u32[]{:S(2)}) copy-start(s32[1,1,1,4]{3,2,1,0:T(1,128)} %param.19) | copy-start | bytes 52
  0.7 2.5 %copy-start.9 = (s32[1,1,1,4,512]{4,3,2,1,0:T(4,128)S(1)}, s32[1,1,1,4,512]{4,3,2,1,0:T(4,128)}, u32[]{:S(2)}) copy-start(s32[1,1,1,4,512]{4,3,2,1,0:T(4,128)} %param.18) | copy-start | bytes 24580
  10.1 18.2 %copy-start = (f32[1,1,1,8,8192]{4,3,2,1,0:T(8,128)S(1)}, f32[1,1,1,8,8192]{4,3,2,1,0:T(8,128)}, u32[]{:S(2)}) copy-start(f32[1,1,1,8,8192]{4,3,2,1,0:T(8,128)} %param.16) | copy-start | bytes 786436
  10.1 18.3 %copy-start.10 = (f32[4,128]{1,0:T(4,128)S(1)}, f32[4,128]{1,0:T(4,128)}, u32[]{:S(2)}) copy-start(f32[4,128]{1,0:T(4,128)} %param.25) | copy-start | bytes 6148
  10.1 18.3 %copy-start.11 = (f32[4,128]{1,0:T(4,128)S(1)}, f32[4,128]{1,0:T(4,128)}, u32[]{:S(2)}) copy-start(f32[4,128]{1,0:T(4,128)} %param.24) | copy-start | bytes 6148
  10.1 18.3 %copy-start.12 = (f32[4,128]{1,0:T(4,128)S(1)}, f32[4,128]{1,0:T(4,128)}, u32[]{:S(2)}) copy-start(f32[4,128]{1,0:T(4,128)} %param.23) | copy-start | bytes 6148
  10.4 18.6 %copy-start.4 = (f32[64,1,1,256]{3,2,1,0:T(1,128)S(1)}, f32[64,1,1,256]{3,2,1,0:T(1,128)}, u32[]{:S(2)}) copy-start(f32[64,1,1,256]{3,2,1,0:T(1,128)} %param.20) | copy-start | bytes 196612
  10.5 19.2 %collective-permute-start = (f32[9,512]{1,0:T(8,128)S(1)}, f32[9,512]{1,0:T(8,128)S(1)}, u32[]{:S(2)}, u32[]{:S(2)}) collective-permute-start(f32[9,512]{1,0:T(8,128)S(1)} %bitcast.155), channel_id=1, source_target_pairs={{0,32},{32,64},{64,96},{96,128},{128,160},{160,192},{192,224},{224... | collective-permute-start | bytes 55304 | tf_op jit(solution)/shard_map/ppermute | solution.py:24
  13.9 15.8 %collective-permute-start.1 = (f32[9,512]{1,0:T(8,128)S(1)}, f32[9,512]{1,0:T(8,128)S(1)}, u32[]{:S(2)}, u32[]{:S(2)}) collective-permute-start(f32[9,512]{1,0:T(8,128)S(1)} %bitcast.156), channel_id=1, source_target_pairs={{0,480},{32,0},{64,32},{96,64},{128,96},{160,128},{192,160},{224,1... | collective-permute-start | bytes 55304 | tf_op jit(solution)/shard_map/ppermute | solution.py:24
  20.2 8.8 %copy-start.5 = (f32[64,1,1,256]{3,2,1,0:T(1,128)S(1)}, f32[64,1,1,256]{3,2,1,0:T(1,128)}, u32[]{:S(2)}) copy-start(f32[64,1,1,256]{3,2,1,0:T(1,128)} %param.22) | copy-start | bytes 196612
  20.3 9.5 %collective-permute-start.2 = (f32[9,512]{1,0:T(8,128)S(1)}, f32[9,512]{1,0:T(8,128)S(1)}, u32[]{:S(2)}, u32[]{:S(2)}) collective-permute-start(f32[9,512]{1,0:T(8,128)S(1)} %bitcast.157), channel_id=1, source_target_pairs={{0,2},{2,4},{4,6},{6,8},{8,10},{10,12},{12,14},{14,16},{16,18},{18... | collective-permute-start | bytes 55304 | tf_op jit(solution)/shard_map/ppermute | solution.py:24
  20.3 9.5 %collective-permute-start.3 = (f32[9,512]{1,0:T(8,128)S(1)}, f32[9,512]{1,0:T(8,128)S(1)}, u32[]{:S(2)}, u32[]{:S(2)}) collective-permute-start(f32[9,512]{1,0:T(8,128)S(1)} %bitcast.158), channel_id=1, source_target_pairs={{0,30},{2,0},{4,2},{6,4},{8,6},{10,8},{12,10},{14,12},{16,14},{18,... | collective-permute-start | bytes 55304 | tf_op jit(solution)/shard_map/ppermute | solution.py:24
  39.8 10.0 %copy-start.3 = (f32[64,1,1,256]{3,2,1,0:T(1,128)S(1)}, f32[64,1,1,256]{3,2,1,0:T(1,128)}, u32[]{:S(2)}) copy-start(f32[64,1,1,256]{3,2,1,0:T(1,128)} %param.21) | copy-start | bytes 196612
  54.0 4.9 %copy-start.1 = (f32[2,64,128]{2,1,0:T(8,128)S(1)}, f32[2,64,128]{2,1,0:T(8,128)}, u32[]{:S(2)}) copy-start(f32[2,64,128]{2,1,0:T(8,128)} %get-tuple-element.207) | copy-start | bytes 196612
  54.7 9.4 %collective-permute-start.4 = (f32[4,256]{1,0:T(4,128)S(1)}, f32[4,256]{1,0:T(4,128)S(1)}, u32[]{:S(2)}, u32[]{:S(2)}) collective-permute-start(f32[4,256]{1,0:T(4,128)S(1)} %broadcast_select_fusion), channel_id=1, source_target_pairs={{0,1},{1,0},{2,3},{3,2},{4,5},{5,4},{6,7},{7,6},{8,9},{9,8},{10,11... | collective-permute-start | bytes 12296 | tf_op jit(solution)/shard_map/ppermute | solution.py:302
  57.2 7.6 %copy-start.8 = (f32[4,256]{1,0:T(4,128)S(1)}, f32[4,256]{1,0:T(4,128)}, u32[]{:S(2)}) copy-start(f32[4,256]{1,0:T(4,128)} %get-tuple-element.208) | copy-start | bytes 12292
  57.2 10.2 %copy-start.6 = (f32[64,256]{1,0:T(8,128)S(1)}, f32[64,256]{1,0:T(8,128)}, u32[]{:S(2)}) copy-start(f32[64,256]{1,0:T(8,128)} %get-tuple-element.206) | copy-start | bytes 196612
  57.2 10.2 %copy-start.7 = (f32[64,256]{1,0:T(8,128)S(1)}, f32[64,256]{1,0:T(8,128)}, u32[]{:S(2)}) copy-start(f32[64,256]{1,0:T(8,128)} %get-tuple-element.210) | copy-start | bytes 196612

commit v2 on v1

--- a/solution.py
+++ b/solution.py
@@ -185,6 +185,158 @@
     )
     forcing = jnp.stack([vel_tile + BUOYANCY * heating, pres_tile])
     return (resident, arrived, forcing)
+
+
+def split_pieces(value):
+    high = value.astype(jnp.bfloat16)
+    rest = value - high.astype(jnp.float32)
+    middle = rest.astype(jnp.bfloat16)
+    low = (rest - middle.astype(jnp.float32)).astype(jnp.bfloat16)
+    return (high, middle, low)
+
+
+def condense_chunk(records, cells, occupied, sat_pieces):
+    level_count = sat_pieces[0].shape[0]
+    column_count = sat_pieces[0].shape[1]
+    width = cells.shape[1]
+    shift = column_count.bit_length() - 1
+    levels = lax.shift_right_logical(cells, shift)
+    columns = jnp.bitwise_and(cells, column_count - 1)
+    col_hot = jnp.where(
+        lax.broadcasted_iota(jnp.int32, (column_count, width), 0) == columns, 1.0, 0.0
+    ).astype(jnp.bfloat16)
+    level_mask = lax.broadcasted_iota(jnp.int32, (level_count, width), 0) == levels
+    rows = None
+    for piece in sat_pieces:
+        part = jnp.dot(piece, col_hot, preferred_element_type=jnp.float32)
+        rows = part if rows is None else rows + part
+    excess = jnp.sum(jnp.where(level_mask, rows, 0.0), axis=0, keepdims=True)
+    radius = jnp.where(occupied, records[0:1], 1.0)
+    dry_radius = records[2:3]
+    solute = records[3:4]
+    radius_cubed = radius * radius * radius
+    squared = jnp.maximum(
+        radius * radius
+        + GROW
+        * (
+            excess
+            - CURVATURE / radius
+            + solute * dry_radius * dry_radius * dry_radius / radius_cubed
+        ),
+        FLOOR_SQ,
+    )
+    grown = jnp.sqrt(squared)
+    condensed = jnp.where(occupied, records[1:2] * (grown * grown * grown - radius_cubed), 0.0)
+    heat = None
+    for piece in split_pieces(condensed):
+        spread = jnp.where(level_mask, piece.astype(jnp.float32), 0.0).astype(jnp.bfloat16)
+        part = lax.dot_general(
+            spread, col_hot, (((1,), (1,)), ((), ())), preferred_element_type=jnp.float32
+        )
+        heat = part if heat is None else heat + part
+    updated = jnp.concatenate([grown, records[1:]], axis=0)
+    updated = jnp.where(occupied, updated, 0.0)
+    return (updated, heat)
+
+
+def resident_kernel(rec_ref, cell_ref, stay_ref, sat_ref, out_ref, heat_ref):
+    step = pl.program_id(0)
+    sat_pieces = split_pieces(sat_ref[...])
+    updated, heat = condense_chunk(rec_ref[...], cell_ref[...], stay_ref[...] > 0.0, sat_pieces)
+    out_ref[...] = updated
+
+    @pl.when(step == 0)
+    def _():
+        heat_ref[...] = heat
+
+    @pl.when(step > 0)
+    def _():
+        heat_ref[...] += heat
+
+
+def arrival_kernel(in_ref, sat_ref, res_ref, vel_ref, out_ref, force_ref, heat_acc):
+    step = pl.program_id(0)
+    record_width = out_ref.shape[0]
+    packet = in_ref[...]
+    records = packet[:record_width]
+    cells = (packet[record_width : record_width + 1] + 0.5).astype(jnp.int32)
+    occupied = records[1:2] > 0.0
+    updated, heat = condense_chunk(records, cells, occupied, split_pieces(sat_ref[...]))
+    out_ref[...] = updated
+
+    @pl.when(step == 0)
+    def _():
+        heat_acc[...] = res_ref[...] + heat
+
+    @pl.when(step > 0)
+    def _():
+        heat_acc[...] += heat
+
+    @pl.when(step == pl.num_programs(0) - 1)
+    def _():
+        force_ref[...] = vel_ref[...] + BUOYANCY * heat_acc[...]
+
+
+def settle_residents(records, cell_ids, staying, sat_tile):
+    record_width, drop_count = records.shape
+    level_count, column_count = sat_tile.shape
+    chunk = min(1024, drop_count)
+    whole = lambda j: (0, 0)
+    by_chunk = lambda j: (0, j)
+    return pl.pallas_call(
+        resident_kernel,
+        grid=(drop_count // chunk,),
+        out_shape=(
+            jax.ShapeDtypeStruct((record_width, drop_count), jnp.float32),
+            jax.ShapeDtypeStruct((level_count, column_count), jnp.float32),
+        ),
+        in_specs=[
+            pl.BlockSpec((record_width, chunk), by_chunk),
+            pl.BlockSpec((1, chunk), by_chunk),
+            pl.BlockSpec((1, chunk), by_chunk),
+            pl.BlockSpec((level_count, column_count), whole),
+        ],
+        out_specs=(
+            pl.BlockSpec((record_width, chunk), by_chunk),
+            pl.BlockSpec((level_count, column_count), whole),
+        ),
+        cost_estimate=pl.CostEstimate(
+            flops=12 * level_count * column_count * drop_count,
+            bytes_accessed=4 * (2 * record_width + 2) * drop_count,
+            transcendentals=drop_count,
+        ),
+    )(records, cell_ids.reshape(1, drop_count), staying.astype(jnp.float32).reshape(1, drop_count), sat_tile)
+
+
+def settle_arrivals(packet_in, sat_tile, heat_res, vel_tile):
+    faces, packet_width, slot_count = packet_in.shape
+    record_width = packet_width - 1
+    level_count, column_count = sat_tile.shape
+    whole = lambda f: (0, 0)
+    return pl.pallas_call(
+        arrival_kernel,
+        grid=(faces,),
+        out_shape=(
+            jax.ShapeDtypeStruct((faces, record_width, slot_count), jnp.float32),
+            jax.ShapeDtypeStruct((level_count, column_count), jnp.float32),
+        ),
+        in_specs=[
+            pl.BlockSpec((None, packet_width, slot_count), lambda f: (f, 0, 0)),
+            pl.BlockSpec((level_count, column_count), whole),
+            pl.BlockSpec((level_count, column_count), whole),
+            pl.BlockSpec((level_count, column_count), whole),
+        ],
+        out_specs=(
+            pl.BlockSpec((None, record_width, slot_count), lambda f: (f, 0, 0)),
+            pl.BlockSpec((level_count, column_count), whole),
+        ),
+        scratch_shapes=[pltpu.VMEM((level_count, column_count), jnp.float32)],
+        cost_estimate=pl.CostEstimate(
+            flops=12 * level_count * column_count * faces * slot_count,
+            bytes_accessed=4 * (2 * packet_width) * faces * slot_count,
+            transcendentals=faces * slot_count,
+        ),
+    )(packet_in, sat_tile, heat_res, vel_tile)
 
 
 def along_x(packet_face, offset):
@@ -329,10 +481,10 @@
     from_east = along_x(packet[1], -1)
     from_south = along_y(packet[2], 1)
     from_north = along_y(packet[3], -1)
+    resident, heat_res = settle_residents(records, cell_ids, staying, sat_tile)
     packet_in = jnp.stack([from_west, from_east, from_south, from_north])
-    resident, arrived, forcing = settle(
-        records, cell_ids, staying, packet_in, sat_tile, velocity[:, 0, 0, :], pressure[:, 0, 0, :]
-    )
+    arrived, force_v = settle_arrivals(packet_in, sat_tile, heat_res, velocity[:, 0, 0, :])
+    forcing = jnp.stack([force_v, pressure[:, 0, 0, :]])
     solved_v, solved_p = solve_split(forcing, block_inverse, forward_map, backward_map)
     new_velocity = solved_v[:, None, None, :]
     new_pressure = solved_p[:, None, None, :]

time: 69.2 us -> 66.5 us (0.961)
  matrix products: 22.9 us -> 5.04 us
  Pallas kernels: 3.48 us -> 17.9 us
  waiting for transfers between devices: 5.15 us -> 5.99 us
    dot_general x10 -> x0, matrix products: 17.9 us -> none  [the longest x5 9.56 us: add_one_block(): jnp.einsum('nl,nc->lc', levels, columns, precision=EXACT, preferred_eleme...]
    pallas_call x0 -> x2, Pallas kernels: none -> 14.4 us  [the longest x1 10.2 us: settle_residents(): pl.pallas_call(resident_kernel, grid=(drop_count // chunk,), out_shape=(j...]
    select_n x14 -> x0, other arithmetic: 1.63 us -> none  [the longest x2 1.44 us: condense(): updated = jnp.where(occupied[..., None, :], updated, 0.0)]
    dynamic_update_slice x5 -> x0, local copies, waits for them, and re-layouts: 1.02 us -> none  [read_cells(): return lax.map(read_one_block, cell_ids.reshape(-1, block_rows)).reshape(-1)]
    ppermute x1, waiting for transfers between devices: 5 us -> 5.98 us  [solve_split(): received = lax.ppermute(message, 'gz', [(0, 1), (1, 0)])]
    broadcast_in_dim x1, other arithmetic: 0.1 us -> 0.97 us  [body(): new_pressure = solved_p[:, None, None, :]]
    slice x1, local copies, waits for them, and re-layouts: 0.22 us -> 1.07 us  [solve_split(): new_p = sp + extra[1, :, 0:1] * r0[None, :] + extra[1, :, 1:2] * r1[None, :]]
    unnamed x45 -> x29, local copies, waits for them, and re-layouts: 3.76 us -> 4.35 us
  transfers between devices with their start and end apart: 5 -> 5, of which waited for: 2 -> 1; matrix products, arithmetic and copies ran while one was open for 5% -> 5% of each run, Pallas kernels for 0% -> 16%
where the time goes in v2:
time: 66.5 us; the launch traced here: 65.7 us
  starting transfers between devices  20 us (30%)
  Pallas kernels  17.9 us (27%)
  other arithmetic  7.86 us (12%)
  local copies, waits for them, and re-layouts  7.84 us (12%)
  waiting for transfers between devices  5.99 us (9%)
  matrix products  5.04 us (8%)
  between operations  0.9 us (1%)
    ppermute x4, starting transfers between devices, shifted(): return lax.ppermute(value, axis, pairs)  17.7 us
    pallas_call x1, Pallas kernels, settle_residents(): pl.pallas_call(resident_kernel, grid=(drop_count // chunk,), out_shape=(j...  10.2 us
    ppermute x1, waiting for transfers between devices, solve_split(): received = lax.ppermute(message, 'gz', [(0, 1), (1, 0)])  5.98 us
    dot_general x2, matrix products, pick_block(): jnp.einsum('nh,rhl->nrl', upper, table, precision=EXACT, preferred_elemen...  4.59 us
    unnamed x29, local copies, waits for them, and re-layouts  4.35 us
    pallas_call x1, Pallas kernels, settle_arrivals(): pl.pallas_call(arrival_kernel, grid=(faces,), out_shape=(jax.ShapeDtypeSt...  4.19 us
    pallas_call x1, Pallas kernels, solve_local(): pl.pallas_call(solve_kernel, out_shape=(jax.ShapeDtypeStruct((levels, col...  3.47 us
    add x1, other arithmetic, solve_split(): r0 = received[0] + received[2, 0] * last[0] + received[2, 1] * last[1]  3.22 us
  transfers between devices with their start and end apart: 5, of which 1 were waited for; matrix products, arithmetic and copies ran while one was open for 5% of the time, Pallas kernels for 16%

profile of v2, /device:TPU:32, one launch (start us, length us, event | category | flops | bytes accessed | tf_op | source)
XLA Modules:
  0.0 65.7 jit_solution(3423870828750028658)
XLA Ops:
  0.6 0.0 copy-start.3
  0.6 0.0 copy-start.8
  0.7 0.0 copy-start.4
  0.7 1.0 %copy.43 = f32[1,8,64,128]{3,2,1,0:T(8,128)S(1)} copy(f32[1,8,64,128]{3,1,2,0:T(8,128)} %bitcast.85) | data formatting | bytes 524288
  1.7 0.0 copy-done.3
  1.8 0.5 broadcast.410
  2.3 0.0 copy-done.8
  2.3 0.7 %reduce.13 = s32[4]{0:T(128)S(1)} reduce(s32[1,1,1,4]{3,2,1,0:T(1,128)S(1)} %copy-done.8, s32[]{:T(128)} %broadcast.410), dimensions={0,1,2}, to_apply=%param.15.reduce_sub_computation.3 | reduce | bytes 36 | tf_op args[3]
  2.9 0.1 lt.45
  3.0 0.1 broadcast_bitcast_fusion
  3.1 0.0 copy-done.4
  3.2 6.9 %while.14 = (s32[]{:T(128)}, f32[2,1024,9]{1,0,2:T(2,128)S(1)}, f32[2,64,128]{2,1,0:T(8,128)S(1)}, s32[2,1024]{1,0:T(2,128)S(1)}, f32[9,64,128]{2,1,0:T(8,128)S(...) while((s32[]{:T(128)}, f32[2,1024,9]{1,0,2:T(2,128)S(1)}, f32[2,64,128]{2,1,0:T(8,128)S(1)}, ...), condition=%wide.region_2.3_spmd, body=%wide.region_0.2_spmd.sunk | while | flops 926296064 | bytes 1603685 | solution.py:154
  3.3 0.2 fusion.31
  3.5 0.1 fusion.30
  3.6 2.3 %multiply_reduce_fusion.2 = f32[1024,9]{0,1:T(8,128)S(1)} fusion(f32[1024,128]{0,1:T(8,128)S(1)} %fusion.30, f32[9,64,128]{2,1,0:T(8,128)S(1)} %get-tuple-element.210, s32[1024]{0:T(1024)S(1)} %get-tuple-element.189), kind=kOutput, calls=%fused_computation.clone.1 | convolution fusion | flops 908385280 | bytes 860160 | tf_op jit(solution)/shard_map/while/body/eval_jaxpr/nh,rhl->nrl/dot_general | solution.py:144
  5.9 0.7 %dynamic_update_slice.18 = f32[2,1024,9]{1,0,2:T(2,128)S(1)} dynamic-update-slice(f32[2,1024,9]{1,0,2:T(2,128)S(1)} %get-tuple-element.199, f32[1,1024,9]{1,0,2:T(1,128)S(1)} %copy.47, s32[]{:T(128)} %get-tuple-element.198, s32[]{:T(128)} %constant.123.clone.1..sunk, s32[]{:T(128)} %constant.123.clone.1..sunk) | dynamic-update-slice | bytes 73732 | tf_op jit(solution)/shard_map/while/body/jit(dynamic_update_index_in_dim)/dynamic_update_slice | solution.py:154
  6.7 0.2 fusion.31
  6.9 0.1 fusion.30
  7.0 2.3 %multiply_reduce_fusion.2 = f32[1024,9]{0,1:T(8,128)S(1)} fusion(f32[1024,128]{0,1:T(8,128)S(1)} %fusion.30, f32[9,64,128]{2,1,0:T(8,128)S(1)} %get-tuple-element.210, s32[1024]{0:T(1024)S(1)} %get-tuple-element.189), kind=kOutput, calls=%fused_computation.clone.1 | convolution fusion | flops 908385280 | bytes 860160 | tf_op jit(solution)/shard_map/while/body/eval_jaxpr/nh,rhl->nrl/dot_general | solution.py:144
  9.3 0.7 %dynamic_update_slice.18 = f32[2,1024,9]{1,0,2:T(2,128)S(1)} dynamic-update-slice(f32[2,1024,9]{1,0,2:T(2,128)S(1)} %get-tuple-element.199, f32[1,1024,9]{1,0,2:T(1,128)S(1)} %copy.47, s32[]{:T(128)} %get-tuple-element.198, s32[]{:T(128)} %constant.123.clone.1..sunk, s32[]{:T(128)} %constant.123.clone.1..sunk) | dynamic-update-slice | bytes 73732 | tf_op jit(solution)/shard_map/while/body/jit(dynamic_update_index_in_dim)/dynamic_update_slice | solution.py:154
  10.1 0.0 copy-start.1
  10.1 0.0 copy-start.2
  10.1 0.1 reshape.383
  10.2 0.1 iota_compare_fusion.2
  10.3 0.1 fusion.15
  10.5 3.4 %collective-permute-start = (f32[9,512]{1,0:T(8,128)S(1)}, f32[9,512]{1,0:T(8,128)S(1)}, u32[]{:S(2)}, u32[]{:S(2)}) collective-permute-start(f32[9,512]{1,0:T(8,128)S(1)} %get-tuple-element.131), channel_id=1, source_target_pairs={{0,32},{32,64},{64,96},{96,128},{128,160},{160,192},{192,224},{224... | collective-permute-start | bytes 55304 | tf_op jit(solution)/shard_map/ppermute | solution.py:24
  13.9 6.4 %collective-permute-start.1 = (f32[9,512]{1,0:T(8,128)S(1)}, f32[9,512]{1,0:T(8,128)S(1)}, u32[]{:S(2)}, u32[]{:S(2)}) collective-permute-start(f32[9,512]{1,0:T(8,128)S(1)} %get-tuple-element.134), channel_id=1, source_target_pairs={{0,480},{32,0},{64,32},{96,64},{128,96},{160,128},{192,160},{224,1... | collective-permute-start | bytes 55304 | tf_op jit(solution)/shard_map/ppermute | solution.py:24
  20.2 0.0 collective-permute-start.2
  20.3 7.9 %collective-permute-start.3 = (f32[9,512]{1,0:T(8,128)S(1)}, f32[9,512]{1,0:T(8,128)S(1)}, u32[]{:S(2)}, u32[]{:S(2)}) collective-permute-start(f32[9,512]{1,0:T(8,128)S(1)} %get-tuple-element.132), channel_id=1, source_target_pairs={{0,30},{2,0},{4,2},{6,4},{8,6},{10,8},{12,10},{14,12},{16,14},{18,... | collective-permute-start | bytes 55304 | tf_op jit(solution)/shard_map/ppermute | solution.py:24
  28.2 0.6 compare_convert_fusion
  28.8 0.0 copy-done.1
  28.8 0.0 copy-done.2
  28.8 0.7 %copy_bitcast_fusion.3 = (f32[64,256]{1,0:T(8,128)}, f32[64,256]{1,0:T(8,128)}) fusion(f32[64,1,1,256]{3,2,1,0:T(1,128)S(1)} %copy-done.1, f32[64,1,1,256]{3,2,1,0:T(1,128)S(1)} %copy-done.2), kind=kLoop, calls=%fused_computation.29 | loop fusion | bytes 262144
  29.5 0.0 copy-start.5
  29.5 0.0 copy-start.6
  29.5 0.0 copy-start.7
  29.5 0.0 copy-start
  29.5 10.2 %shard_map.129 = (f32[8,8192]{1,0:T(8,128)}, f32[64,256]{1,0:T(8,128)}) custom-call(f32[8,8192]{1,0:T(8,128)} %bitcast.86, s32[1,8192]{1,0:T(1,128)} %bitcast.89, f32[1,8192]{1,0:T(1,128)} %bitcast.90, f32[64,256]{1,0:T(8,128)} %get-tuple-element.148.sat_ref), custom_call_target="tpu_custom_call" | custom-call | flops 1610612736 | bytes 589824 | tf_op jit(solution)/shard_map/pallas_call | solution.py:286
  39.7 0.0 copy-done.5
  39.8 0.0 copy-done.6
  39.8 0.0 copy-done.7
  39.8 0.6 pad_maximum_fusion.2.maps_ref
  40.4 0.0 copy-done
  40.4 0.6 copy.45
  41.0 0.0 collective-permute-done
  41.0 0.0 collective-permute-done.1
  41.0 0.0 collective-permute-done.2
  41.0 0.0 collective-permute-done.3
  41.0 0.7 pad_maximum_fusion.1.in_ref
  41.7 4.2 %shard_map.130 = (f32[4,8,512]{2,1,0:T(8,128)}, f32[64,256]{1,0:T(8,128)}) custom-call(f32[4,9,512]{2,1,0:T(8,128)} %pad_maximum_fusion.1.in_ref, f32[64,256]{1,0:T(8,128)} %get-tuple-element.148.sat_ref, f32[64,256]{1,0:T(8,128)} %get-tuple-element.97.res_ref, f32[64,256]{1,0:T(8,128)} %get-tuple-element.147.vel_ref), custom_call_target="tpu_custom_call" | custom-call | flops 402653184 | bytes 147456 | tf_op jit(solution)/shard_map/pallas_call | solution.py:316
  45.9 3.5 %shard_map.131 = (f32[64,256]{1,0:T(8,128)}, f32[64,256]{1,0:T(8,128)}, f32[4,256]{1,0:T(4,128)}, f32[4,256]{1,0:T(4,128)}, f32[2,64,128]{2,1,0:T(8,128)}) custom-call(s32[1]{0:T(128)} %bitcast.22.off_ref, f32[12,128]{1,0:T(8,128)} %pad_maximum_fusion.2.maps_ref, f32[64,256]{1,0:T(8,128)} %get-tuple-element.99.fv_ref, f32[64,256]{1,0:T(8,128)} %bitcast.87), custom_call_target="tpu_custom_call" | custom-call | flops 655360 | bytes 393216 | tf_op jit(solution)/shard_map/pallas_call | solution.py:428
  49.3 0.7 %broadcast_select_fusion.4 = f32[4,256]{1,0:T(4,128)S(1)} fusion(f32[4,256]{1,0:T(4,128)} %get-tuple-element.102, f32[4,256]{1,0:T(4,128)} %get-tuple-element.103, pred[]{:T(512)S(6)} %eq.103), kind=kLoop, calls=%fused_computation.67 | loop fusion | flops 1024 | bytes 12289 | tf_op jit(solution)/shard_map/jit(_where)/select_n | solution.py:453
  50.0 2.3 %collective-permute-start.4 = (f32[4,256]{1,0:T(4,128)S(1)}, f32[4,256]{1,0:T(4,128)S(1)}, u32[]{:S(2)}, u32[]{:S(2)}) collective-permute-start(f32[4,256]{1,0:T(4,128)S(1)} %broadcast_select_fusion.4), channel_id=1, source_target_pairs={{0,1},{1,0},{2,3},{3,2},{4,5},{5,4},{6,7},{7,6},{8,9},{9,8},{10,11... | collective-permute-start | bytes 12296 | tf_op jit(solution)/shard_map/ppermute | solution.py:454
  52.4 1.1 %slice_reduce_fusion.1 = (f32[64]{0:T(128)S(1)}, f32[64]{0:T(128)S(1)}, f32[64]{0:T(128)S(1)}, f32[64]{0:T(128)S(1)}) fusion(f32[2,64,128]{2,1,0:T(8,128)} %get-tuple-element.101), kind=kLoop, calls=%fused_computation.40 | loop fusion | bytes 2048 | tf_op jit(solution)/shard_map/slice | solution.py:458
  53.5 6.0 %collective-permute-done.4 = f32[4,256]{1,0:T(4,128)S(1)} collective-permute-done((f32[4,256]{1,0:T(4,128)S(1)}, f32[4,256]{1,0:T(4,128)S(1)}, u32[]{:S(2)}, u32[]{:S(2)}) %collective-permute-start.4) | collective-permute-done | bytes 4128 | tf_op jit(solution)/shard_map/ppermute | solution.py:454
  59.4 0.7 %fusion.18 = (f32[1,1]{1,0:T(1,128)}, f32[1,1]{1,0:T(1,128)}, f32[1,1]{1,0:T(1,128)}, f32[1,1]{1,0:T(1,128)}) fusion(f32[4,256]{1,0:T(4,128)S(1)} %collective-permute-done.4), kind=kLoop, calls=%fused_computation.76 | loop fusion | bytes 32 | tf_op jit(solution)/shard_map/slice | solution.py:455
  60.1 3.2 %fusion.17 = (f32[1,256]{1,0:T(1,128)S(1)}, f32[1,256]{1,0:T(1,128)S(1)}) fusion(f32[4,256]{1,0:T(4,128)S(1)} %collective-permute-done.4, f32[4,256]{1,0:T(4,128)} %get-tuple-element.102, f32[]{:T(128)} %bitcast.24, f32[]{:T(128)} %bitcast.23, f32[]{:T(128)} %bitcast.27, f32[]{:T(128)} %bitcast.26), kind=kLoop, calls=%fused_computation.71 | loop fusion | flops 2048 | bytes 6160 | tf_op jit(solution)/shard_map/add | solution.py:455
  63.3 1.0 %add_bitcast_fusion = (f32[64,1,1,256]{3,0,2,1:T(8,128)S(1)}, f32[64,1,1,256]{3,0,2,1:T(8,128)S(1)}) fusion(f32[64,256]{1,0:T(8,128)} %get-tuple-element.104, f32[64]{0:T(128)S(1)} %get-tuple-element.114, f32[64]{0:T(128)S(1)} %get-tuple-element.113, f32[256]{0:T(256)S(1)} %bitcast.98, f32[256]{0:T(256)S(1)} %bitcast.97, f32[64]{0:T(128)S(1)} %get-tuple-element.115, ...), kind=kLoop, calls=%fused_computation.31 | loop fusion | flops 131072 | bytes 265216 | tf_op jit(solution)/shard_map/broadcast_in_dim | solution.py:490
  64.3 0.7 %copy.19 = f32[64,1,1,256]{3,2,1,0:T(1,128)} copy(f32[64,1,1,256]{3,0,2,1:T(8,128)S(1)} %get-tuple-element.142) | data formatting | bytes 131072
  65.0 0.7 %copy.20 = f32[64,1,1,256]{3,2,1,0:T(1,128)} copy(f32[64,1,1,256]{3,0,2,1:T(8,128)S(1)} %get-tuple-element.141) | data formatting | bytes 131072
  (25 shorter events, 0.4 us)
Async XLA Ops:
  0.6 1.1 %copy-start.3 = (s32[1,1,1,8192]{3,2,1,0:T(1,128)S(1)}, s32[1,1,1,8192]{3,2,1,0:T(1,128)}, u32[]{:S(2)}) copy-start(s32[1,1,1,8192]{3,2,1,0:T(1,128)} %param.13) | copy-start | bytes 98308
  0.6 1.6 %copy-start.8 = (s32[1,1,1,4]{3,2,1,0:T(1,128)S(1)}, s32[1,1,1,4]{3,2,1,0:T(1,128)}, u32[]{:S(2)}) copy-start(s32[1,1,1,4]{3,2,1,0:T(1,128)} %param.15) | copy-start | bytes 52
  0.7 2.5 %copy-start.4 = (s32[1,1,1,4,512]{4,3,2,1,0:T(4,128)S(1)}, s32[1,1,1,4,512]{4,3,2,1,0:T(4,128)}, u32[]{:S(2)}) copy-start(s32[1,1,1,4,512]{4,3,2,1,0:T(4,128)} %param.14) | copy-start | bytes 24580
  10.1 18.8 %copy-start.1 = (f32[64,1,1,256]{3,2,1,0:T(1,128)S(1)}, f32[64,1,1,256]{3,2,1,0:T(1,128)}, u32[]{:S(2)}) copy-start(f32[64,1,1,256]{3,2,1,0:T(1,128)} %param.17) | copy-start | bytes 196612
  10.1 18.8 %copy-start.2 = (f32[64,1,1,256]{3,2,1,0:T(1,128)S(1)}, f32[64,1,1,256]{3,2,1,0:T(1,128)}, u32[]{:S(2)}) copy-start(f32[64,1,1,256]{3,2,1,0:T(1,128)} %param.16) | copy-start | bytes 196612
  10.5 30.5 %collective-permute-start = (f32[9,512]{1,0:T(8,128)S(1)}, f32[9,512]{1,0:T(8,128)S(1)}, u32[]{:S(2)}, u32[]{:S(2)}) collective-permute-start(f32[9,512]{1,0:T(8,128)S(1)} %get-tuple-element.131), channel_id=1, source_target_pairs={{0,32},{32,64},{64,96},{96,128},{128,160},{160,192},{192,224},{224... | collective-permute-start | bytes 55304 | tf_op jit(solution)/shard_map/ppermute | solution.py:24
  13.9 27.1 %collective-permute-start.1 = (f32[9,512]{1,0:T(8,128)S(1)}, f32[9,512]{1,0:T(8,128)S(1)}, u32[]{:S(2)}, u32[]{:S(2)}) collective-permute-start(f32[9,512]{1,0:T(8,128)S(1)} %get-tuple-element.134), channel_id=1, source_target_pairs={{0,480},{32,0},{64,32},{96,64},{128,96},{160,128},{192,160},{224,1... | collective-permute-start | bytes 55304 | tf_op jit(solution)/shard_map/ppermute | solution.py:24
  20.2 20.8 %collective-permute-start.2 = (f32[9,512]{1,0:T(8,128)S(1)}, f32[9,512]{1,0:T(8,128)S(1)}, u32[]{:S(2)}, u32[]{:S(2)}) collective-permute-start(f32[9,512]{1,0:T(8,128)S(1)} %get-tuple-element.133), channel_id=1, source_target_pairs={{0,2},{2,4},{4,6},{6,8},{8,10},{10,12},{12,14},{14,16},{16,18},{18... | collective-permute-start | bytes 55304 | tf_op jit(solution)/shard_map/ppermute | solution.py:24
  20.3 20.7 %collective-permute-start.3 = (f32[9,512]{1,0:T(8,128)S(1)}, f32[9,512]{1,0:T(8,128)S(1)}, u32[]{:S(2)}, u32[]{:S(2)}) collective-permute-start(f32[9,512]{1,0:T(8,128)S(1)} %get-tuple-element.132), channel_id=1, source_target_pairs={{0,30},{2,0},{4,2},{6,4},{8,6},{10,8},{12,10},{14,12},{16,14},{18,... | collective-permute-start | bytes 55304 | tf_op jit(solution)/shard_map/ppermute | solution.py:24
  29.5 10.3 %copy-start.5 = (f32[4,128]{1,0:T(4,128)S(1)}, f32[4,128]{1,0:T(4,128)}, u32[]{:S(2)}) copy-start(f32[4,128]{1,0:T(4,128)} %param.21) | copy-start | bytes 6148
  29.5 10.3 %copy-start.6 = (f32[4,128]{1,0:T(4,128)S(1)}, f32[4,128]{1,0:T(4,128)}, u32[]{:S(2)}) copy-start(f32[4,128]{1,0:T(4,128)} %param.20) | copy-start | bytes 6148
  29.5 10.3 %copy-start.7 = (f32[4,128]{1,0:T(4,128)S(1)}, f32[4,128]{1,0:T(4,128)}, u32[]{:S(2)}) copy-start(f32[4,128]{1,0:T(4,128)} %param.19) | copy-start | bytes 6148
  29.5 10.9 %copy-start = (f32[64,1,1,256]{3,2,1,0:T(1,128)S(1)}, f32[64,1,1,256]{3,2,1,0:T(1,128)}, u32[]{:S(2)}) copy-start(f32[64,1,1,256]{3,2,1,0:T(1,128)} %param.18) | copy-start | bytes 196612
  50.0 9.4 %collective-permute-start.4 = (f32[4,256]{1,0:T(4,128)S(1)}, f32[4,256]{1,0:T(4,128)S(1)}, u32[]{:S(2)}, u32[]{:S(2)}) collective-permute-start(f32[4,256]{1,0:T(4,128)S(1)} %broadcast_select_fusion.4), channel_id=1, source_target_pairs={{0,1},{1,0},{2,3},{3,2},{4,5},{5,4},{6,7},{7,6},{8,9},{9,8},{10,11... | collective-permute-start | bytes 12296 | tf_op jit(solution)/shard_map/ppermute | solution.py:454

commit v3 on v0

v3 whole, which is shorter than its diff:
```python
import math

import jax
import jax.numpy as jnp
from jax import lax
from jax.sharding import PartitionSpec as P
from jax.experimental import pallas as pl
from jax.experimental.pallas import tpu as pltpu

CX = 8
CY = 32


GROW = 0.4
CURVATURE = 0.05
FLOOR_SQ = 0.09
BUOYANCY = 0.5
EXACT = lax.Precision.HIGHEST


def shifted(value, axis, steps):
    count = lax.axis_size(axis)
    pairs = [(source, (source + steps) % count) for source in range(count)]
    return lax.ppermute(value, axis, pairs)


def one_hot_of(index, width, dtype):
    return (index[:, None] == lax.broadcasted_iota(jnp.int32, (1, width), 1)).astype(dtype)


def emit_packets(records, cell_ids, leavers, live_count, width_x, width_y):
    record_width, drop_count = records.shape
    slot_count = leavers.shape[1]
    slot_ids = lax.broadcasted_iota(jnp.int32, (4, slot_count), 1)
    face_ids = lax.broadcasted_iota(jnp.int32, (4, slot_count), 0)
    in_use = slot_ids < live_count[:, None]
    inner = min(128, drop_count)
    outer = drop_count // inner
    table = jnp.concatenate([records, cell_ids.astype(jnp.float32)[None, :]], axis=0).reshape(
        record_width + 1, outer, inner
    )
    flat_leavers = leavers.reshape(-1)
    flat_use = in_use.reshape(-1).astype(jnp.bfloat16)
    block_rows = math.gcd(4 * slot_count, 1024)

    def pick_block(inputs):
        ids_block, use_block = inputs
        upper = one_hot_of(ids_block // inner, outer, jnp.float32)
        lower = one_hot_of(ids_block % inner, inner, jnp.float32)
        rows = jnp.einsum(
            "nh,rhl->nrl", upper, table, precision=EXACT, preferred_element_type=jnp.float32
        )
        picked_block = jnp.sum(rows * lower[:, None, :], axis=2)
        upper_used = upper.astype(jnp.bfloat16) * use_block[:, None]
        counts = jnp.einsum(
            "nh,nl->hl", upper_used, lower.astype(jnp.bfloat16), preferred_element_type=jnp.float32
        )
        return (picked_block, counts)

    picked_blocks, count_blocks = lax.map(
        pick_block, (flat_leavers.reshape(-1, block_rows), flat_use.reshape(-1, block_rows))
    )
    picked_all = picked_blocks.reshape(4, slot_count, record_width + 1)
    departed = jnp.sum(count_blocks, axis=0).reshape(-1)
    picked = jnp.moveaxis(picked_all[:, :, :record_width], 2, 1)
    source = (picked_all[:, :, record_width] + 0.5).astype(jnp.int32)
    height = source // (width_x * width_y)
    cell_x = source // width_y % width_x
    cell_y = source % width_y
    new_x = jnp.where(face_ids == 0, 0, jnp.where(face_ids == 1, width_x - 1, cell_x))
    new_y = jnp.where(face_ids == 2, 0, jnp.where(face_ids == 3, width_y - 1, cell_y))
    target = height * (width_x * width_y) + new_x * width_y + new_y
    packet = jnp.concatenate([picked, target.astype(records.dtype)[:, None, :]], axis=1)
    packet = jnp.where(in_use[:, None, :], packet, 0.0)
    return (packet, departed == 0.0)


def split_pieces(value):
    high = value.astype(jnp.bfloat16)
    rest = value - high.astype(jnp.float32)
    middle = rest.astype(jnp.bfloat16)
    low = (rest - middle.astype(jnp.float32)).astype(jnp.bfloat16)
    return (high, middle, low)


def stacked_pieces(value):
    return jnp.concatenate(split_pieces(value), axis=0)


def condense_chunk(records, cells, occupied, sat_stack):
    rows = sat_stack.shape[0] // 3
    lanes = sat_stack.shape[1]
    width = cells.shape[1]
    shift = lanes.bit_length() - 1
    row_of = lax.shift_right_logical(cells, shift)
    lane_of = jnp.bitwise_and(cells, lanes - 1)
    lane_mask = lax.broadcasted_iota(jnp.int32, (lanes, width), 0) == lane_of
    lane_hot = jnp.where(lane_mask, 1.0, 0.0).astype(jnp.bfloat16)
    row_mask = lax.broadcasted_iota(jnp.int32, (rows, width), 0) == row_of
    row_hot = jnp.where(row_mask, 1.0, 0.0).astype(jnp.bfloat16)
    picked = jnp.dot(sat_stack, lane_hot, preferred_element_type=jnp.float32)
    picked = picked[:rows] + picked[rows : 2 * rows] + picked[2 * rows :]
    excess = jnp.sum(jnp.where(row_mask, picked, 0.0), axis=0, keepdims=True)
    radius = jnp.where(occupied, records[0:1], 1.0)
    dry_radius = records[2:3]
    solute = records[3:4]
    radius_cubed = radius * radius * radius
    squared = jnp.maximum(
        radius * radius
        + GROW
        * (
            excess
            - CURVATURE / radius
            + solute * dry_radius * dry_radius * dry_radius / radius_cubed
        ),
        FLOOR_SQ,
    )
    grown = jnp.sqrt(squared)
    condensed = jnp.where(occupied, records[1:2] * (grown * grown * grown - radius_cubed), 0.0)
    spread = jnp.concatenate([row_hot * piece for piece in split_pieces(condensed)], axis=0)
    heat = lax.dot_general(
        spread, lane_hot, (((1,), (1,)), ((), ())), preferred_element_type=jnp.float32
    )
    heat = heat[:rows] + heat[rows : 2 * rows] + heat[2 * rows :]
    updated = jnp.concatenate([grown, records[1:]], axis=0)
    updated = jnp.where(occupied, updated, 0.0)
    return (updated, heat)


def resident_kernel(rec_ref, cell_ref, stay_ref, sat_ref, out_ref, heat_ref):
    step = pl.program_id(0)
    updated, heat = condense_chunk(
        rec_ref[...], cell_ref[...], stay_ref[...] > 0.0, stacked_pieces(sat_ref[...])
    )
    out_ref[...] = updated

    @pl.when(step == 0)
    def _():
        heat_ref[...] = heat

    @pl.when(step > 0)
    def _():
        heat_ref[...] += heat


def arrival_kernel(w_ref, e_ref, s_ref, n_ref, sat_ref, res_ref, vel_ref, out_ref, force_ref):
    record_width = out_ref.shape[1]
    sat_stack = stacked_pieces(sat_ref[...])
    total = res_ref[...]
    for face, in_ref in enumerate((w_ref, e_ref, s_ref, n_ref)):
        packet = in_ref[...]
        records = packet[:record_width]
        cells = (packet[record_width : record_width + 1] + 0.5).astype(jnp.int32)
        occupied = records[1:2] > 0.0
        updated, heat = condense_chunk(records, cells, occupied, sat_stack)
        out_ref[face] = updated
        total = total + heat
    force_ref[...] = vel_ref[...] + BUOYANCY * total


def settle_residents(records, cell_row, staying_row, sat_view):
    record_width, drop_count = records.shape
    rows, lanes = sat_view.shape
    chunk = min(4096, drop_count)
    whole = lambda j: (0, 0)
    by_chunk = lambda j: (0, j)
    return pl.pallas_call(
        resident_kernel,
        grid=(drop_count // chunk,),
        out_shape=(
            jax.ShapeDtypeStruct((record_width, drop_count), jnp.float32),
            jax.ShapeDtypeStruct((rows, lanes), jnp.float32),
        ),
        in_specs=[
            pl.BlockSpec((record_width, chunk), by_chunk),
            pl.BlockSpec((1, chunk), by_chunk),
            pl.BlockSpec((1, chunk), by_chunk),
            pl.BlockSpec((rows, lanes), whole),
        ],
        out_specs=(
            pl.BlockSpec((record_width, chunk), by_chunk),
            pl.BlockSpec((rows, lanes), whole),
        ),
        cost_estimate=pl.CostEstimate(
            flops=12 * rows * lanes * drop_count,
            bytes_accessed=4 * (2 * record_width + 2) * drop_count,
            transcendentals=drop_count,
        ),
    )(records, cell_row, staying_row, sat_view)


def settle_arrivals(faces_in, sat_view, heat_res, vel_view):
    packet_width, slot_count = faces_in[0].shape
    record_width = packet_width - 1
    vmem = pl.BlockSpec(memory_space=pltpu.VMEM)
    return pl.pallas_call(
        arrival_kernel,
        out_shape=(
            jax.ShapeDtypeStruct((len(faces_in), record_width, slot_count), jnp.float32),
            jax.ShapeDtypeStruct(sat_view.shape, jnp.float32),
        ),
        in_specs=[vmem] * (len(faces_in) + 3),
        out_specs=(vmem, vmem),
        cost_estimate=pl.CostEstimate(
            flops=12 * sat_view.size * len(faces_in) * slot_count,
            bytes_accessed=4 * (2 * packet_width) * len(faces_in) * slot_count,
            transcendentals=len(faces_in) * slot_count,
        ),
    )(*faces_in, sat_view, heat_res, vel_view)


def solve_kernel(
    off_ref, bi_ref, fm_ref, bm_ref, fv_ref, fp_ref, sv_ref, sp_ref, msg_ref, coef_ref, xs_ref
):
    rows = fv_ref.shape[0]
    levels = coef_ref.shape[1]
    per = rows // levels
    off = off_ref[0]
    upper = jnp.where(off > 0, 1.0, 0.0).astype(jnp.float32)
    lower = 1.0 - upper
    zero = jnp.zeros((per, fv_ref.shape[1]), jnp.float32)

    def forward(k, carry):
        uv, up, x0, x1, x2, x3 = carry
        level = off + k
        b0 = bi_ref[0, level]
        b1 = bi_ref[1, level]
        b2 = bi_ref[2, level]
        b3 = bi_ref[3, level]
        f0 = fm_ref[0, level]
        f1 = fm_ref[1, level]
        f2 = fm_ref[2, level]
        f3 = fm_ref[3, level]
        at = pl.ds(pl.multiple_of(k * per, per), per)
        gv = fv_ref[at, :]
        gp = fp_ref[at, :]
        nuv = (b0 * gv + b1 * gp) + (f0 * uv + f1 * up)
        nup = (b2 * gv + b3 * gp) + (f2 * uv + f3 * up)
        sv_ref[at, :] = nuv
        sp_ref[at, :] = nup
        y0 = f0 * x0 + f1 * x2
        y1 = f0 * x1 + f1 * x3
        y2 = f2 * x0 + f3 * x2
        y3 = f2 * x1 + f3 * x3
        xs_ref[0, k] = y0
        xs_ref[1, k] = y1
        xs_ref[2, k] = y2
        xs_ref[3, k] = y3
        return (nuv, nup, y0, y1, y2, y3)

    uv, up, _, _, _, _ = lax.fori_loop(
        0, levels, forward, (zero, zero, upper, 0.0 * upper, 0.0 * upper, upper), unroll=4
    )

    def backward(step, carry):
        sv, sp, c0, c1, c2, c3 = carry
        k = levels - 1 - step
        level = off + k
        m0 = bm_ref[0, level]
        m1 = bm_ref[1, level]
        m2 = bm_ref[2, level]
        m3 = bm_ref[3, level]
        at = pl.ds(pl.multiple_of(k * per, per), per)
        nsv = sv_ref[at, :] + (m0 * sv + m1 * sp)
        nsp = sp_ref[at, :] + (m2 * sv + m3 * sp)
        sv_ref[at, :] = nsv
        sp_ref[at, :] = nsp
        d0 = xs_ref[0, k] + (m0 * c0 + m1 * c2)
        d1 = xs_ref[1, k] + (m0 * c1 + m1 * c3)
        d2 = xs_ref[2, k] + (m2 * c0 + m3 * c2)
        d3 = xs_ref[3, k] + (m2 * c1 + m3 * c3)
        coef_ref[0, k] = d0
        coef_ref[1, k] = d1
        coef_ref[2, k] = d2
        coef_ref[3, k] = d3
        return (nsv, nsp, d0, d1, d2, d3)

    sv, sp, d0, d1, d2, d3 = lax.fori_loop(
        0, levels, backward, (zero, zero, lower, 0.0 * lower, 0.0 * lower, lower), unroll=4
    )
    lanes = fv_ref.shape[1]
    msg_ref[0:per, :] = lower * uv + upper * sv
    msg_ref[per : 2 * per, :] = lower * up + upper * sp
    for index, value in enumerate((d0, d1, d2, d3)):
        msg_ref[2 * per + index : 2 * per + index + 1, :] = jnp.full((1, lanes), upper * value, jnp.float32)


def correct_kernel(coef_ref, own_ref, recv_ref, sv_ref, sp_ref, nv_ref, np_ref):
    rows = sv_ref.shape[0]
    levels = coef_ref.shape[1]
    per = rows // levels
    own0 = own_ref[0:per, :]
    own1 = own_ref[per : 2 * per, :]
    extra = [recv_ref[2 * per + i : 2 * per + i + 1, :] for i in range(4)]
    v0 = recv_ref[0:per, :] + extra[0] * own0 + extra[1] * own1
    v1 = recv_ref[per : 2 * per, :] + extra[2] * own0 + extra[3] * own1

    def fix(k, carry):
        at = pl.ds(pl.multiple_of(k * per, per), per)
        nv_ref[at, :] = sv_ref[at, :] + (coef_ref[0, k] * v0 + coef_ref[1, k] * v1)
        np_ref[at, :] = sp_ref[at, :] + (coef_ref[2, k] * v0 + coef_ref[3, k] * v1)
        return carry

    lax.fori_loop(0, levels, fix, 0, unroll=8)


def solve_split(force_view, pres_view, levels, block_inverse, forward_map, backward_map):
    assert lax.axis_size("gz") == 2
    rows, lanes = force_view.shape
    per = rows // levels
    offset = jnp.full((1,), lax.axis_index("gz") * levels, jnp.int32)
    smem = pl.BlockSpec(memory_space=pltpu.SMEM)
    vmem = pl.BlockSpec(memory_space=pltpu.VMEM)
    sv, sp, message, coef = pl.pallas_call(
        solve_kernel,
        out_shape=(
            jax.ShapeDtypeStruct((rows, lanes), jnp.float32),
            jax.ShapeDtypeStruct((rows, lanes), jnp.float32),
            jax.ShapeDtypeStruct((2 * per + 4, lanes), jnp.float32),
            jax.ShapeDtypeStruct((4, levels), jnp.float32),
        ),
        in_specs=[smem, smem, smem, smem, vmem, vmem],
        out_specs=(vmem, vmem, vmem, smem),
        scratch_shapes=[pltpu.SMEM((4, levels), jnp.float32)],
        cost_estimate=pl.CostEstimate(
            flops=40 * rows * lanes, bytes_accessed=24 * rows * lanes, transcendentals=0
        ),
    )(offset, block_inverse, forward_map, backward_map, force_view, pres_view)
    received = lax.ppermute(message, "gz", [(0, 1), (1, 0)])
    return pl.pallas_call(
        correct_kernel,
        out_shape=(
            jax.ShapeDtypeStruct((rows, lanes), jnp.float32),
            jax.ShapeDtypeStruct((rows, lanes), jnp.float32),
        ),
        in_specs=[smem, vmem, vmem, vmem, vmem],
        out_specs=(vmem, vmem),
        cost_estimate=pl.CostEstimate(
            flops=8 * rows * lanes, bytes_accessed=16 * rows * lanes, transcendentals=0
        ),
    )(coef, message, received, sv, sp)


def along_x(packet_face, offset):
    return shifted(packet_face, "gx", offset)


def along_y(packet_face, offset):
    return shifted(packet_face, "gy", offset)


def body(
    droplets,
    cell_index,
    crossing,
    crossing_count,
    saturation,
    velocity,
    pressure,
    block_inverse,
    forward_map,
    backward_map,
):
    records = droplets[0, 0, 0]
    cell_ids = cell_index[0, 0, 0]
    levels = saturation.shape[0]
    view = (saturation.size // 128, 128)
    sat_view = saturation.reshape(view)
    packet, staying = emit_packets(
        records, cell_ids, crossing[0, 0, 0], crossing_count[0, 0, 0], CX, CY
    )
    from_west = along_x(packet[0], 1)
    from_east = along_x(packet[1], -1)
    from_south = along_y(packet[2], 1)
    from_north = along_y(packet[3], -1)
    resident, heat_res = settle_residents(
        records,
        cell_index.reshape(1, -1),
        staying.astype(jnp.float32).reshape(1, -1),
        sat_view,
    )
    arrived, force_view = settle_arrivals(
        (from_west, from_east, from_south, from_north), sat_view, heat_res, velocity.reshape(view)
    )
    solved_v, solved_p = solve_split(
        force_view, pressure.reshape(view), levels, block_inverse, forward_map, backward_map
    )
    new_velocity = solved_v.reshape(velocity.shape)
    new_pressure = solved_p.reshape(pressure.shape)
    return (resident[None, None, None], arrived[None, None, None], new_velocity, new_pressure)


def solution(mesh):
    return jax.shard_map(
        body,
        mesh=mesh,
        in_specs=(
            P("gz", "gx", "gy", None, None),
            P("gz", "gx", "gy", None),
            P("gz", "gx", "gy", None, None),
            P("gz", "gx", "gy", None),
            P("gz", "gx", "gy", None),
            P("gz", "gx", "gy", None),
            P("gz", "gx", "gy", None),
            P(),
            P(),
            P(),
        ),
        out_specs=(
            P("gz", "gx", "gy", None, None),
            P("gz", "gx", "gy", None, None, None),
            P("gz", "gx", "gy", None),
            P("gz", "gx", "gy", None),
        ),
        check_vma=False,
    )
```

time: 109 us -> 55.1 us (0.51)
  the two profiles are of different devices: /device:TPU:8 before, /device:TPU:32 now
where the time goes in v3:
time: 55.1 us; the launch traced here: 54.7 us
  starting transfers between devices  20.1 us (36%)
  Pallas kernels  15 us (27%)
  waiting for transfers between devices  7.26 us (13%)
  matrix products  5.04 us (9%)
  local copies, waits for them, and re-layouts  4.59 us (8%)
  other arithmetic  1.71 us (3%)
  between operations  0.9 us (2%)
    ppermute x4, starting transfers between devices, shifted(): return lax.ppermute(value, axis, pairs)  17.7 us
    ppermute x1, waiting for transfers between devices, solve_split(): received = lax.ppermute(message, 'gz', [(0, 1), (1, 0)])  7.25 us
    pallas_call x1, Pallas kernels, settle_residents(): pl.pallas_call(resident_kernel, grid=(drop_count // chunk,), out_shape=(j...  6.6 us
    dot_general x2, matrix products, pick_block(): jnp.einsum('nh,rhl->nrl', upper, table, precision=EXACT, preferred_elemen...  4.59 us
    pallas_call x1, Pallas kernels, solve_split(): pl.pallas_call(solve_kernel, out_shape=(jax.ShapeDtypeStruct((rows, lanes...  3.5 us
    pallas_call x1, Pallas kernels, settle_arrivals(): pl.pallas_call(arrival_kernel, out_shape=(jax.ShapeDtypeStruct((len(faces...  3.08 us
    unnamed x23, local copies, waits for them, and re-layouts  2.84 us
    ppermute x1, starting transfers between devices, solve_split(): received = lax.ppermute(message, 'gz', [(0, 1), (1, 0)])  2.36 us
  transfers between devices with their start and end apart: 5, of which 1 were waited for; matrix products, arithmetic and copies ran while one was open for 1% of the time, Pallas kernels for 12%

profile of v3, /device:TPU:32, one launch (start us, length us, event | category | flops | bytes accessed | tf_op | source)
XLA Modules:
  0.0 54.7 jit_solution(9840237582628285755)
XLA Ops:
  0.6 0.0 copy-start
  0.6 0.0 copy-start.3
  0.7 0.0 copy-start.1
  0.7 1.0 %copy.37 = f32[1,8,64,128]{3,2,1,0:T(8,128)S(1)} copy(f32[1,8,64,128]{3,1,2,0:T(8,128)} %bitcast.69) | data formatting | bytes 524288
  1.7 0.0 copy-done
  1.8 0.5 broadcast.402
  2.3 0.0 copy-done.3
  2.3 0.7 %reduce.5 = s32[4]{0:T(128)S(1)} reduce(s32[1,1,1,4]{3,2,1,0:T(1,128)S(1)} %copy-done.3, s32[]{:T(128)} %broadcast.402), dimensions={0,1,2}, to_apply=%param.15.reduce_sub_computation.3 | reduce | bytes 36 | tf_op args[3]
  2.9 0.1 lt.45
  3.0 0.1 broadcast_bitcast_fusion
  3.1 0.0 copy-done.1
  3.2 6.9 %while.14 = (s32[]{:T(128)}, f32[2,1024,9]{1,0,2:T(2,128)S(1)}, f32[2,64,128]{2,1,0:T(8,128)S(1)}, s32[2,1024]{1,0:T(2,128)S(1)}, f32[9,64,128]{2,1,0:T(8,128)S(...) while((s32[]{:T(128)}, f32[2,1024,9]{1,0,2:T(2,128)S(1)}, f32[2,64,128]{2,1,0:T(8,128)S(1)}, ...), condition=%wide.region_2.3_spmd, body=%wide.region_0.2_spmd.sunk | while | flops 926296064 | bytes 1603685 | solution.py:60
  3.3 0.2 fusion.28
  3.5 0.1 fusion.27
  3.6 2.3 %multiply_reduce_fusion.2 = f32[1024,9]{0,1:T(8,128)S(1)} fusion(f32[1024,128]{0,1:T(8,128)S(1)} %fusion.27, f32[9,64,128]{2,1,0:T(8,128)S(1)} %get-tuple-element.198, s32[1024]{0:T(1024)S(1)} %get-tuple-element.177), kind=kOutput, calls=%fused_computation.clone.1 | convolution fusion | flops 908385280 | bytes 860160 | tf_op jit(solution)/shard_map/while/body/eval_jaxpr/nh,rhl->nrl/dot_general | solution.py:50
  5.9 0.7 %dynamic_update_slice.18 = f32[2,1024,9]{1,0,2:T(2,128)S(1)} dynamic-update-slice(f32[2,1024,9]{1,0,2:T(2,128)S(1)} %get-tuple-element.187, f32[1,1024,9]{1,0,2:T(1,128)S(1)} %copy.40, s32[]{:T(128)} %get-tuple-element.186, s32[]{:T(128)} %constant.123.clone.1..sunk, s32[]{:T(128)} %constant.123.clone.1..sunk) | dynamic-update-slice | bytes 73732 | tf_op jit(solution)/shard_map/while/body/jit(dynamic_update_index_in_dim)/dynamic_update_slice | solution.py:60
  6.7 0.2 fusion.28
  6.9 0.1 fusion.27
  7.0 2.3 %multiply_reduce_fusion.2 = f32[1024,9]{0,1:T(8,128)S(1)} fusion(f32[1024,128]{0,1:T(8,128)S(1)} %fusion.27, f32[9,64,128]{2,1,0:T(8,128)S(1)} %get-tuple-element.198, s32[1024]{0:T(1024)S(1)} %get-tuple-element.177), kind=kOutput, calls=%fused_computation.clone.1 | convolution fusion | flops 908385280 | bytes 860160 | tf_op jit(solution)/shard_map/while/body/eval_jaxpr/nh,rhl->nrl/dot_general | solution.py:50
  9.3 0.7 %dynamic_update_slice.18 = f32[2,1024,9]{1,0,2:T(2,128)S(1)} dynamic-update-slice(f32[2,1024,9]{1,0,2:T(2,128)S(1)} %get-tuple-element.187, f32[1,1024,9]{1,0,2:T(1,128)S(1)} %copy.40, s32[]{:T(128)} %get-tuple-element.186, s32[]{:T(128)} %constant.123.clone.1..sunk, s32[]{:T(128)} %constant.123.clone.1..sunk) | dynamic-update-slice | bytes 73732 | tf_op jit(solution)/shard_map/while/body/jit(dynamic_update_index_in_dim)/dynamic_update_slice | solution.py:60
  10.1 0.1 reshape.399
  10.2 0.1 iota_compare_fusion.2
  10.3 0.1 fusion.15
  10.5 3.4 %collective-permute-start = (f32[9,512]{1,0:T(8,128)S(1)}, f32[9,512]{1,0:T(8,128)S(1)}, u32[]{:S(2)}, u32[]{:S(2)}) collective-permute-start(f32[9,512]{1,0:T(8,128)S(1)} %get-tuple-element.132), channel_id=1, source_target_pairs={{0,32},{32,64},{64,96},{96,128},{128,160},{160,192},{192,224},{224... | collective-permute-start | bytes 55304 | tf_op jit(solution)/shard_map/ppermute | solution.py:24
  13.9 6.4 %collective-permute-start.1 = (f32[9,512]{1,0:T(8,128)S(1)}, f32[9,512]{1,0:T(8,128)S(1)}, u32[]{:S(2)}, u32[]{:S(2)}) collective-permute-start(f32[9,512]{1,0:T(8,128)S(1)} %get-tuple-element.131), channel_id=1, source_target_pairs={{0,480},{32,0},{64,32},{96,64},{128,96},{160,128},{192,160},{224,1... | collective-permute-start | bytes 55304 | tf_op jit(solution)/shard_map/ppermute | solution.py:24
  20.2 0.0 collective-permute-start.2
  20.2 7.9 %collective-permute-start.3 = (f32[9,512]{1,0:T(8,128)S(1)}, f32[9,512]{1,0:T(8,128)S(1)}, u32[]{:S(2)}, u32[]{:S(2)}) collective-permute-start(f32[9,512]{1,0:T(8,128)S(1)} %get-tuple-element.129), channel_id=1, source_target_pairs={{0,30},{2,0},{4,2},{6,4},{8,6},{10,8},{12,10},{14,12},{16,14},{18,... | collective-permute-start | bytes 55304 | tf_op jit(solution)/shard_map/ppermute | solution.py:24
  28.2 0.6 %compare_convert_fusion = f32[64,128]{1,0:T(8,128)} fusion(f32[64,128]{1,0:T(8,128)S(1)} %reduce_sum.21), kind=kLoop, calls=%fused_computation.37 | loop fusion | flops 16384 | bytes 65536 | tf_op jit(solution)/shard_map/convert_element_type | solution.py:379
  28.8 6.6 %shard_map.129 = (f32[8,8192]{1,0:T(8,128)}, f32[128,128]{1,0:T(8,128)}) custom-call(f32[8,8192]{1,0:T(8,128)} %bitcast.70, s32[1,8192]{1,0:T(1,128)} %bitcast.73, f32[1,8192]{1,0:T(1,128)} %bitcast.74, f32[128,128]{1,0:T(8,128)} %bitcast.78), custom_call_target="tpu_custom_call" | custom-call | flops 1610612736 | bytes 589824 | tf_op jit(solution)/shard_map/pallas_call | solution.py:167
  35.4 0.0 collective-permute-done.w_ref
  35.4 0.0 copy-start.4
  35.4 0.0 collective-permute-done.1.e_ref
  35.4 0.0 copy-start.5
  35.4 0.0 collective-permute-done.2.s_ref
  35.5 0.0 copy-start.6
  35.5 0.0 collective-permute-done.3.n_ref
  35.5 0.0 copy-start.7
  35.5 0.5 copy-done.4
  36.0 0.0 copy-done.5
  36.0 0.0 copy-done.6
  36.1 0.0 copy-done.7
  36.1 3.1 %shard_map.130 = (f32[4,8,512]{2,1,0:T(8,128)}, f32[128,128]{1,0:T(8,128)}) custom-call(f32[9,512]{1,0:T(8,128)} %copy-done.4, f32[9,512]{1,0:T(8,128)} %copy-done.5, f32[9,512]{1,0:T(8,128)} %copy-done.6, f32[9,512]{1,0:T(8,128)} %copy-done.7, f32[128,128]{1,0:T(8,128)} %bitcast.79, f32[128,128]{1,0:T(8,128)} %get-tuple-element.98.res_ref, f32[128,128]{1,0:T(8,128)} %bitcast.80), custom_call_target="tpu_custom_call" | custom-call | flops 402653184 | bytes 147456 | tf_op jit(solution)/shard_map/pallas_call | solution.py:196
  39.2 3.5 %shard_map.131 = (f32[128,128]{1,0:T(8,128)}, f32[128,128]{1,0:T(8,128)}, f32[8,128]{1,0:T(8,128)}, f32[4,64]{1,0:T(4,128)}) custom-call(s32[1]{0:T(128)} %bitcast.20.off_ref, f32[4,128]{1,0:T(4,128)} %bi_ref.1, f32[4,128]{1,0:T(4,128)} %fm_ref.1, f32[4,128]{1,0:T(4,128)} %bm_ref.1, f32[128,128]{1,0:T(8,128)} %get-tuple-element.100.fv_ref, f32[128,128]{1,0:T(8,128)} %bitcast.72), custom_call_target="tpu_custom_call" | custom-call | flops 655360 | bytes 393216 | tf_op jit(solution)/shard_map/pallas_call | solution.py:314
  42.7 2.4 %collective-permute-start.4 = (f32[8,128]{1,0:T(8,128)}, f32[8,128]{1,0:T(8,128)S(1)}, u32[]{:S(2)}, u32[]{:S(2)}) collective-permute-start(f32[8,128]{1,0:T(8,128)} %get-tuple-element.102.own_ref), channel_id=1, source_target_pairs={{0,1},{1,0},{2,3},{3,2},{4,5},{5,4},{6,7},{7,6},{8,9},{9,8},{10,11... | collective-permute-start | bytes 12296 | tf_op jit(solution)/shard_map/ppermute | solution.py:329
  45.0 7.2 %collective-permute-done.4.recv_ref = f32[8,128]{1,0:T(8,128)S(1)} collective-permute-done((f32[8,128]{1,0:T(8,128)}, f32[8,128]{1,0:T(8,128)S(1)}, u32[]{:S(2)}, u32[]{:S(2)}) %collective-permute-start.4) | collective-permute-done | bytes 4128 | tf_op jit(solution)/shard_map/ppermute | solution.py:329
  52.3 0.0 copy-start.2
  52.3 0.6 %copy-done.2 = f32[8,128]{1,0:T(8,128)} copy-done((f32[8,128]{1,0:T(8,128)}, f32[8,128]{1,0:T(8,128)S(1)}, u32[]{:S(2)}) %copy-start.2) | copy-done | bytes 4120
  52.9 1.9 %shard_map.132 = (f32[128,128]{1,0:T(8,128)}, f32[128,128]{1,0:T(8,128)}) custom-call(f32[4,64]{1,0:T(4,128)} %get-tuple-element.101.coef_ref, f32[8,128]{1,0:T(8,128)} %get-tuple-element.102.own_ref, f32[8,128]{1,0:T(8,128)} %copy-done.2, f32[128,128]{1,0:T(8,128)} %get-tuple-element.103.sv_ref, f32[128,128]{1,0:T(8,128)} %get-tuple-element.104.sp_ref), custom_call_target="tpu_custom_call" | custom-call | flops 131072 | bytes 262144 | tf_op jit(solution)/shard_map/pallas_call | solution.py:330
  (25 shorter events, 0.4 us)
Async XLA Ops:
  0.6 1.1 %copy-start = (s32[1,1,1,8192]{3,2,1,0:T(1,128)S(1)}, s32[1,1,1,8192]{3,2,1,0:T(1,128)}, u32[]{:S(2)}) copy-start(s32[1,1,1,8192]{3,2,1,0:T(1,128)} %param.13) | copy-start | bytes 98308
  0.6 1.6 %copy-start.3 = (s32[1,1,1,4]{3,2,1,0:T(1,128)S(1)}, s32[1,1,1,4]{3,2,1,0:T(1,128)}, u32[]{:S(2)}) copy-start(s32[1,1,1,4]{3,2,1,0:T(1,128)} %param.15) | copy-start | bytes 52
  0.7 2.5 %copy-start.1 = (s32[1,1,1,4,512]{4,3,2,1,0:T(4,128)S(1)}, s32[1,1,1,4,512]{4,3,2,1,0:T(4,128)}, u32[]{:S(2)}) copy-start(s32[1,1,1,4,512]{4,3,2,1,0:T(4,128)} %param.14) | copy-start | bytes 24580
  10.5 25.0 %collective-permute-start = (f32[9,512]{1,0:T(8,128)S(1)}, f32[9,512]{1,0:T(8,128)S(1)}, u32[]{:S(2)}, u32[]{:S(2)}) collective-permute-start(f32[9,512]{1,0:T(8,128)S(1)} %get-tuple-element.132), channel_id=1, source_target_pairs={{0,32},{32,64},{64,96},{96,128},{128,160},{160,192},{192,224},{224... | collective-permute-start | bytes 55304 | tf_op jit(solution)/shard_map/ppermute | solution.py:24
  13.9 21.6 %collective-permute-start.1 = (f32[9,512]{1,0:T(8,128)S(1)}, f32[9,512]{1,0:T(8,128)S(1)}, u32[]{:S(2)}, u32[]{:S(2)}) collective-permute-start(f32[9,512]{1,0:T(8,128)S(1)} %get-tuple-element.131), channel_id=1, source_target_pairs={{0,480},{32,0},{64,32},{96,64},{128,96},{160,128},{192,160},{224,1... | collective-permute-start | bytes 55304 | tf_op jit(solution)/shard_map/ppermute | solution.py:24
  20.2 15.2 %collective-permute-start.2 = (f32[9,512]{1,0:T(8,128)S(1)}, f32[9,512]{1,0:T(8,128)S(1)}, u32[]{:S(2)}, u32[]{:S(2)}) collective-permute-start(f32[9,512]{1,0:T(8,128)S(1)} %get-tuple-element.130), channel_id=1, source_target_pairs={{0,2},{2,4},{4,6},{6,8},{8,10},{10,12},{12,14},{14,16},{16,18},{18... | collective-permute-start | bytes 55304 | tf_op jit(solution)/shard_map/ppermute | solution.py:24
  20.2 15.2 %collective-permute-start.3 = (f32[9,512]{1,0:T(8,128)S(1)}, f32[9,512]{1,0:T(8,128)S(1)}, u32[]{:S(2)}, u32[]{:S(2)}) collective-permute-start(f32[9,512]{1,0:T(8,128)S(1)} %get-tuple-element.129), channel_id=1, source_target_pairs={{0,30},{2,0},{4,2},{6,4},{8,6},{10,8},{12,10},{14,12},{16,14},{18,... | collective-permute-start | bytes 55304 | tf_op jit(solution)/shard_map/ppermute | solution.py:24
  35.4 0.6 %copy-start.4 = (f32[9,512]{1,0:T(8,128)}, f32[9,512]{1,0:T(8,128)S(1)}, u32[]{:S(2)}) copy-start(f32[9,512]{1,0:T(8,128)S(1)} %collective-permute-done.w_ref) | copy-start | bytes 55300
  35.4 0.6 %copy-start.5 = (f32[9,512]{1,0:T(8,128)}, f32[9,512]{1,0:T(8,128)S(1)}, u32[]{:S(2)}) copy-start(f32[9,512]{1,0:T(8,128)S(1)} %collective-permute-done.1.e_ref) | copy-start | bytes 55300
  35.5 0.6 %copy-start.6 = (f32[9,512]{1,0:T(8,128)}, f32[9,512]{1,0:T(8,128)S(1)}, u32[]{:S(2)}) copy-start(f32[9,512]{1,0:T(8,128)S(1)} %collective-permute-done.2.s_ref) | copy-start | bytes 55300
  35.5 0.6 %copy-start.7 = (f32[9,512]{1,0:T(8,128)}, f32[9,512]{1,0:T(8,128)S(1)}, u32[]{:S(2)}) copy-start(f32[9,512]{1,0:T(8,128)S(1)} %collective-permute-done.3.n_ref) | copy-start | bytes 55300
  42.7 9.6 %collective-permute-start.4 = (f32[8,128]{1,0:T(8,128)}, f32[8,128]{1,0:T(8,128)S(1)}, u32[]{:S(2)}, u32[]{:S(2)}) collective-permute-start(f32[8,128]{1,0:T(8,128)} %get-tuple-element.102.own_ref), channel_id=1, source_target_pairs={{0,1},{1,0},{2,3},{3,2},{4,5},{5,4},{6,7},{7,6},{8,9},{9,8},{10,11... | collective-permute-start | bytes 12296 | tf_op jit(solution)/shard_map/ppermute | solution.py:329
  52.3 0.6 %copy-start.2 = (f32[8,128]{1,0:T(8,128)}, f32[8,128]{1,0:T(8,128)S(1)}, u32[]{:S(2)}) copy-start(f32[8,128]{1,0:T(8,128)S(1)} %collective-permute-done.4.recv_ref) | copy-start | bytes 12292

commit v4 on v3

--- a/solution.py
+++ b/solution.py
@@ -41,7 +41,7 @@
     )
     flat_leavers = leavers.reshape(-1)
     flat_use = in_use.reshape(-1).astype(jnp.bfloat16)
-    block_rows = math.gcd(4 * slot_count, 1024)
+    block_rows = 4 * slot_count
 
     def pick_block(inputs):
         ids_block, use_block = inputs
@@ -77,10 +77,8 @@
 
 def split_pieces(value):
     high = value.astype(jnp.bfloat16)
-    rest = value - high.astype(jnp.float32)
-    middle = rest.astype(jnp.bfloat16)
-    low = (rest - middle.astype(jnp.float32)).astype(jnp.bfloat16)
-    return (high, middle, low)
+    low = (value - high.astype(jnp.float32)).astype(jnp.bfloat16)
+    return (high, low)
 
 
 def stacked_pieces(value):
@@ -88,7 +86,7 @@
 
 
 def condense_chunk(records, cells, occupied, sat_stack):
-    rows = sat_stack.shape[0] // 3
+    rows = sat_stack.shape[0] // 2
     lanes = sat_stack.shape[1]
     width = cells.shape[1]
     shift = lanes.bit_length() - 1
@@ -99,7 +97,7 @@
     row_mask = lax.broadcasted_iota(jnp.int32, (rows, width), 0) == row_of
     row_hot = jnp.where(row_mask, 1.0, 0.0).astype(jnp.bfloat16)
     picked = jnp.dot(sat_stack, lane_hot, preferred_element_type=jnp.float32)
-    picked = picked[:rows] + picked[rows : 2 * rows] + picked[2 * rows :]
+    picked = picked[:rows] + picked[rows:]
     excess = jnp.sum(jnp.where(row_mask, picked, 0.0), axis=0, keepdims=True)
     radius = jnp.where(occupied, records[0:1], 1.0)
     dry_radius = records[2:3]
@@ -121,7 +119,7 @@
     heat = lax.dot_general(
         spread, lane_hot, (((1,), (1,)), ((), ())), preferred_element_type=jnp.float32
     )
-    heat = heat[:rows] + heat[rows : 2 * rows] + heat[2 * rows :]
+    heat = heat[:rows] + heat[rows:]
     updated = jnp.concatenate([grown, records[1:]], axis=0)
     updated = jnp.where(occupied, updated, 0.0)
     return (updated, heat)
@@ -141,21 +139,6 @@
     @pl.when(step > 0)
     def _():
         heat_ref[...] += heat
-
-
-def arrival_kernel(w_ref, e_ref, s_ref, n_ref, sat_ref, res_ref, vel_ref, out_ref, force_ref):
-    record_width = out_ref.shape[1]
-    sat_stack = stacked_pieces(sat_ref[...])
-    total = res_ref[...]
-    for face, in_ref in enumerate((w_ref, e_ref, s_ref, n_ref)):
-        packet = in_ref[...]
-        records = packet[:record_width]
-        cells = (packet[record_width : record_width + 1] + 0.5).astype(jnp.int32)
-        occupied = records[1:2] > 0.0
-        updated, heat = condense_chunk(records, cells, occupied, sat_stack)
-        out_ref[face] = updated
-        total = total + heat
-    force_ref[...] = vel_ref[...] + BUOYANCY * total
 
 
 def settle_residents(records, cell_row, staying_row, sat_view):
@@ -189,36 +172,29 @@
     )(records, cell_row, staying_row, sat_view)
 
 
-def settle_arrivals(faces_in, sat_view, heat_res, vel_view):
-    packet_width, slot_count = faces_in[0].shape
-    record_width = packet_width - 1
-    vmem = pl.BlockSpec(memory_space=pltpu.VMEM)
-    return pl.pallas_call(
-        arrival_kernel,
-        out_shape=(
-            jax.ShapeDtypeStruct((len(faces_in), record_width, slot_count), jnp.float32),
-            jax.ShapeDtypeStruct(sat_view.shape, jnp.float32),
-        ),
-        in_specs=[vmem] * (len(faces_in) + 3),
-        out_specs=(vmem, vmem),
-        cost_estimate=pl.CostEstimate(
-            flops=12 * sat_view.size * len(faces_in) * slot_count,
-            bytes_accessed=4 * (2 * packet_width) * len(faces_in) * slot_count,
-            transcendentals=len(faces_in) * slot_count,
-        ),
-    )(*faces_in, sat_view, heat_res, vel_view)
-
-
-def solve_kernel(
-    off_ref, bi_ref, fm_ref, bm_ref, fv_ref, fp_ref, sv_ref, sp_ref, msg_ref, coef_ref, xs_ref
-):
-    rows = fv_ref.shape[0]
-    levels = coef_ref.shape[1]
+def arrivals_into(faces, sat_ref, res_ref, vel_ref, out_ref, force_ref):
+    record_width = out_ref.shape[1]
+    sat_stack = stacked_pieces(sat_ref[...])
+    total = res_ref[...]
+    for face, in_ref in enumerate(faces):
+        packet = in_ref[...]
+        records = packet[:record_width]
+        cells = (packet[record_width : record_width + 1] + 0.5).astype(jnp.int32)
+        occupied = records[1:2] > 0.0
+        updated, heat = condense_chunk(records, cells, occupied, sat_stack)
+        out_ref[face] = updated
+        total = total + heat
+    force_ref[...] = vel_ref[...] + BUOYANCY * total
+
+
+def solve_into(off_ref, bi_ref, fm_ref, bm_ref, fv_ref, fp_ref, sv_ref, sp_ref, msg_ref, coef_ref, xs_ref):
+    rows, lanes = fv_ref.shape
+    levels = xs_ref.shape[1]
     per = rows // levels
     off = off_ref[0]
     upper = jnp.where(off > 0, 1.0, 0.0).astype(jnp.float32)
     lower = 1.0 - upper
-    zero = jnp.zeros((per, fv_ref.shape[1]), jnp.float32)
+    zero = jnp.zeros((per, lanes), jnp.float32)
 
     def forward(k, carry):
         uv, up, x0, x1, x2, x3 = carry
@@ -269,76 +245,91 @@
         d1 = xs_ref[1, k] + (m0 * c1 + m1 * c3)
         d2 = xs_ref[2, k] + (m2 * c0 + m3 * c2)
         d3 = xs_ref[3, k] + (m2 * c1 + m3 * c3)
-        coef_ref[0, k] = d0
-        coef_ref[1, k] = d1
-        coef_ref[2, k] = d2
-        coef_ref[3, k] = d3
+        coef_ref[0, at, :] = jnp.full((per, lanes), d0, jnp.float32)
+        coef_ref[1, at, :] = jnp.full((per, lanes), d1, jnp.float32)
+        coef_ref[2, at, :] = jnp.full((per, lanes), d2, jnp.float32)
+        coef_ref[3, at, :] = jnp.full((per, lanes), d3, jnp.float32)
         return (nsv, nsp, d0, d1, d2, d3)
 
     sv, sp, d0, d1, d2, d3 = lax.fori_loop(
         0, levels, backward, (zero, zero, lower, 0.0 * lower, 0.0 * lower, lower), unroll=4
     )
-    lanes = fv_ref.shape[1]
     msg_ref[0:per, :] = lower * uv + upper * sv
     msg_ref[per : 2 * per, :] = lower * up + upper * sp
     for index, value in enumerate((d0, d1, d2, d3)):
         msg_ref[2 * per + index : 2 * per + index + 1, :] = jnp.full((1, lanes), upper * value, jnp.float32)
 
 
+def arrive_solve_kernel(
+    off_ref, bi_ref, fm_ref, bm_ref, w_ref, e_ref, s_ref, n_ref, sat_ref, res_ref, vel_ref, pres_ref,
+    out_ref, sv_ref, sp_ref, msg_ref, coef_ref, force_ref, xs_ref,
+):
+    arrivals_into((w_ref, e_ref, s_ref, n_ref), sat_ref, res_ref, vel_ref, out_ref, force_ref)
+    solve_into(off_ref, bi_ref, fm_ref, bm_ref, force_ref, pres_ref, sv_ref, sp_ref, msg_ref, coef_ref, xs_ref)
+
+
 def correct_kernel(coef_ref, own_ref, recv_ref, sv_ref, sp_ref, nv_ref, np_ref):
-    rows = sv_ref.shape[0]
-    levels = coef_ref.shape[1]
-    per = rows // levels
+    rows, lanes = sv_ref.shape
+    per = (own_ref.shape[0] - 4) // 2
     own0 = own_ref[0:per, :]
     own1 = own_ref[per : 2 * per, :]
     extra = [recv_ref[2 * per + i : 2 * per + i + 1, :] for i in range(4)]
     v0 = recv_ref[0:per, :] + extra[0] * own0 + extra[1] * own1
     v1 = recv_ref[per : 2 * per, :] + extra[2] * own0 + extra[3] * own1
-
-    def fix(k, carry):
-        at = pl.ds(pl.multiple_of(k * per, per), per)
-        nv_ref[at, :] = sv_ref[at, :] + (coef_ref[0, k] * v0 + coef_ref[1, k] * v1)
-        np_ref[at, :] = sp_ref[at, :] + (coef_ref[2, k] * v0 + coef_ref[3, k] * v1)
-        return carry
-
-    lax.fori_loop(0, levels, fix, 0, unroll=8)
-
-
-def solve_split(force_view, pres_view, levels, block_inverse, forward_map, backward_map):
+    phase = lax.broadcasted_iota(jnp.int32, (rows, lanes), 0) % per
+    t0 = jnp.zeros((rows, lanes), jnp.float32)
+    t1 = jnp.zeros((rows, lanes), jnp.float32)
+    for p in range(per):
+        t0 = jnp.where(phase == p, v0[p : p + 1], t0)
+        t1 = jnp.where(phase == p, v1[p : p + 1], t1)
+    nv_ref[...] = sv_ref[...] + (coef_ref[0] * t0 + coef_ref[1] * t1)
+    np_ref[...] = sp_ref[...] + (coef_ref[2] * t0 + coef_ref[3] * t1)
+
+
+def settle_and_solve(faces_in, sat_view, heat_res, vel_view, pres_view, levels, block_inverse, forward_map, backward_map):
     assert lax.axis_size("gz") == 2
-    rows, lanes = force_view.shape
+    packet_width, slot_count = faces_in[0].shape
+    record_width = packet_width - 1
+    rows, lanes = sat_view.shape
     per = rows // levels
     offset = jnp.full((1,), lax.axis_index("gz") * levels, jnp.int32)
     smem = pl.BlockSpec(memory_space=pltpu.SMEM)
     vmem = pl.BlockSpec(memory_space=pltpu.VMEM)
-    sv, sp, message, coef = pl.pallas_call(
-        solve_kernel,
+    arrived, sv, sp, message, coef = pl.pallas_call(
+        arrive_solve_kernel,
         out_shape=(
+            jax.ShapeDtypeStruct((len(faces_in), record_width, slot_count), jnp.float32),
             jax.ShapeDtypeStruct((rows, lanes), jnp.float32),
             jax.ShapeDtypeStruct((rows, lanes), jnp.float32),
             jax.ShapeDtypeStruct((2 * per + 4, lanes), jnp.float32),
-            jax.ShapeDtypeStruct((4, levels), jnp.float32),
-        ),
-        in_specs=[smem, smem, smem, smem, vmem, vmem],
-        out_specs=(vmem, vmem, vmem, smem),
-        scratch_shapes=[pltpu.SMEM((4, levels), jnp.float32)],
+            jax.ShapeDtypeStruct((4, rows, lanes), jnp.float32),
+        ),
+        in_specs=[smem] * 4 + [vmem] * (len(faces_in) + 4),
+        out_specs=(vmem,) * 5,
+        scratch_shapes=[
+            pltpu.VMEM((rows, lanes), jnp.float32),
+            pltpu.SMEM((4, levels), jnp.float32),
+        ],
         cost_estimate=pl.CostEstimate(
-            flops=40 * rows * lanes, bytes_accessed=24 * rows * lanes, transcendentals=0
-        ),
-    )(offset, block_inverse, forward_map, backward_map, force_view, pres_view)
+            flops=8 * sat_view.size * len(faces_in) * slot_count + 40 * rows * lanes,
+            bytes_accessed=4 * (2 * packet_width) * len(faces_in) * slot_count + 40 * rows * lanes,
+            transcendentals=len(faces_in) * slot_count,
+        ),
+    )(offset, block_inverse, forward_map, backward_map, *faces_in, sat_view, heat_res, vel_view, pres_view)
     received = lax.ppermute(message, "gz", [(0, 1), (1, 0)])
-    return pl.pallas_call(
+    new_v, new_p = pl.pallas_call(
         correct_kernel,
         out_shape=(
             jax.ShapeDtypeStruct((rows, lanes), jnp.float32),
             jax.ShapeDtypeStruct((rows, lanes), jnp.float32),
         ),
-        in_specs=[smem, vmem, vmem, vmem, vmem],
+        in_specs=[vmem] * 5,
         out_specs=(vmem, vmem),
         cost_estimate=pl.CostEstimate(
-            flops=8 * rows * lanes, bytes_accessed=16 * rows * lanes, transcendentals=0
+            flops=8 * rows * lanes, bytes_accessed=32 * rows * lanes, transcendentals=0
         ),
     )(coef, message, received, sv, sp)
+    return arrived, new_v, new_p
 
 
 def along_x(packet_face, offset):
@@ -379,11 +370,16 @@
         staying.astype(jnp.float32).reshape(1, -1),
         sat_view,
     )
-    arrived, force_view = settle_arrivals(
-        (from_west, from_east, from_south, from_north), sat_view, heat_res, velocity.reshape(view)
-    )
-    solved_v, solved_p = solve_split(
-        force_view, pressure.reshape(view), levels, block_inverse, forward_map, backward_map
+    arrived, solved_v, solved_p = settle_and_solve(
+        (from_west, from_east, from_south, from_north),
+        sat_view,
+        heat_res,
+        velocity.reshape(view),
+        pressure.reshape(view),
+        levels,
+        block_inverse,
+        forward_map,
+        backward_map,
     )
     new_velocity = solved_v.reshape(velocity.shape)
     new_pressure = solved_p.reshape(pressure.shape)

time: 55.1 us -> 48.3 us (0.88)
  Pallas kernels: 15 us -> 11.8 us
  local copies, waits for them, and re-layouts: 4.59 us -> 2.14 us
  other arithmetic: 1.71 us -> 0.39 us
    pallas_call x3 -> x2, Pallas kernels: 8.42 us -> 6.43 us  [the longest x1 4.75 us: settle_and_solve(): pl.pallas_call(arrive_solve_kernel, out_shape=(jax.ShapeDtypeStruct((len(...]
    dynamic_update_slice x4 -> x0, local copies, waits for them, and re-layouts: 1.48 us -> none  [emit_packets(): lax.map(pick_block, (flat_leavers.reshape(-1, block_rows), flat_use.resha...]
    pallas_call x1, Pallas kernels: 6.6 us -> 5.33 us  [settle_residents(): pl.pallas_call(resident_kernel, grid=(drop_count // chunk,), out_shape=(j...]
    unnamed x23 -> x20, local copies, waits for them, and re-layouts: 2.84 us -> 2.07 us
    unnamed x1 -> x0, other arithmetic: 0.66 us -> none
    convert_element_type x2 -> x0, other arithmetic: 0.63 us -> none  [the longest x1 0.62 us: body(): staying.astype(jnp.float32).reshape(1, -1)]
    dot_general x2 -> x1, matrix products: 4.59 us -> 4.62 us  [pick_block(): jnp.einsum('nh,rhl->nrl', upper, table, precision=EXACT, preferred_elemen...]
  transfers between devices with their start and end apart: 5 -> 5, of which waited for: 1 -> 1; matrix products, arithmetic and copies ran while one was open for 1% -> 2% of each run, Pallas kernels for 12% -> 11%
where the time goes in v4:
time: 48.3 us; the launch traced here: 48 us
  starting transfers between devices  20.1 us (42%)
  Pallas kernels  11.8 us (24%)
  waiting for transfers between devices  7.26 us (15%)
  matrix products  5.54 us (11%)
  local copies, waits for them, and re-layouts  2.14 us (4%)
  between operations  0.86 us (2%)
    ppermute x4, starting transfers between devices, shifted(): return lax.ppermute(value, axis, pairs)  17.7 us
    ppermute x1, waiting for transfers between devices, settle_and_solve(): received = lax.ppermute(message, 'gz', [(0, 1), (1, 0)])  7.25 us
    pallas_call x1, Pallas kernels, settle_residents(): pl.pallas_call(resident_kernel, grid=(drop_count // chunk,), out_shape=(j...  5.33 us
    pallas_call x1, Pallas kernels, settle_and_solve(): pl.pallas_call(arrive_solve_kernel, out_shape=(jax.ShapeDtypeStruct((len(...  4.75 us
    dot_general x1, matrix products, pick_block(): jnp.einsum('nh,rhl->nrl', upper, table, precision=EXACT, preferred_elemen...  4.62 us
    ppermute x1, starting transfers between devices, settle_and_solve(): received = lax.ppermute(message, 'gz', [(0, 1), (1, 0)])  2.35 us
    unnamed x20, local copies, waits for them, and re-layouts  2.07 us
    pallas_call x1, Pallas kernels, settle_and_solve(): pl.pallas_call(correct_kernel, out_shape=(jax.ShapeDtypeStruct((rows, lan...  1.68 us
  transfers between devices with their start and end apart: 5, of which 1 were waited for; matrix products, arithmetic and copies ran while one was open for 2% of the time, Pallas kernels for 11%

profile of v4, /device:TPU:32, one launch (start us, length us, event | category | flops | bytes accessed | tf_op | source)
XLA Modules:
  0.0 48.0 jit_solution(15290441138360012208)
XLA Ops:
  0.6 0.0 copy-start
  0.6 0.0 copy-start.1
  0.7 0.7 %copy.22 = s32[1,4,4,128]{3,1,2,0:T(4,128)S(1)} copy(s32[1,4,4,128]{3,2,1,0:T(4,128)} %bitcast.54) | data formatting | bytes 16384
  1.4 0.1 fusion.1
  1.5 0.0 copy-done
  1.6 0.1 copy.33
  1.6 0.0 copy-done.1
  1.7 0.0 copy-start.3
  1.7 4.6 %multiply_reduce_fusion = f32[2048,9]{0,1:T(8,128)S(1)} fusion(f32[2048,128]{0,1:T(8,128)S(1)} %fusion.1, f32[1,64,128]{2,1,0:T(8,128)S(1)} %bitcast.53, f32[8,64,128]{2,1,0:T(8,128)S(1)} %bitcast.50, s32[2048]{0:T(1024)S(1)} %get-tuple-element.52), kind=kOutput, calls=%fused_computation | convolution fusion | flops 1816844288 | bytes 1425408 | tf_op jit(solution)/shard_map/while/body/eval_jaxpr/nh,rhl->nrl/dot_general | solution.py:50
  6.3 0.1 reshape.401
  6.4 0.0 copy-done.3
  6.4 0.1 iota_compare_fusion.2
  6.5 0.1 fusion.17
  6.7 3.4 %collective-permute-start = (f32[9,512]{1,0:T(8,128)S(1)}, f32[9,512]{1,0:T(8,128)S(1)}, u32[]{:S(2)}, u32[]{:S(2)}) collective-permute-start(f32[9,512]{1,0:T(8,128)S(1)} %get-tuple-element.51), channel_id=1, source_target_pairs={{0,32},{32,64},{64,96},{96,128},{128,160},{160,192},{192,224},{224... | collective-permute-start | bytes 55304 | tf_op jit(solution)/shard_map/ppermute | solution.py:24
  10.1 6.4 %collective-permute-start.1 = (f32[9,512]{1,0:T(8,128)S(1)}, f32[9,512]{1,0:T(8,128)S(1)}, u32[]{:S(2)}, u32[]{:S(2)}) collective-permute-start(f32[9,512]{1,0:T(8,128)S(1)} %get-tuple-element.50), channel_id=1, source_target_pairs={{0,480},{32,0},{64,32},{96,64},{128,96},{160,128},{192,160},{224,1... | collective-permute-start | bytes 55304 | tf_op jit(solution)/shard_map/ppermute | solution.py:24
  16.5 0.0 collective-permute-start.2
  16.5 7.9 %collective-permute-start.3 = (f32[9,512]{1,0:T(8,128)S(1)}, f32[9,512]{1,0:T(8,128)S(1)}, u32[]{:S(2)}, u32[]{:S(2)}) collective-permute-start(f32[9,512]{1,0:T(8,128)S(1)} %get-tuple-element.48), channel_id=1, source_target_pairs={{0,30},{2,0},{4,2},{6,4},{8,6},{10,8},{12,10},{14,12},{16,14},{18,... | collective-permute-start | bytes 55304 | tf_op jit(solution)/shard_map/ppermute | solution.py:24
  24.4 0.9 %fusion = f32[64,128]{1,0:T(8,128)} fusion(s32[2048]{0:T(1024)S(1)} %get-tuple-element.53, s32[2048]{0:T(1024)S(1)} %get-tuple-element.52, bf16[2048]{0:T(1024)(128)(2,1)S(1)} %bitcast.55), kind=kOutput, calls=%fused_computation.2 | convolution fusion | flops 35274752 | bytes 53248 | tf_op jit(solution)/shard_map/while/body/eval_jaxpr/nh,nl->hl/dot_general | solution.py:55
  25.3 5.3 %shard_map.129 = (f32[8,8192]{1,0:T(8,128)}, f32[128,128]{1,0:T(8,128)}) custom-call(f32[8,8192]{1,0:T(8,128)} %bitcast.48, s32[1,8192]{1,0:T(1,128)} %bitcast.52, f32[1,8192]{1,0:T(1,128)} %bitcast.65, f32[128,128]{1,0:T(8,128)} %bitcast.57), custom_call_target="tpu_custom_call" | custom-call | flops 1610612736 | bytes 589824 | tf_op jit(solution)/shard_map/pallas_call | solution.py:150
  30.7 0.0 collective-permute-done.w_ref
  30.7 0.0 copy-start.4
  30.7 0.0 collective-permute-done.1.e_ref
  30.7 0.0 copy-start.5
  30.7 0.0 collective-permute-done.2.s_ref
  30.7 0.0 copy-start.6
  30.7 0.0 collective-permute-done.3.n_ref
  30.7 0.0 copy-start.7
  30.8 0.5 %copy-done.4 = f32[9,512]{1,0:T(8,128)} copy-done((f32[9,512]{1,0:T(8,128)}, f32[9,512]{1,0:T(8,128)S(1)}, u32[]{:S(2)}) %copy-start.4) | copy-done | bytes 18456
  31.3 0.0 copy-done.5
  31.3 0.0 copy-done.6
  31.3 0.0 copy-done.7
  31.4 4.8 %shard_map.130 = (f32[4,8,512]{2,1,0:T(8,128)}, f32[128,128]{1,0:T(8,128)}, f32[128,128]{1,0:T(8,128)}, f32[8,128]{1,0:T(8,128)}, f32[4,128,128]{2,1,0:T(8,128)}) custom-call(s32[1]{0:T(128)} %bitcast.8.off_ref, f32[4,128]{1,0:T(4,128)} %bi_ref.1, f32[4,128]{1,0:T(4,128)} %fm_ref.1, f32[4,128]{1,0:T(4,128)} %bm_ref.1, f32[9,512]{1,0:T(8,128)} %copy-done.4, ...), custom_call_target="tpu_custom_call" | custom-call | flops 269090816 | bytes 802816 | tf_op jit(solution)/shard_map/pallas_call | solution.py:298
  36.1 2.4 %collective-permute-start.4 = (f32[8,128]{1,0:T(8,128)}, f32[8,128]{1,0:T(8,128)S(1)}, u32[]{:S(2)}, u32[]{:S(2)}) collective-permute-start(f32[8,128]{1,0:T(8,128)} %get-tuple-element.35.own_ref), channel_id=1, source_target_pairs={{0,1},{1,0},{2,3},{3,2},{4,5},{5,4},{6,7},{7,6},{8,9},{9,8},{10,11... | collective-permute-start | bytes 12296 | tf_op jit(solution)/shard_map/ppermute | solution.py:319
  38.5 7.2 %collective-permute-done.4.recv_ref = f32[8,128]{1,0:T(8,128)S(1)} collective-permute-done((f32[8,128]{1,0:T(8,128)}, f32[8,128]{1,0:T(8,128)S(1)}, u32[]{:S(2)}, u32[]{:S(2)}) %collective-permute-start.4) | collective-permute-done | bytes 4128 | tf_op jit(solution)/shard_map/ppermute | solution.py:319
  45.7 0.0 copy-start.2
  45.7 0.6 %copy-done.2 = f32[8,128]{1,0:T(8,128)} copy-done((f32[8,128]{1,0:T(8,128)}, f32[8,128]{1,0:T(8,128)S(1)}, u32[]{:S(2)}) %copy-start.2) | copy-done | bytes 4120
  46.3 1.7 %shard_map.131 = (f32[128,128]{1,0:T(8,128)}, f32[128,128]{1,0:T(8,128)}) custom-call(f32[4,128,128]{2,1,0:T(8,128)} %get-tuple-element.34.coef_ref, f32[8,128]{1,0:T(8,128)} %get-tuple-element.35.own_ref, f32[8,128]{1,0:T(8,128)} %copy-done.2, f32[128,128]{1,0:T(8,128)} %get-tuple-element.36.sv_ref, f32[128,128]{1,0:T(8,128)} %get-tuple-element.37.sp_ref), custom_call_target="tpu_custom_call" | custom-call | flops 131072 | bytes 524288 | tf_op jit(solution)/shard_map/pallas_call | solution.py:320
  (10 shorter events, 0.1 us)
Async XLA Ops:
  0.6 1.0 %copy-start = (f32[1,1,1,8,8192]{4,3,2,1,0:T(8,128)S(1)}, f32[1,1,1,8,8192]{4,3,2,1,0:T(8,128)}, u32[]{:S(2)}) copy-start(f32[1,1,1,8,8192]{4,3,2,1,0:T(8,128)} %param.10) | copy-start | bytes 786436
  0.6 1.0 %copy-start.1 = (s32[1,1,1,8192]{3,2,1,0:T(1,128)S(1)}, s32[1,1,1,8192]{3,2,1,0:T(1,128)}, u32[]{:S(2)}) copy-start(s32[1,1,1,8192]{3,2,1,0:T(1,128)} %param.11) | copy-start | bytes 98308
  1.7 4.8 %copy-start.3 = (s32[1,1,1,4]{3,2,1,0:T(1,128)S(1)}, s32[1,1,1,4]{3,2,1,0:T(1,128)}, u32[]{:S(2)}) copy-start(s32[1,1,1,4]{3,2,1,0:T(1,128)} %param.13) | copy-start | bytes 52
  6.7 24.0 %collective-permute-start = (f32[9,512]{1,0:T(8,128)S(1)}, f32[9,512]{1,0:T(8,128)S(1)}, u32[]{:S(2)}, u32[]{:S(2)}) collective-permute-start(f32[9,512]{1,0:T(8,128)S(1)} %get-tuple-element.51), channel_id=1, source_target_pairs={{0,32},{32,64},{64,96},{96,128},{128,160},{160,192},{192,224},{224... | collective-permute-start | bytes 55304 | tf_op jit(solution)/shard_map/ppermute | solution.py:24
  10.1 20.6 %collective-permute-start.1 = (f32[9,512]{1,0:T(8,128)S(1)}, f32[9,512]{1,0:T(8,128)S(1)}, u32[]{:S(2)}, u32[]{:S(2)}) collective-permute-start(f32[9,512]{1,0:T(8,128)S(1)} %get-tuple-element.50), channel_id=1, source_target_pairs={{0,480},{32,0},{64,32},{96,64},{128,96},{160,128},{192,160},{224,1... | collective-permute-start | bytes 55304 | tf_op jit(solution)/shard_map/ppermute | solution.py:24
  16.5 14.3 %collective-permute-start.2 = (f32[9,512]{1,0:T(8,128)S(1)}, f32[9,512]{1,0:T(8,128)S(1)}, u32[]{:S(2)}, u32[]{:S(2)}) collective-permute-start(f32[9,512]{1,0:T(8,128)S(1)} %get-tuple-element.49), channel_id=1, source_target_pairs={{0,2},{2,4},{4,6},{6,8},{8,10},{10,12},{12,14},{14,16},{16,18},{18... | collective-permute-start | bytes 55304 | tf_op jit(solution)/shard_map/ppermute | solution.py:24
  16.5 14.2 %collective-permute-start.3 = (f32[9,512]{1,0:T(8,128)S(1)}, f32[9,512]{1,0:T(8,128)S(1)}, u32[]{:S(2)}, u32[]{:S(2)}) collective-permute-start(f32[9,512]{1,0:T(8,128)S(1)} %get-tuple-element.48), channel_id=1, source_target_pairs={{0,30},{2,0},{4,2},{6,4},{8,6},{10,8},{12,10},{14,12},{16,14},{18,... | collective-permute-start | bytes 55304 | tf_op jit(solution)/shard_map/ppermute | solution.py:24
  30.7 0.6 %copy-start.4 = (f32[9,512]{1,0:T(8,128)}, f32[9,512]{1,0:T(8,128)S(1)}, u32[]{:S(2)}) copy-start(f32[9,512]{1,0:T(8,128)S(1)} %collective-permute-done.w_ref) | copy-start | bytes 55300
  30.7 0.6 %copy-start.5 = (f32[9,512]{1,0:T(8,128)}, f32[9,512]{1,0:T(8,128)S(1)}, u32[]{:S(2)}) copy-start(f32[9,512]{1,0:T(8,128)S(1)} %collective-permute-done.1.e_ref) | copy-start | bytes 55300
  30.7 0.6 %copy-start.6 = (f32[9,512]{1,0:T(8,128)}, f32[9,512]{1,0:T(8,128)S(1)}, u32[]{:S(2)}) copy-start(f32[9,512]{1,0:T(8,128)S(1)} %collective-permute-done.2.s_ref) | copy-start | bytes 55300
  30.7 0.6 %copy-start.7 = (f32[9,512]{1,0:T(8,128)}, f32[9,512]{1,0:T(8,128)S(1)}, u32[]{:S(2)}) copy-start(f32[9,512]{1,0:T(8,128)S(1)} %collective-permute-done.3.n_ref) | copy-start | bytes 55300
  36.1 9.6 %collective-permute-start.4 = (f32[8,128]{1,0:T(8,128)}, f32[8,128]{1,0:T(8,128)S(1)}, u32[]{:S(2)}, u32[]{:S(2)}) collective-permute-start(f32[8,128]{1,0:T(8,128)} %get-tuple-element.35.own_ref), channel_id=1, source_target_pairs={{0,1},{1,0},{2,3},{3,2},{4,5},{5,4},{6,7},{7,6},{8,9},{9,8},{10,11... | collective-permute-start | bytes 12296 | tf_op jit(solution)/shard_map/ppermute | solution.py:319
  45.7 0.6 %copy-start.2 = (f32[8,128]{1,0:T(8,128)}, f32[8,128]{1,0:T(8,128)S(1)}, u32[]{:S(2)}) copy-start(f32[8,128]{1,0:T(8,128)S(1)} %collective-permute-done.4.recv_ref) | copy-start | bytes 12292

commit v5 on v4

--- a/solution.py
+++ b/solution.py
@@ -73,6 +73,81 @@
     packet = jnp.concatenate([picked, target.astype(records.dtype)[:, None, :]], axis=1)
     packet = jnp.where(in_use[:, None, :], packet, 0.0)
     return (packet, departed == 0.0)
+
+
+def emit_kernel(count_ref, view_ref, cells_ref, cross_ref, *outs):
+    face_refs = outs[:-1]
+    stay_ref = outs[-1]
+    view_rows, lanes = view_ref.shape
+    outer = cells_ref.shape[0]
+    record_width = view_rows // outer
+    slot_count = cross_ref.shape[1]
+    shift = lanes.bit_length() - 1
+    rec_stack = jnp.concatenate(split_pieces3(view_ref[...]), axis=0)
+    cell_stack = jnp.concatenate(split_pieces3(cells_ref[...].astype(jnp.float32)), axis=0)
+    counted = jnp.zeros((outer, lanes), jnp.float32)
+    for face, out_ref in enumerate(face_refs):
+        index = cross_ref[face : face + 1, :]
+        high = lax.shift_right_logical(index, shift)
+        low = jnp.bitwise_and(index, lanes - 1)
+        lane_hot = jnp.where(
+            lax.broadcasted_iota(jnp.int32, (lanes, slot_count), 0) == low, 1.0, 0.0
+        ).astype(jnp.bfloat16)
+        high_mask = lax.broadcasted_iota(jnp.int32, (outer, slot_count), 0) == high
+        got = jnp.dot(rec_stack, lane_hot, preferred_element_type=jnp.float32)
+        got = got[:view_rows] + got[view_rows : 2 * view_rows] + got[2 * view_rows :]
+        got = got.reshape(outer, record_width, slot_count)
+        picked = jnp.sum(jnp.where(high_mask[:, None, :], got, 0.0), axis=0)
+        got_cell = jnp.dot(cell_stack, lane_hot, preferred_element_type=jnp.float32)
+        got_cell = got_cell[:outer] + got_cell[outer : 2 * outer] + got_cell[2 * outer :]
+        source = (jnp.sum(jnp.where(high_mask, got_cell, 0.0), axis=0, keepdims=True) + 0.5).astype(jnp.int32)
+        height = lax.shift_right_logical(source, (CX * CY).bit_length() - 1)
+        cell_x = jnp.bitwise_and(lax.shift_right_logical(source, CY.bit_length() - 1), CX - 1)
+        cell_y = jnp.bitwise_and(source, CY - 1)
+        new_x = 0 if face == 0 else (CX - 1 if face == 1 else cell_x)
+        new_y = 0 if face == 2 else (CY - 1 if face == 3 else cell_y)
+        target = (height * (CX * CY) + new_x * CY + new_y).astype(jnp.float32)
+        in_use = lax.broadcasted_iota(jnp.int32, (1, slot_count), 1) < count_ref[face]
+        packet = jnp.concatenate([picked, jnp.broadcast_to(target, (1, slot_count))], axis=0)
+        out_ref[...] = jnp.where(in_use, packet, 0.0)
+        used_high = jnp.where(high_mask & in_use, 1.0, 0.0).astype(jnp.bfloat16)
+        counted = counted + lax.dot_general(
+            used_high, lane_hot, (((1,), (1,)), ((), ())), preferred_element_type=jnp.float32
+        )
+    stay_ref[...] = jnp.where(counted == 0.0, 1.0, 0.0)
+
+
+def emit_faces(records, cell_index, crossing, crossing_count):
+    record_width, drop_count = records.shape
+    lanes = 128
+    outer = drop_count // lanes
+    faces, slot_count = crossing.shape
+    view = records.reshape(record_width, outer, lanes).transpose(1, 0, 2).reshape(outer * record_width, lanes)
+    smem = pl.BlockSpec(memory_space=pltpu.SMEM)
+    vmem = pl.BlockSpec(memory_space=pltpu.VMEM)
+    results = pl.pallas_call(
+        emit_kernel,
+        out_shape=tuple(
+            jax.ShapeDtypeStruct((record_width + 1, slot_count), jnp.float32) for _ in range(faces)
+        )
+        + (jax.ShapeDtypeStruct((outer, lanes), jnp.float32),),
+        in_specs=[smem, vmem, vmem, vmem],
+        out_specs=(vmem,) * (faces + 1),
+        cost_estimate=pl.CostEstimate(
+            flops=6 * (record_width + 1) * drop_count * faces * slot_count // outer,
+            bytes_accessed=4 * (record_width + 1) * drop_count + 8 * (record_width + 1) * faces * slot_count,
+            transcendentals=0,
+        ),
+    )(crossing_count, view, cell_index.reshape(outer, lanes), crossing)
+    return results[:faces], results[faces]
+
+
+def split_pieces3(value):
+    high = value.astype(jnp.bfloat16)
+    rest = value - high.astype(jnp.float32)
+    middle = rest.astype(jnp.bfloat16)
+    low = (rest - middle.astype(jnp.float32)).astype(jnp.bfloat16)
+    return (high, middle, low)
 
 
 def split_pieces(value):
@@ -357,17 +432,17 @@
     levels = saturation.shape[0]
     view = (saturation.size // 128, 128)
     sat_view = saturation.reshape(view)
-    packet, staying = emit_packets(
-        records, cell_ids, crossing[0, 0, 0], crossing_count[0, 0, 0], CX, CY
-    )
-    from_west = along_x(packet[0], 1)
-    from_east = along_x(packet[1], -1)
-    from_south = along_y(packet[2], 1)
-    from_north = along_y(packet[3], -1)
+    faces_out, staying_view = emit_faces(
+        records, cell_index, crossing[0, 0, 0], crossing_count[0, 0, 0]
+    )
+    from_west = along_x(faces_out[0], 1)
+    from_east = along_x(faces_out[1], -1)
+    from_south = along_y(faces_out[2], 1)
+    from_north = along_y(faces_out[3], -1)
     resident, heat_res = settle_residents(
         records,
         cell_index.reshape(1, -1),
-        staying.astype(jnp.float32).reshape(1, -1),
+        staying_view.reshape(1, -1),
         sat_view,
     )
     arrived, solved_v, solved_p = settle_and_solve(

time: 48.3 us -> 45.2 us (0.936)
  matrix products: 5.54 us -> 0 us
  Pallas kernels: 11.8 us -> 15.7 us
  local copies, waits for them, and re-layouts: 2.14 us -> 1.18 us
    dot_general x2 -> x0, matrix products: 5.54 us -> none  [the longest x1 4.62 us: pick_block(): jnp.einsum('nh,rhl->nrl', upper, table, precision=EXACT, preferred_elemen...]
    pallas_call x0 -> x1, Pallas kernels: none -> 4 us  [emit_faces(): pl.pallas_call(emit_kernel, out_shape=tuple((jax.ShapeDtypeStruct((record...]
    unnamed x20 -> x10, local copies, waits for them, and re-layouts: 2.07 us -> 1.18 us
  transfers between devices with their start and end apart: 5 -> 5, of which waited for: 1 -> 1; matrix products, arithmetic and copies ran while one was open for 2% -> 0% of each run, Pallas kernels for 11% -> 12%
where the time goes in v5:
time: 45.2 us; the launch traced here: 45 us
  starting transfers between devices  20.1 us (44%)
  Pallas kernels  15.7 us (35%)
  waiting for transfers between devices  7.24 us (16%)
  local copies, waits for them, and re-layouts  1.18 us (3%)
  between operations  0.73 us (2%)
    ppermute x4, starting transfers between devices, shifted(): return lax.ppermute(value, axis, pairs)  17.7 us
    ppermute x1, waiting for transfers between devices, settle_and_solve(): received = lax.ppermute(message, 'gz', [(0, 1), (1, 0)])  7.23 us
    pallas_call x1, Pallas kernels, settle_residents(): pl.pallas_call(resident_kernel, grid=(drop_count // chunk,), out_shape=(j...  5.32 us
    pallas_call x1, Pallas kernels, settle_and_solve(): pl.pallas_call(arrive_solve_kernel, out_shape=(jax.ShapeDtypeStruct((len(...  4.74 us
    pallas_call x1, Pallas kernels, emit_faces(): pl.pallas_call(emit_kernel, out_shape=tuple((jax.ShapeDtypeStruct((record...  4 us
    ppermute x1, starting transfers between devices, settle_and_solve(): received = lax.ppermute(message, 'gz', [(0, 1), (1, 0)])  2.37 us
    pallas_call x1, Pallas kernels, settle_and_solve(): pl.pallas_call(correct_kernel, out_shape=(jax.ShapeDtypeStruct((rows, lan...  1.68 us
    unnamed x10, local copies, waits for them, and re-layouts  1.18 us
  transfers between devices with their start and end apart: 5, of which 1 were waited for; matrix products, arithmetic and copies ran while one was open for 0% of the time, Pallas kernels for 12%

profile of v5, /device:TPU:32, one launch (start us, length us, event | category | flops | bytes accessed | tf_op | source)
XLA Modules:
  0.0 45.0 jit_solution(13558880016508083563)
XLA Ops:
  0.6 4.0 %shard_map.129 = (f32[9,512]{1,0:T(8,128)}, f32[9,512]{1,0:T(8,128)}, f32[9,512]{1,0:T(8,128)}, f32[9,512]{1,0:T(8,128)}, f32[64,128]{1,0:T(8,128)}) custom-call(s32[4]{0:T(128)} %bitcast.24, f32[512,128]{1,0:T(8,128)} %bitcast.19, s32[64,128]{1,0:T(8,128)} %bitcast.21, s32[4,512]{1,0:T(4,128)} %bitcast.23), custom_call_target="tpu_custom_call" | custom-call | flops 14155776 | bytes 442368 | tf_op jit(solution)/shard_map/pallas_call | solution.py:128
  4.6 3.4 %collective-permute-start = (f32[9,512]{1,0:T(8,128)}, f32[9,512]{1,0:T(8,128)S(1)}, u32[]{:S(2)}, u32[]{:S(2)}) collective-permute-start(f32[9,512]{1,0:T(8,128)} %get-tuple-element.20), channel_id=1, source_target_pairs={{0,32},{32,64},{64,96},{96,128},{128,160},{160,192},{192,224},{224... | collective-permute-start | bytes 55304 | tf_op jit(solution)/shard_map/ppermute | solution.py:24
  8.0 6.4 %collective-permute-start.1 = (f32[9,512]{1,0:T(8,128)}, f32[9,512]{1,0:T(8,128)S(1)}, u32[]{:S(2)}, u32[]{:S(2)}) collective-permute-start(f32[9,512]{1,0:T(8,128)} %get-tuple-element.21), channel_id=1, source_target_pairs={{0,480},{32,0},{64,32},{96,64},{128,96},{160,128},{192,160},{224,1... | collective-permute-start | bytes 55304 | tf_op jit(solution)/shard_map/ppermute | solution.py:24
  14.4 0.0 collective-permute-start.2
  14.4 7.9 %collective-permute-start.3 = (f32[9,512]{1,0:T(8,128)}, f32[9,512]{1,0:T(8,128)S(1)}, u32[]{:S(2)}, u32[]{:S(2)}) collective-permute-start(f32[9,512]{1,0:T(8,128)} %get-tuple-element.23), channel_id=1, source_target_pairs={{0,30},{2,0},{4,2},{6,4},{8,6},{10,8},{12,10},{14,12},{16,14},{18,... | collective-permute-start | bytes 55304 | tf_op jit(solution)/shard_map/ppermute | solution.py:24
  22.3 5.3 %shard_map.130 = (f32[8,8192]{1,0:T(8,128)}, f32[128,128]{1,0:T(8,128)}) custom-call(f32[8,8192]{1,0:T(8,128)} %bitcast.20, s32[1,8192]{1,0:T(1,128)} %bitcast.22, f32[1,8192]{1,0:T(1,128)} %bitcast.31, f32[128,128]{1,0:T(8,128)} %bitcast.25), custom_call_target="tpu_custom_call" | custom-call | flops 1610612736 | bytes 589824 | tf_op jit(solution)/shard_map/pallas_call | solution.py:225
  27.7 0.0 collective-permute-done.w_ref
  27.7 0.0 copy-start.1
  27.7 0.0 collective-permute-done.1.e_ref
  27.7 0.0 copy-start.2
  27.7 0.0 collective-permute-done.2.s_ref
  27.7 0.0 copy-start.3
  27.7 0.0 collective-permute-done.3.n_ref
  27.7 0.0 copy-start.4
  27.7 0.5 %copy-done.1 = f32[9,512]{1,0:T(8,128)} copy-done((f32[9,512]{1,0:T(8,128)}, f32[9,512]{1,0:T(8,128)S(1)}, u32[]{:S(2)}) %copy-start.1) | copy-done | bytes 18456
  28.3 0.0 copy-done.2
  28.3 0.0 copy-done.3
  28.3 0.0 copy-done.4
  28.3 4.7 %shard_map.131 = (f32[4,8,512]{2,1,0:T(8,128)}, f32[128,128]{1,0:T(8,128)}, f32[128,128]{1,0:T(8,128)}, f32[8,128]{1,0:T(8,128)}, f32[4,128,128]{2,1,0:T(8,128)}) custom-call(s32[1]{0:T(128)} %bitcast.11.off_ref, f32[4,128]{1,0:T(4,128)} %bi_ref.1, f32[4,128]{1,0:T(4,128)} %fm_ref.1, f32[4,128]{1,0:T(4,128)} %bm_ref.1, f32[9,512]{1,0:T(8,128)} %copy-done.1, ...), custom_call_target="tpu_custom_call" | custom-call | flops 269090816 | bytes 802816 | tf_op jit(solution)/shard_map/pallas_call | solution.py:373
  33.1 2.4 %collective-permute-start.4 = (f32[8,128]{1,0:T(8,128)}, f32[8,128]{1,0:T(8,128)S(1)}, u32[]{:S(2)}, u32[]{:S(2)}) collective-permute-start(f32[8,128]{1,0:T(8,128)} %get-tuple-element.27.own_ref), channel_id=1, source_target_pairs={{0,1},{1,0},{2,3},{3,2},{4,5},{5,4},{6,7},{7,6},{8,9},{9,8},{10,11... | collective-permute-start | bytes 12296 | tf_op jit(solution)/shard_map/ppermute | solution.py:394
  35.5 7.2 %collective-permute-done.4.recv_ref = f32[8,128]{1,0:T(8,128)S(1)} collective-permute-done((f32[8,128]{1,0:T(8,128)}, f32[8,128]{1,0:T(8,128)S(1)}, u32[]{:S(2)}, u32[]{:S(2)}) %collective-permute-start.4) | collective-permute-done | bytes 4128 | tf_op jit(solution)/shard_map/ppermute | solution.py:394
  42.7 0.0 copy-start
  42.7 0.6 %copy-done = f32[8,128]{1,0:T(8,128)} copy-done((f32[8,128]{1,0:T(8,128)}, f32[8,128]{1,0:T(8,128)S(1)}, u32[]{:S(2)}) %copy-start) | copy-done | bytes 4120
  43.3 1.7 %shard_map.132 = (f32[128,128]{1,0:T(8,128)}, f32[128,128]{1,0:T(8,128)}) custom-call(f32[4,128,128]{2,1,0:T(8,128)} %get-tuple-element.26.coef_ref, f32[8,128]{1,0:T(8,128)} %get-tuple-element.27.own_ref, f32[8,128]{1,0:T(8,128)} %copy-done, f32[128,128]{1,0:T(8,128)} %get-tuple-element.28.sv_ref, f32[128,128]{1,0:T(8,128)} %get-tuple-element.29.sp_ref), custom_call_target="tpu_custom_call" | custom-call | flops 131072 | bytes 524288 | tf_op jit(solution)/shard_map/pallas_call | solution.py:395
Async XLA Ops:
  4.6 23.0 %collective-permute-start = (f32[9,512]{1,0:T(8,128)}, f32[9,512]{1,0:T(8,128)S(1)}, u32[]{:S(2)}, u32[]{:S(2)}) collective-permute-start(f32[9,512]{1,0:T(8,128)} %get-tuple-element.20), channel_id=1, source_target_pairs={{0,32},{32,64},{64,96},{96,128},{128,160},{160,192},{192,224},{224... | collective-permute-start | bytes 55304 | tf_op jit(solution)/shard_map/ppermute | solution.py:24
  8.0 19.7 %collective-permute-start.1 = (f32[9,512]{1,0:T(8,128)}, f32[9,512]{1,0:T(8,128)S(1)}, u32[]{:S(2)}, u32[]{:S(2)}) collective-permute-start(f32[9,512]{1,0:T(8,128)} %get-tuple-element.21), channel_id=1, source_target_pairs={{0,480},{32,0},{64,32},{96,64},{128,96},{160,128},{192,160},{224,1... | collective-permute-start | bytes 55304 | tf_op jit(solution)/shard_map/ppermute | solution.py:24
  14.4 13.3 %collective-permute-start.2 = (f32[9,512]{1,0:T(8,128)}, f32[9,512]{1,0:T(8,128)S(1)}, u32[]{:S(2)}, u32[]{:S(2)}) collective-permute-start(f32[9,512]{1,0:T(8,128)} %get-tuple-element.22), channel_id=1, source_target_pairs={{0,2},{2,4},{4,6},{6,8},{8,10},{10,12},{12,14},{14,16},{16,18},{18... | collective-permute-start | bytes 55304 | tf_op jit(solution)/shard_map/ppermute | solution.py:24
  14.4 13.3 %collective-permute-start.3 = (f32[9,512]{1,0:T(8,128)}, f32[9,512]{1,0:T(8,128)S(1)}, u32[]{:S(2)}, u32[]{:S(2)}) collective-permute-start(f32[9,512]{1,0:T(8,128)} %get-tuple-element.23), channel_id=1, source_target_pairs={{0,30},{2,0},{4,2},{6,4},{8,6},{10,8},{12,10},{14,12},{16,14},{18,... | collective-permute-start | bytes 55304 | tf_op jit(solution)/shard_map/ppermute | solution.py:24
  27.7 0.6 %copy-start.1 = (f32[9,512]{1,0:T(8,128)}, f32[9,512]{1,0:T(8,128)S(1)}, u32[]{:S(2)}) copy-start(f32[9,512]{1,0:T(8,128)S(1)} %collective-permute-done.w_ref) | copy-start | bytes 55300
  27.7 0.6 %copy-start.2 = (f32[9,512]{1,0:T(8,128)}, f32[9,512]{1,0:T(8,128)S(1)}, u32[]{:S(2)}) copy-start(f32[9,512]{1,0:T(8,128)S(1)} %collective-permute-done.1.e_ref) | copy-start | bytes 55300
  27.7 0.6 %copy-start.3 = (f32[9,512]{1,0:T(8,128)}, f32[9,512]{1,0:T(8,128)S(1)}, u32[]{:S(2)}) copy-start(f32[9,512]{1,0:T(8,128)S(1)} %collective-permute-done.2.s_ref) | copy-start | bytes 55300
  27.7 0.6 %copy-start.4 = (f32[9,512]{1,0:T(8,128)}, f32[9,512]{1,0:T(8,128)S(1)}, u32[]{:S(2)}) copy-start(f32[9,512]{1,0:T(8,128)S(1)} %collective-permute-done.3.n_ref) | copy-start | bytes 55300
  33.1 9.6 %collective-permute-start.4 = (f32[8,128]{1,0:T(8,128)}, f32[8,128]{1,0:T(8,128)S(1)}, u32[]{:S(2)}, u32[]{:S(2)}) collective-permute-start(f32[8,128]{1,0:T(8,128)} %get-tuple-element.27.own_ref), channel_id=1, source_target_pairs={{0,1},{1,0},{2,3},{3,2},{4,5},{5,4},{6,7},{7,6},{8,9},{9,8},{10,11... | collective-permute-start | bytes 12296 | tf_op jit(solution)/shard_map/ppermute | solution.py:394
  42.7 0.6 %copy-start = (f32[8,128]{1,0:T(8,128)}, f32[8,128]{1,0:T(8,128)S(1)}, u32[]{:S(2)}) copy-start(f32[8,128]{1,0:T(8,128)S(1)} %collective-permute-done.4.recv_ref) | copy-start | bytes 12292

commit v6 on v5

--- a/solution.py
+++ b/solution.py
@@ -83,23 +83,25 @@
     record_width = view_rows // outer
     slot_count = cross_ref.shape[1]
     shift = lanes.bit_length() - 1
-    rec_stack = jnp.concatenate(split_pieces3(view_ref[...]), axis=0)
-    cell_stack = jnp.concatenate(split_pieces3(cells_ref[...].astype(jnp.float32)), axis=0)
+    rec_stack = jnp.concatenate(split_pieces3(view_ref[...]), axis=1)
+    cell_stack = jnp.concatenate(split_pieces3(cells_ref[...].astype(jnp.float32)), axis=1)
     counted = jnp.zeros((outer, lanes), jnp.float32)
     for face, out_ref in enumerate(face_refs):
         index = cross_ref[face : face + 1, :]
         high = lax.shift_right_logical(index, shift)
         low = jnp.bitwise_and(index, lanes - 1)
         lane_hot = jnp.where(
-            lax.broadcasted_iota(jnp.int32, (lanes, slot_count), 0) == low, 1.0, 0.0
-        ).astype(jnp.bfloat16)
+            lax.broadcasted_iota(jnp.int32, (lanes, slot_count), 0).astype(jnp.bfloat16)
+            == low.astype(jnp.bfloat16),
+            jnp.bfloat16(1.0),
+            jnp.bfloat16(0.0),
+        )
         high_mask = lax.broadcasted_iota(jnp.int32, (outer, slot_count), 0) == high
-        got = jnp.dot(rec_stack, lane_hot, preferred_element_type=jnp.float32)
-        got = got[:view_rows] + got[view_rows : 2 * view_rows] + got[2 * view_rows :]
+        lane_hot3 = jnp.concatenate([lane_hot, lane_hot, lane_hot], axis=0)
+        got = jnp.dot(rec_stack, lane_hot3, preferred_element_type=jnp.float32)
         got = got.reshape(outer, record_width, slot_count)
         picked = jnp.sum(jnp.where(high_mask[:, None, :], got, 0.0), axis=0)
-        got_cell = jnp.dot(cell_stack, lane_hot, preferred_element_type=jnp.float32)
-        got_cell = got_cell[:outer] + got_cell[outer : 2 * outer] + got_cell[2 * outer :]
+        got_cell = jnp.dot(cell_stack, lane_hot3, preferred_element_type=jnp.float32)
         source = (jnp.sum(jnp.where(high_mask, got_cell, 0.0), axis=0, keepdims=True) + 0.5).astype(jnp.int32)
         height = lax.shift_right_logical(source, (CX * CY).bit_length() - 1)
         cell_x = jnp.bitwise_and(lax.shift_right_logical(source, CY.bit_length() - 1), CX - 1)
@@ -157,22 +159,21 @@
 
 
 def stacked_pieces(value):
-    return jnp.concatenate(split_pieces(value), axis=0)
+    return jnp.concatenate(split_pieces(value), axis=1)
 
 
 def condense_chunk(records, cells, occupied, sat_stack):
-    rows = sat_stack.shape[0] // 2
-    lanes = sat_stack.shape[1]
+    rows = sat_stack.shape[0]
+    lanes = sat_stack.shape[1] // 2
     width = cells.shape[1]
     shift = lanes.bit_length() - 1
     row_of = lax.shift_right_logical(cells, shift)
     lane_of = jnp.bitwise_and(cells, lanes - 1)
-    lane_mask = lax.broadcasted_iota(jnp.int32, (lanes, width), 0) == lane_of
-    lane_hot = jnp.where(lane_mask, 1.0, 0.0).astype(jnp.bfloat16)
+    lane_mask = lax.broadcasted_iota(jnp.int32, (lanes, width), 0).astype(jnp.bfloat16) == lane_of.astype(jnp.bfloat16)
+    lane_hot = jnp.where(lane_mask, jnp.bfloat16(1.0), jnp.bfloat16(0.0))
     row_mask = lax.broadcasted_iota(jnp.int32, (rows, width), 0) == row_of
-    row_hot = jnp.where(row_mask, 1.0, 0.0).astype(jnp.bfloat16)
-    picked = jnp.dot(sat_stack, lane_hot, preferred_element_type=jnp.float32)
-    picked = picked[:rows] + picked[rows:]
+    row_hot = jnp.where(lax.broadcasted_iota(jnp.int32, (rows, width), 0).astype(jnp.bfloat16) == row_of.astype(jnp.bfloat16), jnp.bfloat16(1.0), jnp.bfloat16(0.0))
+    picked = jnp.dot(sat_stack, jnp.concatenate([lane_hot, lane_hot], axis=0), preferred_element_type=jnp.float32)
     excess = jnp.sum(jnp.where(row_mask, picked, 0.0), axis=0, keepdims=True)
     radius = jnp.where(occupied, records[0:1], 1.0)
     dry_radius = records[2:3]

time: 45.2 us -> 43.6 us (0.965)
  Pallas kernels: 15.7 us -> 14.1 us
    pallas_call x1, Pallas kernels: 5.32 us -> 4.28 us  [settle_residents(): pl.pallas_call(resident_kernel, grid=(drop_count // chunk,), out_shape=(j...]
    pallas_call x1, Pallas kernels: 4 us -> 3.37 us  [emit_faces(): pl.pallas_call(emit_kernel, out_shape=tuple((jax.ShapeDtypeStruct((record...]
  transfers between devices with their start and end apart: 5 -> 5, of which waited for: 1 -> 1; matrix products, arithmetic and copies ran while one was open for 0% -> 0% of each run, Pallas kernels for 12% -> 10%
where the time goes in v6:
time: 43.6 us; the launch traced here: 43.3 us
  starting transfers between devices  20.1 us (46%)
  Pallas kernels  14.1 us (32%)
  waiting for transfers between devices  7.24 us (17%)
  local copies, waits for them, and re-layouts  1.18 us (3%)
  between operations  0.73 us (2%)
    ppermute x4, starting transfers between devices, shifted(): return lax.ppermute(value, axis, pairs)  17.7 us
    ppermute x1, waiting for transfers between devices, settle_and_solve(): received = lax.ppermute(message, 'gz', [(0, 1), (1, 0)])  7.23 us
    pallas_call x1, Pallas kernels, settle_and_solve(): pl.pallas_call(arrive_solve_kernel, out_shape=(jax.ShapeDtypeStruct((len(...  4.72 us
    pallas_call x1, Pallas kernels, settle_residents(): pl.pallas_call(resident_kernel, grid=(drop_count // chunk,), out_shape=(j...  4.28 us
    pallas_call x1, Pallas kernels, emit_faces(): pl.pallas_call(emit_kernel, out_shape=tuple((jax.ShapeDtypeStruct((record...  3.37 us
    ppermute x1, starting transfers between devices, settle_and_solve(): received = lax.ppermute(message, 'gz', [(0, 1), (1, 0)])  2.37 us
    pallas_call x1, Pallas kernels, settle_and_solve(): pl.pallas_call(correct_kernel, out_shape=(jax.ShapeDtypeStruct((rows, lan...  1.68 us
    unnamed x10, local copies, waits for them, and re-layouts  1.18 us
  transfers between devices with their start and end apart: 5, of which 1 were waited for; matrix products, arithmetic and copies ran while one was open for 0% of the time, Pallas kernels for 10%

profile of v6, /device:TPU:32, one launch (start us, length us, event | category | flops | bytes accessed | tf_op | source)
XLA Modules:
  0.0 43.3 jit_solution(11493305886442132778)
XLA Ops:
  0.6 3.4 %shard_map.129 = (f32[9,512]{1,0:T(8,128)}, f32[9,512]{1,0:T(8,128)}, f32[9,512]{1,0:T(8,128)}, f32[9,512]{1,0:T(8,128)}, f32[64,128]{1,0:T(8,128)}) custom-call(s32[4]{0:T(128)} %bitcast.24, f32[512,128]{1,0:T(8,128)} %bitcast.19, s32[64,128]{1,0:T(8,128)} %bitcast.21, s32[4,512]{1,0:T(4,128)} %bitcast.23), custom_call_target="tpu_custom_call" | custom-call | flops 14155776 | bytes 442368 | tf_op jit(solution)/shard_map/pallas_call | solution.py:130
  4.0 3.4 %collective-permute-start = (f32[9,512]{1,0:T(8,128)}, f32[9,512]{1,0:T(8,128)S(1)}, u32[]{:S(2)}, u32[]{:S(2)}) collective-permute-start(f32[9,512]{1,0:T(8,128)} %get-tuple-element.20), channel_id=1, source_target_pairs={{0,32},{32,64},{64,96},{96,128},{128,160},{160,192},{192,224},{224... | collective-permute-start | bytes 55304 | tf_op jit(solution)/shard_map/ppermute | solution.py:24
  7.4 6.3 %collective-permute-start.1 = (f32[9,512]{1,0:T(8,128)}, f32[9,512]{1,0:T(8,128)S(1)}, u32[]{:S(2)}, u32[]{:S(2)}) collective-permute-start(f32[9,512]{1,0:T(8,128)} %get-tuple-element.21), channel_id=1, source_target_pairs={{0,480},{32,0},{64,32},{96,64},{128,96},{160,128},{192,160},{224,1... | collective-permute-start | bytes 55304 | tf_op jit(solution)/shard_map/ppermute | solution.py:24
  13.8 0.0 collective-permute-start.2
  13.8 7.9 %collective-permute-start.3 = (f32[9,512]{1,0:T(8,128)}, f32[9,512]{1,0:T(8,128)S(1)}, u32[]{:S(2)}, u32[]{:S(2)}) collective-permute-start(f32[9,512]{1,0:T(8,128)} %get-tuple-element.23), channel_id=1, source_target_pairs={{0,30},{2,0},{4,2},{6,4},{8,6},{10,8},{12,10},{14,12},{16,14},{18,... | collective-permute-start | bytes 55304 | tf_op jit(solution)/shard_map/ppermute | solution.py:24
  21.7 4.3 %shard_map.130 = (f32[8,8192]{1,0:T(8,128)}, f32[128,128]{1,0:T(8,128)}) custom-call(f32[8,8192]{1,0:T(8,128)} %bitcast.20, s32[1,8192]{1,0:T(1,128)} %bitcast.22, f32[1,8192]{1,0:T(1,128)} %bitcast.31, f32[128,128]{1,0:T(8,128)} %bitcast.25), custom_call_target="tpu_custom_call" | custom-call | flops 1610612736 | bytes 589824 | tf_op jit(solution)/shard_map/pallas_call | solution.py:226
  26.0 0.0 collective-permute-done.w_ref
  26.0 0.0 copy-start.1
  26.0 0.0 collective-permute-done.1.e_ref
  26.0 0.0 copy-start.2
  26.0 0.0 collective-permute-done.2.s_ref
  26.1 0.0 copy-start.3
  26.1 0.0 collective-permute-done.3.n_ref
  26.1 0.0 copy-start.4
  26.1 0.5 %copy-done.1 = f32[9,512]{1,0:T(8,128)} copy-done((f32[9,512]{1,0:T(8,128)}, f32[9,512]{1,0:T(8,128)S(1)}, u32[]{:S(2)}) %copy-start.1) | copy-done | bytes 18456
  26.6 0.0 copy-done.2
  26.6 0.0 copy-done.3
  26.7 0.0 copy-done.4
  26.7 4.7 %shard_map.131 = (f32[4,8,512]{2,1,0:T(8,128)}, f32[128,128]{1,0:T(8,128)}, f32[128,128]{1,0:T(8,128)}, f32[8,128]{1,0:T(8,128)}, f32[4,128,128]{2,1,0:T(8,128)}) custom-call(s32[1]{0:T(128)} %bitcast.11.off_ref, f32[4,128]{1,0:T(4,128)} %bi_ref.1, f32[4,128]{1,0:T(4,128)} %fm_ref.1, f32[4,128]{1,0:T(4,128)} %bm_ref.1, f32[9,512]{1,0:T(8,128)} %copy-done.1, ...), custom_call_target="tpu_custom_call" | custom-call | flops 269090816 | bytes 802816 | tf_op jit(solution)/shard_map/pallas_call | solution.py:374
  31.4 2.4 %collective-permute-start.4 = (f32[8,128]{1,0:T(8,128)}, f32[8,128]{1,0:T(8,128)S(1)}, u32[]{:S(2)}, u32[]{:S(2)}) collective-permute-start(f32[8,128]{1,0:T(8,128)} %get-tuple-element.27.own_ref), channel_id=1, source_target_pairs={{0,1},{1,0},{2,3},{3,2},{4,5},{5,4},{6,7},{7,6},{8,9},{9,8},{10,11... | collective-permute-start | bytes 12296 | tf_op jit(solution)/shard_map/ppermute | solution.py:395
  33.8 7.2 %collective-permute-done.4.recv_ref = f32[8,128]{1,0:T(8,128)S(1)} collective-permute-done((f32[8,128]{1,0:T(8,128)}, f32[8,128]{1,0:T(8,128)S(1)}, u32[]{:S(2)}, u32[]{:S(2)}) %collective-permute-start.4) | collective-permute-done | bytes 4128 | tf_op jit(solution)/shard_map/ppermute | solution.py:395
  41.0 0.0 copy-start
  41.0 0.6 %copy-done = f32[8,128]{1,0:T(8,128)} copy-done((f32[8,128]{1,0:T(8,128)}, f32[8,128]{1,0:T(8,128)S(1)}, u32[]{:S(2)}) %copy-start) | copy-done | bytes 4120
  41.6 1.7 %shard_map.132 = (f32[128,128]{1,0:T(8,128)}, f32[128,128]{1,0:T(8,128)}) custom-call(f32[4,128,128]{2,1,0:T(8,128)} %get-tuple-element.26.coef_ref, f32[8,128]{1,0:T(8,128)} %get-tuple-element.27.own_ref, f32[8,128]{1,0:T(8,128)} %copy-done, f32[128,128]{1,0:T(8,128)} %get-tuple-element.28.sv_ref, f32[128,128]{1,0:T(8,128)} %get-tuple-element.29.sp_ref), custom_call_target="tpu_custom_call" | custom-call | flops 131072 | bytes 524288 | tf_op jit(solution)/shard_map/pallas_call | solution.py:396
Async XLA Ops:
  4.0 22.0 %collective-permute-start = (f32[9,512]{1,0:T(8,128)}, f32[9,512]{1,0:T(8,128)S(1)}, u32[]{:S(2)}, u32[]{:S(2)}) collective-permute-start(f32[9,512]{1,0:T(8,128)} %get-tuple-element.20), channel_id=1, source_target_pairs={{0,32},{32,64},{64,96},{96,128},{128,160},{160,192},{192,224},{224... | collective-permute-start | bytes 55304 | tf_op jit(solution)/shard_map/ppermute | solution.py:24
  7.4 18.6 %collective-permute-start.1 = (f32[9,512]{1,0:T(8,128)}, f32[9,512]{1,0:T(8,128)S(1)}, u32[]{:S(2)}, u32[]{:S(2)}) collective-permute-start(f32[9,512]{1,0:T(8,128)} %get-tuple-element.21), channel_id=1, source_target_pairs={{0,480},{32,0},{64,32},{96,64},{128,96},{160,128},{192,160},{224,1... | collective-permute-start | bytes 55304 | tf_op jit(solution)/shard_map/ppermute | solution.py:24
  13.8 12.3 %collective-permute-start.2 = (f32[9,512]{1,0:T(8,128)}, f32[9,512]{1,0:T(8,128)S(1)}, u32[]{:S(2)}, u32[]{:S(2)}) collective-permute-start(f32[9,512]{1,0:T(8,128)} %get-tuple-element.22), channel_id=1, source_target_pairs={{0,2},{2,4},{4,6},{6,8},{8,10},{10,12},{12,14},{14,16},{16,18},{18... | collective-permute-start | bytes 55304 | tf_op jit(solution)/shard_map/ppermute | solution.py:24
  13.8 12.3 %collective-permute-start.3 = (f32[9,512]{1,0:T(8,128)}, f32[9,512]{1,0:T(8,128)S(1)}, u32[]{:S(2)}, u32[]{:S(2)}) collective-permute-start(f32[9,512]{1,0:T(8,128)} %get-tuple-element.23), channel_id=1, source_target_pairs={{0,30},{2,0},{4,2},{6,4},{8,6},{10,8},{12,10},{14,12},{16,14},{18,... | collective-permute-start | bytes 55304 | tf_op jit(solution)/shard_map/ppermute | solution.py:24
  26.0 0.6 %copy-start.1 = (f32[9,512]{1,0:T(8,128)}, f32[9,512]{1,0:T(8,128)S(1)}, u32[]{:S(2)}) copy-start(f32[9,512]{1,0:T(8,128)S(1)} %collective-permute-done.w_ref) | copy-start | bytes 55300
  26.0 0.6 %copy-start.2 = (f32[9,512]{1,0:T(8,128)}, f32[9,512]{1,0:T(8,128)S(1)}, u32[]{:S(2)}) copy-start(f32[9,512]{1,0:T(8,128)S(1)} %collective-permute-done.1.e_ref) | copy-start | bytes 55300
  26.1 0.6 %copy-start.3 = (f32[9,512]{1,0:T(8,128)}, f32[9,512]{1,0:T(8,128)S(1)}, u32[]{:S(2)}) copy-start(f32[9,512]{1,0:T(8,128)S(1)} %collective-permute-done.2.s_ref) | copy-start | bytes 55300
  26.1 0.6 %copy-start.4 = (f32[9,512]{1,0:T(8,128)}, f32[9,512]{1,0:T(8,128)S(1)}, u32[]{:S(2)}) copy-start(f32[9,512]{1,0:T(8,128)S(1)} %collective-permute-done.3.n_ref) | copy-start | bytes 55300
  31.4 9.6 %collective-permute-start.4 = (f32[8,128]{1,0:T(8,128)}, f32[8,128]{1,0:T(8,128)S(1)}, u32[]{:S(2)}, u32[]{:S(2)}) collective-permute-start(f32[8,128]{1,0:T(8,128)} %get-tuple-element.27.own_ref), channel_id=1, source_target_pairs={{0,1},{1,0},{2,3},{3,2},{4,5},{5,4},{6,7},{7,6},{8,9},{9,8},{10,11... | collective-permute-start | bytes 12296 | tf_op jit(solution)/shard_map/ppermute | solution.py:395
  41.0 0.6 %copy-start = (f32[8,128]{1,0:T(8,128)}, f32[8,128]{1,0:T(8,128)S(1)}, u32[]{:S(2)}) copy-start(f32[8,128]{1,0:T(8,128)S(1)} %collective-permute-done.4.recv_ref) | copy-start | bytes 12292

commit v7 on v6

--- a/solution.py
+++ b/solution.py
@@ -271,6 +271,8 @@
     upper = jnp.where(off > 0, 1.0, 0.0).astype(jnp.float32)
     lower = 1.0 - upper
     zero = jnp.zeros((per, lanes), jnp.float32)
+    one = jnp.ones((1, lanes), jnp.float32)
+    flat = jnp.zeros((1, lanes), jnp.float32)
 
     def forward(k, carry):
         uv, up, x0, x1, x2, x3 = carry
@@ -294,14 +296,14 @@
         y1 = f0 * x1 + f1 * x3
         y2 = f2 * x0 + f3 * x2
         y3 = f2 * x1 + f3 * x3
-        xs_ref[0, k] = y0
-        xs_ref[1, k] = y1
-        xs_ref[2, k] = y2
-        xs_ref[3, k] = y3
+        xs_ref[0, pl.ds(k, 1), :] = y0
+        xs_ref[1, pl.ds(k, 1), :] = y1
+        xs_ref[2, pl.ds(k, 1), :] = y2
+        xs_ref[3, pl.ds(k, 1), :] = y3
         return (nuv, nup, y0, y1, y2, y3)
 
     uv, up, _, _, _, _ = lax.fori_loop(
-        0, levels, forward, (zero, zero, upper, 0.0 * upper, 0.0 * upper, upper), unroll=4
+        0, levels, forward, (zero, zero, upper * one, flat, flat, upper * one), unroll=True
     )
 
     def backward(step, carry):
@@ -317,23 +319,23 @@
         nsp = sp_ref[at, :] + (m2 * sv + m3 * sp)
         sv_ref[at, :] = nsv
         sp_ref[at, :] = nsp
-        d0 = xs_ref[0, k] + (m0 * c0 + m1 * c2)
-        d1 = xs_ref[1, k] + (m0 * c1 + m1 * c3)
-        d2 = xs_ref[2, k] + (m2 * c0 + m3 * c2)
-        d3 = xs_ref[3, k] + (m2 * c1 + m3 * c3)
-        coef_ref[0, at, :] = jnp.full((per, lanes), d0, jnp.float32)
-        coef_ref[1, at, :] = jnp.full((per, lanes), d1, jnp.float32)
-        coef_ref[2, at, :] = jnp.full((per, lanes), d2, jnp.float32)
-        coef_ref[3, at, :] = jnp.full((per, lanes), d3, jnp.float32)
+        d0 = xs_ref[0, pl.ds(k, 1), :] + (m0 * c0 + m1 * c2)
+        d1 = xs_ref[1, pl.ds(k, 1), :] + (m0 * c1 + m1 * c3)
+        d2 = xs_ref[2, pl.ds(k, 1), :] + (m2 * c0 + m3 * c2)
+        d3 = xs_ref[3, pl.ds(k, 1), :] + (m2 * c1 + m3 * c3)
+        coef_ref[0, at, :] = jnp.broadcast_to(d0, (per, lanes))
+        coef_ref[1, at, :] = jnp.broadcast_to(d1, (per, lanes))
+        coef_ref[2, at, :] = jnp.broadcast_to(d2, (per, lanes))
+        coef_ref[3, at, :] = jnp.broadcast_to(d3, (per, lanes))
         return (nsv, nsp, d0, d1, d2, d3)
 
     sv, sp, d0, d1, d2, d3 = lax.fori_loop(
-        0, levels, backward, (zero, zero, lower, 0.0 * lower, 0.0 * lower, lower), unroll=4
+        0, levels, backward, (zero, zero, lower * one, flat, flat, lower * one), unroll=True
     )
     msg_ref[0:per, :] = lower * uv + upper * sv
     msg_ref[per : 2 * per, :] = lower * up + upper * sp
     for index, value in enumerate((d0, d1, d2, d3)):
-        msg_ref[2 * per + index : 2 * per + index + 1, :] = jnp.full((1, lanes), upper * value, jnp.float32)
+        msg_ref[2 * per + index : 2 * per + index + 1, :] = upper * value
 
 
 def arrive_solve_kernel(
@@ -384,7 +386,7 @@
         out_specs=(vmem,) * 5,
         scratch_shapes=[
             pltpu.VMEM((rows, lanes), jnp.float32),
-            pltpu.SMEM((4, levels), jnp.float32),
+            pltpu.VMEM((4, levels, lanes), jnp.float32),
         ],
         cost_estimate=pl.CostEstimate(
             flops=8 * sat_view.size * len(faces_in) * slot_count + 40 * rows * lanes,

time: 43.6 us -> 42.6 us (0.977)
  Pallas kernels: 14.1 us -> 13.1 us
    pallas_call x1, Pallas kernels: 4.72 us -> 3.73 us  [settle_and_solve(): pl.pallas_call(arrive_solve_kernel, out_shape=(jax.ShapeDtypeStruct((len(...]
where the time goes in v7:
time: 42.6 us; the launch traced here: 42.3 us
  starting transfers between devices  20.1 us (47%)
  Pallas kernels  13.1 us (31%)
  waiting for transfers between devices  7.24 us (17%)
  local copies, waits for them, and re-layouts  1.18 us (3%)
  between operations  0.73 us (2%)
    ppermute x4, starting transfers between devices, shifted(): return lax.ppermute(value, axis, pairs)  17.7 us
    ppermute x1, waiting for transfers between devices, settle_and_solve(): received = lax.ppermute(message, 'gz', [(0, 1), (1, 0)])  7.23 us
    pallas_call x1, Pallas kernels, settle_residents(): pl.pallas_call(resident_kernel, grid=(drop_count // chunk,), out_shape=(j...  4.28 us
    pallas_call x1, Pallas kernels, settle_and_solve(): pl.pallas_call(arrive_solve_kernel, out_shape=(jax.ShapeDtypeStruct((len(...  3.73 us
    pallas_call x1, Pallas kernels, emit_faces(): pl.pallas_call(emit_kernel, out_shape=tuple((jax.ShapeDtypeStruct((record...  3.37 us
    ppermute x1, starting transfers between devices, settle_and_solve(): received = lax.ppermute(message, 'gz', [(0, 1), (1, 0)])  2.37 us
    pallas_call x1, Pallas kernels, settle_and_solve(): pl.pallas_call(correct_kernel, out_shape=(jax.ShapeDtypeStruct((rows, lan...  1.68 us
    unnamed x10, local copies, waits for them, and re-layouts  1.18 us
  transfers between devices with their start and end apart: 5, of which 1 were waited for; matrix products, arithmetic and copies ran while one was open for 0% of the time, Pallas kernels for 10%

profile of v7, /device:TPU:32, one launch (start us, length us, event | category | flops | bytes accessed | tf_op | source)
XLA Modules:
  0.0 42.3 jit_solution(10691318560165580917)
XLA Ops:
  0.6 3.4 %shard_map.129 = (f32[9,512]{1,0:T(8,128)}, f32[9,512]{1,0:T(8,128)}, f32[9,512]{1,0:T(8,128)}, f32[9,512]{1,0:T(8,128)}, f32[64,128]{1,0:T(8,128)}) custom-call(s32[4]{0:T(128)} %bitcast.24, f32[512,128]{1,0:T(8,128)} %bitcast.19, s32[64,128]{1,0:T(8,128)} %bitcast.21, s32[4,512]{1,0:T(4,128)} %bitcast.23), custom_call_target="tpu_custom_call" | custom-call | flops 14155776 | bytes 442368 | tf_op jit(solution)/shard_map/pallas_call | solution.py:130
  4.0 3.4 %collective-permute-start = (f32[9,512]{1,0:T(8,128)}, f32[9,512]{1,0:T(8,128)S(1)}, u32[]{:S(2)}, u32[]{:S(2)}) collective-permute-start(f32[9,512]{1,0:T(8,128)} %get-tuple-element.20), channel_id=1, source_target_pairs={{0,32},{32,64},{64,96},{96,128},{128,160},{160,192},{192,224},{224... | collective-permute-start | bytes 55304 | tf_op jit(solution)/shard_map/ppermute | solution.py:24
  7.4 6.3 %collective-permute-start.1 = (f32[9,512]{1,0:T(8,128)}, f32[9,512]{1,0:T(8,128)S(1)}, u32[]{:S(2)}, u32[]{:S(2)}) collective-permute-start(f32[9,512]{1,0:T(8,128)} %get-tuple-element.21), channel_id=1, source_target_pairs={{0,480},{32,0},{64,32},{96,64},{128,96},{160,128},{192,160},{224,1... | collective-permute-start | bytes 55304 | tf_op jit(solution)/shard_map/ppermute | solution.py:24
  13.8 0.0 collective-permute-start.2
  13.8 7.9 %collective-permute-start.3 = (f32[9,512]{1,0:T(8,128)}, f32[9,512]{1,0:T(8,128)S(1)}, u32[]{:S(2)}, u32[]{:S(2)}) collective-permute-start(f32[9,512]{1,0:T(8,128)} %get-tuple-element.23), channel_id=1, source_target_pairs={{0,30},{2,0},{4,2},{6,4},{8,6},{10,8},{12,10},{14,12},{16,14},{18,... | collective-permute-start | bytes 55304 | tf_op jit(solution)/shard_map/ppermute | solution.py:24
  21.7 4.3 %shard_map.130 = (f32[8,8192]{1,0:T(8,128)}, f32[128,128]{1,0:T(8,128)}) custom-call(f32[8,8192]{1,0:T(8,128)} %bitcast.20, s32[1,8192]{1,0:T(1,128)} %bitcast.22, f32[1,8192]{1,0:T(1,128)} %bitcast.31, f32[128,128]{1,0:T(8,128)} %bitcast.25), custom_call_target="tpu_custom_call" | custom-call | flops 1610612736 | bytes 589824 | tf_op jit(solution)/shard_map/pallas_call | solution.py:226
  26.0 0.0 collective-permute-done.w_ref
  26.0 0.0 copy-start.1
  26.0 0.0 collective-permute-done.1.e_ref
  26.0 0.0 copy-start.2
  26.0 0.0 collective-permute-done.2.s_ref
  26.1 0.0 copy-start.3
  26.1 0.0 collective-permute-done.3.n_ref
  26.1 0.0 copy-start.4
  26.1 0.5 %copy-done.1 = f32[9,512]{1,0:T(8,128)} copy-done((f32[9,512]{1,0:T(8,128)}, f32[9,512]{1,0:T(8,128)S(1)}, u32[]{:S(2)}) %copy-start.1) | copy-done | bytes 18456
  26.6 0.0 copy-done.2
  26.6 0.0 copy-done.3
  26.7 0.0 copy-done.4
  26.7 3.7 %shard_map.131 = (f32[4,8,512]{2,1,0:T(8,128)}, f32[128,128]{1,0:T(8,128)}, f32[128,128]{1,0:T(8,128)}, f32[8,128]{1,0:T(8,128)}, f32[4,128,128]{2,1,0:T(8,128)}) custom-call(s32[1]{0:T(128)} %bitcast.11.off_ref, f32[4,128]{1,0:T(4,128)} %bi_ref.1, f32[4,128]{1,0:T(4,128)} %fm_ref.1, f32[4,128]{1,0:T(4,128)} %bm_ref.1, f32[9,512]{1,0:T(8,128)} %copy-done.1, ...), custom_call_target="tpu_custom_call" | custom-call | flops 269090816 | bytes 802816 | tf_op jit(solution)/shard_map/pallas_call | solution.py:376
  30.4 2.4 %collective-permute-start.4 = (f32[8,128]{1,0:T(8,128)}, f32[8,128]{1,0:T(8,128)S(1)}, u32[]{:S(2)}, u32[]{:S(2)}) collective-permute-start(f32[8,128]{1,0:T(8,128)} %get-tuple-element.27.own_ref), channel_id=1, source_target_pairs={{0,1},{1,0},{2,3},{3,2},{4,5},{5,4},{6,7},{7,6},{8,9},{9,8},{10,11... | collective-permute-start | bytes 12296 | tf_op jit(solution)/shard_map/ppermute | solution.py:397
  32.8 7.2 %collective-permute-done.4.recv_ref = f32[8,128]{1,0:T(8,128)S(1)} collective-permute-done((f32[8,128]{1,0:T(8,128)}, f32[8,128]{1,0:T(8,128)S(1)}, u32[]{:S(2)}, u32[]{:S(2)}) %collective-permute-start.4) | collective-permute-done | bytes 4128 | tf_op jit(solution)/shard_map/ppermute | solution.py:397
  40.0 0.0 copy-start
  40.0 0.6 %copy-done = f32[8,128]{1,0:T(8,128)} copy-done((f32[8,128]{1,0:T(8,128)}, f32[8,128]{1,0:T(8,128)S(1)}, u32[]{:S(2)}) %copy-start) | copy-done | bytes 4120
  40.6 1.7 %shard_map.132 = (f32[128,128]{1,0:T(8,128)}, f32[128,128]{1,0:T(8,128)}) custom-call(f32[4,128,128]{2,1,0:T(8,128)} %get-tuple-element.26.coef_ref, f32[8,128]{1,0:T(8,128)} %get-tuple-element.27.own_ref, f32[8,128]{1,0:T(8,128)} %copy-done, f32[128,128]{1,0:T(8,128)} %get-tuple-element.28.sv_ref, f32[128,128]{1,0:T(8,128)} %get-tuple-element.29.sp_ref), custom_call_target="tpu_custom_call" | custom-call | flops 131072 | bytes 524288 | tf_op jit(solution)/shard_map/pallas_call | solution.py:398
Async XLA Ops:
  4.0 22.0 %collective-permute-start = (f32[9,512]{1,0:T(8,128)}, f32[9,512]{1,0:T(8,128)S(1)}, u32[]{:S(2)}, u32[]{:S(2)}) collective-permute-start(f32[9,512]{1,0:T(8,128)} %get-tuple-element.20), channel_id=1, source_target_pairs={{0,32},{32,64},{64,96},{96,128},{128,160},{160,192},{192,224},{224... | collective-permute-start | bytes 55304 | tf_op jit(solution)/shard_map/ppermute | solution.py:24
  7.4 18.6 %collective-permute-start.1 = (f32[9,512]{1,0:T(8,128)}, f32[9,512]{1,0:T(8,128)S(1)}, u32[]{:S(2)}, u32[]{:S(2)}) collective-permute-start(f32[9,512]{1,0:T(8,128)} %get-tuple-element.21), channel_id=1, source_target_pairs={{0,480},{32,0},{64,32},{96,64},{128,96},{160,128},{192,160},{224,1... | collective-permute-start | bytes 55304 | tf_op jit(solution)/shard_map/ppermute | solution.py:24
  13.8 12.3 %collective-permute-start.2 = (f32[9,512]{1,0:T(8,128)}, f32[9,512]{1,0:T(8,128)S(1)}, u32[]{:S(2)}, u32[]{:S(2)}) collective-permute-start(f32[9,512]{1,0:T(8,128)} %get-tuple-element.22), channel_id=1, source_target_pairs={{0,2},{2,4},{4,6},{6,8},{8,10},{10,12},{12,14},{14,16},{16,18},{18... | collective-permute-start | bytes 55304 | tf_op jit(solution)/shard_map/ppermute | solution.py:24
  13.8 12.3 %collective-permute-start.3 = (f32[9,512]{1,0:T(8,128)}, f32[9,512]{1,0:T(8,128)S(1)}, u32[]{:S(2)}, u32[]{:S(2)}) collective-permute-start(f32[9,512]{1,0:T(8,128)} %get-tuple-element.23), channel_id=1, source_target_pairs={{0,30},{2,0},{4,2},{6,4},{8,6},{10,8},{12,10},{14,12},{16,14},{18,... | collective-permute-start | bytes 55304 | tf_op jit(solution)/shard_map/ppermute | solution.py:24
  26.0 0.6 %copy-start.1 = (f32[9,512]{1,0:T(8,128)}, f32[9,512]{1,0:T(8,128)S(1)}, u32[]{:S(2)}) copy-start(f32[9,512]{1,0:T(8,128)S(1)} %collective-permute-done.w_ref) | copy-start | bytes 55300
  26.0 0.6 %copy-start.2 = (f32[9,512]{1,0:T(8,128)}, f32[9,512]{1,0:T(8,128)S(1)}, u32[]{:S(2)}) copy-start(f32[9,512]{1,0:T(8,128)S(1)} %collective-permute-done.1.e_ref) | copy-start | bytes 55300
  26.1 0.6 %copy-start.3 = (f32[9,512]{1,0:T(8,128)}, f32[9,512]{1,0:T(8,128)S(1)}, u32[]{:S(2)}) copy-start(f32[9,512]{1,0:T(8,128)S(1)} %collective-permute-done.2.s_ref) | copy-start | bytes 55300
  26.1 0.6 %copy-start.4 = (f32[9,512]{1,0:T(8,128)}, f32[9,512]{1,0:T(8,128)S(1)}, u32[]{:S(2)}) copy-start(f32[9,512]{1,0:T(8,128)S(1)} %collective-permute-done.3.n_ref) | copy-start | bytes 55300
  30.4 9.6 %collective-permute-start.4 = (f32[8,128]{1,0:T(8,128)}, f32[8,128]{1,0:T(8,128)S(1)}, u32[]{:S(2)}, u32[]{:S(2)}) collective-permute-start(f32[8,128]{1,0:T(8,128)} %get-tuple-element.27.own_ref), channel_id=1, source_target_pairs={{0,1},{1,0},{2,3},{3,2},{4,5},{5,4},{6,7},{7,6},{8,9},{9,8},{10,11... | collective-permute-start | bytes 12296 | tf_op jit(solution)/shard_map/ppermute | solution.py:397
  40.0 0.6 %copy-start = (f32[8,128]{1,0:T(8,128)}, f32[8,128]{1,0:T(8,128)S(1)}, u32[]{:S(2)}) copy-start(f32[8,128]{1,0:T(8,128)S(1)} %collective-permute-done.4.recv_ref) | copy-start | bytes 12292

commit v8 on v7

--- a/solution.py
+++ b/solution.py
@@ -220,7 +220,7 @@
 def settle_residents(records, cell_row, staying_row, sat_view):
     record_width, drop_count = records.shape
     rows, lanes = sat_view.shape
-    chunk = min(4096, drop_count)
+    chunk = min(8192, drop_count)
     whole = lambda j: (0, 0)
     by_chunk = lambda j: (0, j)
     return pl.pallas_call(

time: 42.6 us -> 42.3 us (level)
  no operation moved by 1% of the time
where the time goes in v8:
time: 42.3 us; the launch traced here: 42 us
  starting transfers between devices  20 us (47%)
  Pallas kernels  12.8 us (30%)
  waiting for transfers between devices  7.25 us (17%)
  local copies, waits for them, and re-layouts  1.18 us (3%)
  between operations  0.71 us (2%)
    ppermute x4, starting transfers between devices, shifted(): return lax.ppermute(value, axis, pairs)  17.7 us
    ppermute x1, waiting for transfers between devices, settle_and_solve(): received = lax.ppermute(message, 'gz', [(0, 1), (1, 0)])  7.24 us
    pallas_call x1, Pallas kernels, settle_residents(): pl.pallas_call(resident_kernel, grid=(drop_count // chunk,), out_shape=(j...  4.03 us
    pallas_call x1, Pallas kernels, settle_and_solve(): pl.pallas_call(arrive_solve_kernel, out_shape=(jax.ShapeDtypeStruct((len(...  3.73 us
    pallas_call x1, Pallas kernels, emit_faces(): pl.pallas_call(emit_kernel, out_shape=tuple((jax.ShapeDtypeStruct((record...  3.37 us
    ppermute x1, starting transfers between devices, settle_and_solve(): received = lax.ppermute(message, 'gz', [(0, 1), (1, 0)])  2.36 us
    pallas_call x1, Pallas kernels, settle_and_solve(): pl.pallas_call(correct_kernel, out_shape=(jax.ShapeDtypeStruct((rows, lan...  1.68 us
    unnamed x10, local copies, waits for them, and re-layouts  1.18 us
  transfers between devices with their start and end apart: 5, of which 1 were waited for; matrix products, arithmetic and copies ran while one was open for 0% of the time, Pallas kernels for 10%

profile of v8, /device:TPU:32, one launch (start us, length us, event | category | flops | bytes accessed | tf_op | source)
XLA Modules:
  0.0 42.0 jit_solution(12879468295162832844)
XLA Ops:
  0.6 3.4 %shard_map.129 = (f32[9,512]{1,0:T(8,128)}, f32[9,512]{1,0:T(8,128)}, f32[9,512]{1,0:T(8,128)}, f32[9,512]{1,0:T(8,128)}, f32[64,128]{1,0:T(8,128)}) custom-call(s32[4]{0:T(128)} %bitcast.24, f32[512,128]{1,0:T(8,128)} %bitcast.19, s32[64,128]{1,0:T(8,128)} %bitcast.21, s32[4,512]{1,0:T(4,128)} %bitcast.23), custom_call_target="tpu_custom_call" | custom-call | flops 14155776 | bytes 442368 | tf_op jit(solution)/shard_map/pallas_call | solution.py:130
  4.0 3.4 %collective-permute-start = (f32[9,512]{1,0:T(8,128)}, f32[9,512]{1,0:T(8,128)S(1)}, u32[]{:S(2)}, u32[]{:S(2)}) collective-permute-start(f32[9,512]{1,0:T(8,128)} %get-tuple-element.20), channel_id=1, source_target_pairs={{0,32},{32,64},{64,96},{96,128},{128,160},{160,192},{192,224},{224... | collective-permute-start | bytes 55304 | tf_op jit(solution)/shard_map/ppermute | solution.py:24
  7.4 6.3 %collective-permute-start.1 = (f32[9,512]{1,0:T(8,128)}, f32[9,512]{1,0:T(8,128)S(1)}, u32[]{:S(2)}, u32[]{:S(2)}) collective-permute-start(f32[9,512]{1,0:T(8,128)} %get-tuple-element.21), channel_id=1, source_target_pairs={{0,480},{32,0},{64,32},{96,64},{128,96},{160,128},{192,160},{224,1... | collective-permute-start | bytes 55304 | tf_op jit(solution)/shard_map/ppermute | solution.py:24
  13.8 0.0 collective-permute-start.2
  13.8 7.9 %collective-permute-start.3 = (f32[9,512]{1,0:T(8,128)}, f32[9,512]{1,0:T(8,128)S(1)}, u32[]{:S(2)}, u32[]{:S(2)}) collective-permute-start(f32[9,512]{1,0:T(8,128)} %get-tuple-element.23), channel_id=1, source_target_pairs={{0,30},{2,0},{4,2},{6,4},{8,6},{10,8},{12,10},{14,12},{16,14},{18,... | collective-permute-start | bytes 55304 | tf_op jit(solution)/shard_map/ppermute | solution.py:24
  21.7 4.0 %shard_map.130 = (f32[8,8192]{1,0:T(8,128)}, f32[128,128]{1,0:T(8,128)}) custom-call(f32[8,8192]{1,0:T(8,128)} %bitcast.20, s32[1,8192]{1,0:T(1,128)} %bitcast.22, f32[1,8192]{1,0:T(1,128)} %bitcast.31, f32[128,128]{1,0:T(8,128)} %bitcast.25), custom_call_target="tpu_custom_call" | custom-call | flops 1610612736 | bytes 589824 | tf_op jit(solution)/shard_map/pallas_call | solution.py:226
  25.7 0.0 collective-permute-done.w_ref
  25.8 0.0 copy-start.1
  25.8 0.0 collective-permute-done.1.e_ref
  25.8 0.0 copy-start.2
  25.8 0.0 collective-permute-done.2.s_ref
  25.8 0.0 copy-start.3
  25.8 0.0 collective-permute-done.3.n_ref
  25.8 0.0 copy-start.4
  25.8 0.6 %copy-done.1 = f32[9,512]{1,0:T(8,128)} copy-done((f32[9,512]{1,0:T(8,128)}, f32[9,512]{1,0:T(8,128)S(1)}, u32[]{:S(2)}) %copy-start.1) | copy-done | bytes 18456
  26.4 0.0 copy-done.2
  26.4 0.0 copy-done.3
  26.4 0.0 copy-done.4
  26.4 3.7 %shard_map.131 = (f32[4,8,512]{2,1,0:T(8,128)}, f32[128,128]{1,0:T(8,128)}, f32[128,128]{1,0:T(8,128)}, f32[8,128]{1,0:T(8,128)}, f32[4,128,128]{2,1,0:T(8,128)}) custom-call(s32[1]{0:T(128)} %bitcast.11.off_ref, f32[4,128]{1,0:T(4,128)} %bi_ref.1, f32[4,128]{1,0:T(4,128)} %fm_ref.1, f32[4,128]{1,0:T(4,128)} %bm_ref.1, f32[9,512]{1,0:T(8,128)} %copy-done.1, ...), custom_call_target="tpu_custom_call" | custom-call | flops 269090816 | bytes 802816 | tf_op jit(solution)/shard_map/pallas_call | solution.py:376
  30.1 2.4 %collective-permute-start.4 = (f32[8,128]{1,0:T(8,128)}, f32[8,128]{1,0:T(8,128)S(1)}, u32[]{:S(2)}, u32[]{:S(2)}) collective-permute-start(f32[8,128]{1,0:T(8,128)} %get-tuple-element.27.own_ref), channel_id=1, source_target_pairs={{0,1},{1,0},{2,3},{3,2},{4,5},{5,4},{6,7},{7,6},{8,9},{9,8},{10,11... | collective-permute-start | bytes 12296 | tf_op jit(solution)/shard_map/ppermute | solution.py:397
  32.5 7.2 %collective-permute-done.4.recv_ref = f32[8,128]{1,0:T(8,128)S(1)} collective-permute-done((f32[8,128]{1,0:T(8,128)}, f32[8,128]{1,0:T(8,128)S(1)}, u32[]{:S(2)}, u32[]{:S(2)}) %collective-permute-start.4) | collective-permute-done | bytes 4128 | tf_op jit(solution)/shard_map/ppermute | solution.py:397
  39.7 0.0 copy-start
  39.7 0.6 %copy-done = f32[8,128]{1,0:T(8,128)} copy-done((f32[8,128]{1,0:T(8,128)}, f32[8,128]{1,0:T(8,128)S(1)}, u32[]{:S(2)}) %copy-start) | copy-done | bytes 4120
  40.3 1.7 %shard_map.132 = (f32[128,128]{1,0:T(8,128)}, f32[128,128]{1,0:T(8,128)}) custom-call(f32[4,128,128]{2,1,0:T(8,128)} %get-tuple-element.26.coef_ref, f32[8,128]{1,0:T(8,128)} %get-tuple-element.27.own_ref, f32[8,128]{1,0:T(8,128)} %copy-done, f32[128,128]{1,0:T(8,128)} %get-tuple-element.28.sv_ref, f32[128,128]{1,0:T(8,128)} %get-tuple-element.29.sp_ref), custom_call_target="tpu_custom_call" | custom-call | flops 131072 | bytes 524288 | tf_op jit(solution)/shard_map/pallas_call | solution.py:398
Async XLA Ops:
  4.0 21.7 %collective-permute-start = (f32[9,512]{1,0:T(8,128)}, f32[9,512]{1,0:T(8,128)S(1)}, u32[]{:S(2)}, u32[]{:S(2)}) collective-permute-start(f32[9,512]{1,0:T(8,128)} %get-tuple-element.20), channel_id=1, source_target_pairs={{0,32},{32,64},{64,96},{96,128},{128,160},{160,192},{192,224},{224... | collective-permute-start | bytes 55304 | tf_op jit(solution)/shard_map/ppermute | solution.py:24
  7.4 18.3 %collective-permute-start.1 = (f32[9,512]{1,0:T(8,128)}, f32[9,512]{1,0:T(8,128)S(1)}, u32[]{:S(2)}, u32[]{:S(2)}) collective-permute-start(f32[9,512]{1,0:T(8,128)} %get-tuple-element.21), channel_id=1, source_target_pairs={{0,480},{32,0},{64,32},{96,64},{128,96},{160,128},{192,160},{224,1... | collective-permute-start | bytes 55304 | tf_op jit(solution)/shard_map/ppermute | solution.py:24
  13.8 12.0 %collective-permute-start.2 = (f32[9,512]{1,0:T(8,128)}, f32[9,512]{1,0:T(8,128)S(1)}, u32[]{:S(2)}, u32[]{:S(2)}) collective-permute-start(f32[9,512]{1,0:T(8,128)} %get-tuple-element.22), channel_id=1, source_target_pairs={{0,2},{2,4},{4,6},{6,8},{8,10},{10,12},{12,14},{14,16},{16,18},{18... | collective-permute-start | bytes 55304 | tf_op jit(solution)/shard_map/ppermute | solution.py:24
  13.8 12.0 %collective-permute-start.3 = (f32[9,512]{1,0:T(8,128)}, f32[9,512]{1,0:T(8,128)S(1)}, u32[]{:S(2)}, u32[]{:S(2)}) collective-permute-start(f32[9,512]{1,0:T(8,128)} %get-tuple-element.23), channel_id=1, source_target_pairs={{0,30},{2,0},{4,2},{6,4},{8,6},{10,8},{12,10},{14,12},{16,14},{18,... | collective-permute-start | bytes 55304 | tf_op jit(solution)/shard_map/ppermute | solution.py:24
  25.8 0.6 %copy-start.1 = (f32[9,512]{1,0:T(8,128)}, f32[9,512]{1,0:T(8,128)S(1)}, u32[]{:S(2)}) copy-start(f32[9,512]{1,0:T(8,128)S(1)} %collective-permute-done.w_ref) | copy-start | bytes 55300
  25.8 0.6 %copy-start.2 = (f32[9,512]{1,0:T(8,128)}, f32[9,512]{1,0:T(8,128)S(1)}, u32[]{:S(2)}) copy-start(f32[9,512]{1,0:T(8,128)S(1)} %collective-permute-done.1.e_ref) | copy-start | bytes 55300
  25.8 0.6 %copy-start.3 = (f32[9,512]{1,0:T(8,128)}, f32[9,512]{1,0:T(8,128)S(1)}, u32[]{:S(2)}) copy-start(f32[9,512]{1,0:T(8,128)S(1)} %collective-permute-done.2.s_ref) | copy-start | bytes 55300
  25.8 0.6 %copy-start.4 = (f32[9,512]{1,0:T(8,128)}, f32[9,512]{1,0:T(8,128)S(1)}, u32[]{:S(2)}) copy-start(f32[9,512]{1,0:T(8,128)S(1)} %collective-permute-done.3.n_ref) | copy-start | bytes 55300
  30.1 9.6 %collective-permute-start.4 = (f32[8,128]{1,0:T(8,128)}, f32[8,128]{1,0:T(8,128)S(1)}, u32[]{:S(2)}, u32[]{:S(2)}) collective-permute-start(f32[8,128]{1,0:T(8,128)} %get-tuple-element.27.own_ref), channel_id=1, source_target_pairs={{0,1},{1,0},{2,3},{3,2},{4,5},{5,4},{6,7},{7,6},{8,9},{9,8},{10,11... | collective-permute-start | bytes 12296 | tf_op jit(solution)/shard_map/ppermute | solution.py:397
  39.7 0.6 %copy-start = (f32[8,128]{1,0:T(8,128)}, f32[8,128]{1,0:T(8,128)S(1)}, u32[]{:S(2)}) copy-start(f32[8,128]{1,0:T(8,128)S(1)} %collective-permute-done.4.recv_ref) | copy-start | bytes 12292

commit v9 on v8

--- a/solution.py
+++ b/solution.py
@@ -85,37 +85,43 @@
     shift = lanes.bit_length() - 1
     rec_stack = jnp.concatenate(split_pieces3(view_ref[...]), axis=1)
     cell_stack = jnp.concatenate(split_pieces3(cells_ref[...].astype(jnp.float32)), axis=1)
-    counted = jnp.zeros((outer, lanes), jnp.float32)
+    faces = len(face_refs)
+    width = faces * slot_count
+    index = jnp.concatenate([cross_ref[face : face + 1, :] for face in range(faces)], axis=1)
+    face_of = lax.broadcasted_iota(jnp.int32, (1, width), 1) // slot_count
+    slot_of = lax.broadcasted_iota(jnp.int32, (1, width), 1) % slot_count
+    limit = jnp.zeros((1, width), jnp.int32)
+    for face in range(faces):
+        limit = jnp.where(face_of == face, count_ref[face], limit)
+    in_use = slot_of < limit
+    high = lax.shift_right_logical(index, shift)
+    low = jnp.bitwise_and(index, lanes - 1)
+    lane_hot = jnp.where(
+        lax.broadcasted_iota(jnp.int32, (lanes, width), 0).astype(jnp.bfloat16)
+        == low.astype(jnp.bfloat16),
+        jnp.bfloat16(1.0),
+        jnp.bfloat16(0.0),
+    )
+    high_mask = lax.broadcasted_iota(jnp.int32, (outer, width), 0) == high
+    lane_hot3 = jnp.concatenate([lane_hot, lane_hot, lane_hot], axis=0)
+    got = jnp.dot(rec_stack, lane_hot3, preferred_element_type=jnp.float32)
+    got = got.reshape(outer, record_width, width)
+    picked = jnp.sum(jnp.where(high_mask[:, None, :], got, 0.0), axis=0)
+    got_cell = jnp.dot(cell_stack, lane_hot3, preferred_element_type=jnp.float32)
+    source = (jnp.sum(jnp.where(high_mask, got_cell, 0.0), axis=0, keepdims=True) + 0.5).astype(jnp.int32)
+    height = lax.shift_right_logical(source, (CX * CY).bit_length() - 1)
+    cell_x = jnp.bitwise_and(lax.shift_right_logical(source, CY.bit_length() - 1), CX - 1)
+    cell_y = jnp.bitwise_and(source, CY - 1)
+    new_x = jnp.where(face_of == 0, 0, jnp.where(face_of == 1, CX - 1, cell_x))
+    new_y = jnp.where(face_of == 2, 0, jnp.where(face_of == 3, CY - 1, cell_y))
+    target = (height * (CX * CY) + new_x * CY + new_y).astype(jnp.float32)
+    packet = jnp.where(in_use, jnp.concatenate([picked, target], axis=0), 0.0)
     for face, out_ref in enumerate(face_refs):
-        index = cross_ref[face : face + 1, :]
-        high = lax.shift_right_logical(index, shift)
-        low = jnp.bitwise_and(index, lanes - 1)
-        lane_hot = jnp.where(
-            lax.broadcasted_iota(jnp.int32, (lanes, slot_count), 0).astype(jnp.bfloat16)
-            == low.astype(jnp.bfloat16),
-            jnp.bfloat16(1.0),
-            jnp.bfloat16(0.0),
-        )
-        high_mask = lax.broadcasted_iota(jnp.int32, (outer, slot_count), 0) == high
-        lane_hot3 = jnp.concatenate([lane_hot, lane_hot, lane_hot], axis=0)
-        got = jnp.dot(rec_stack, lane_hot3, preferred_element_type=jnp.float32)
-        got = got.reshape(outer, record_width, slot_count)
-        picked = jnp.sum(jnp.where(high_mask[:, None, :], got, 0.0), axis=0)
-        got_cell = jnp.dot(cell_stack, lane_hot3, preferred_element_type=jnp.float32)
-        source = (jnp.sum(jnp.where(high_mask, got_cell, 0.0), axis=0, keepdims=True) + 0.5).astype(jnp.int32)
-        height = lax.shift_right_logical(source, (CX * CY).bit_length() - 1)
-        cell_x = jnp.bitwise_and(lax.shift_right_logical(source, CY.bit_length() - 1), CX - 1)
-        cell_y = jnp.bitwise_and(source, CY - 1)
-        new_x = 0 if face == 0 else (CX - 1 if face == 1 else cell_x)
-        new_y = 0 if face == 2 else (CY - 1 if face == 3 else cell_y)
-        target = (height * (CX * CY) + new_x * CY + new_y).astype(jnp.float32)
-        in_use = lax.broadcasted_iota(jnp.int32, (1, slot_count), 1) < count_ref[face]
-        packet = jnp.concatenate([picked, jnp.broadcast_to(target, (1, slot_count))], axis=0)
-        out_ref[...] = jnp.where(in_use, packet, 0.0)
-        used_high = jnp.where(high_mask & in_use, 1.0, 0.0).astype(jnp.bfloat16)
-        counted = counted + lax.dot_general(
-            used_high, lane_hot, (((1,), (1,)), ((), ())), preferred_element_type=jnp.float32
-        )
+        out_ref[...] = packet[:, face * slot_count : (face + 1) * slot_count]
+    used_high = jnp.where(high_mask & in_use, 1.0, 0.0).astype(jnp.bfloat16)
+    counted = lax.dot_general(
+        used_high, lane_hot, (((1,), (1,)), ((), ())), preferred_element_type=jnp.float32
+    )
     stay_ref[...] = jnp.where(counted == 0.0, 1.0, 0.0)
 
 
@@ -250,17 +256,16 @@
 
 def arrivals_into(faces, sat_ref, res_ref, vel_ref, out_ref, force_ref):
     record_width = out_ref.shape[1]
+    slot_count = out_ref.shape[2]
     sat_stack = stacked_pieces(sat_ref[...])
-    total = res_ref[...]
-    for face, in_ref in enumerate(faces):
-        packet = in_ref[...]
-        records = packet[:record_width]
-        cells = (packet[record_width : record_width + 1] + 0.5).astype(jnp.int32)
-        occupied = records[1:2] > 0.0
-        updated, heat = condense_chunk(records, cells, occupied, sat_stack)
-        out_ref[face] = updated
-        total = total + heat
-    force_ref[...] = vel_ref[...] + BUOYANCY * total
+    packet = jnp.concatenate([in_ref[...] for in_ref in faces], axis=1)
+    records = packet[:record_width]
+    cells = (packet[record_width : record_width + 1] + 0.5).astype(jnp.int32)
+    occupied = records[1:2] > 0.0
+    updated, heat = condense_chunk(records, cells, occupied, sat_stack)
+    for face in range(len(faces)):
+        out_ref[face] = updated[:, face * slot_count : (face + 1) * slot_count]
+    force_ref[...] = vel_ref[...] + BUOYANCY * (res_ref[...] + heat)
 
 
 def solve_into(off_ref, bi_ref, fm_ref, bm_ref, fv_ref, fp_ref, sv_ref, sp_ref, msg_ref, coef_ref, xs_ref):

time: 42.3 us -> 42 us (level)
  no operation moved by 1% of the time
where the time goes in v9:
time: 42 us; the launch traced here: 41.7 us
  starting transfers between devices  20 us (48%)
  Pallas kernels  12.5 us (30%)
  waiting for transfers between devices  7.26 us (17%)
  local copies, waits for them, and re-layouts  1.18 us (3%)
  between operations  0.71 us (2%)
    ppermute x4, starting transfers between devices, shifted(): return lax.ppermute(value, axis, pairs)  17.7 us
    ppermute x1, waiting for transfers between devices, settle_and_solve(): received = lax.ppermute(message, 'gz', [(0, 1), (1, 0)])  7.25 us
    pallas_call x1, Pallas kernels, settle_residents(): pl.pallas_call(resident_kernel, grid=(drop_count // chunk,), out_shape=(j...  4.02 us
    pallas_call x1, Pallas kernels, settle_and_solve(): pl.pallas_call(arrive_solve_kernel, out_shape=(jax.ShapeDtypeStruct((len(...  3.43 us
    pallas_call x1, Pallas kernels, emit_faces(): pl.pallas_call(emit_kernel, out_shape=tuple((jax.ShapeDtypeStruct((record...  3.34 us
    ppermute x1, starting transfers between devices, settle_and_solve(): received = lax.ppermute(message, 'gz', [(0, 1), (1, 0)])  2.34 us
    pallas_call x1, Pallas kernels, settle_and_solve(): pl.pallas_call(correct_kernel, out_shape=(jax.ShapeDtypeStruct((rows, lan...  1.68 us
    unnamed x10, local copies, waits for them, and re-layouts  1.18 us
  transfers between devices with their start and end apart: 5, of which 1 were waited for; matrix products, arithmetic and copies ran while one was open for 0% of the time, Pallas kernels for 10%

profile of v9, /device:TPU:32, one launch (start us, length us, event | category | flops | bytes accessed | tf_op | source)
XLA Modules:
  0.0 41.7 jit_solution(13607066498675097833)
XLA Ops:
  0.6 3.3 %shard_map.129 = (f32[9,512]{1,0:T(8,128)}, f32[9,512]{1,0:T(8,128)}, f32[9,512]{1,0:T(8,128)}, f32[9,512]{1,0:T(8,128)}, f32[64,128]{1,0:T(8,128)}) custom-call(s32[4]{0:T(128)} %bitcast.24, f32[512,128]{1,0:T(8,128)} %bitcast.19, s32[64,128]{1,0:T(8,128)} %bitcast.21, s32[4,512]{1,0:T(4,128)} %bitcast.23), custom_call_target="tpu_custom_call" | custom-call | flops 14155776 | bytes 442368 | tf_op jit(solution)/shard_map/pallas_call | solution.py:136
  4.0 3.4 %collective-permute-start = (f32[9,512]{1,0:T(8,128)}, f32[9,512]{1,0:T(8,128)S(1)}, u32[]{:S(2)}, u32[]{:S(2)}) collective-permute-start(f32[9,512]{1,0:T(8,128)} %get-tuple-element.20), channel_id=1, source_target_pairs={{0,32},{32,64},{64,96},{96,128},{128,160},{160,192},{192,224},{224... | collective-permute-start | bytes 55304 | tf_op jit(solution)/shard_map/ppermute | solution.py:24
  7.4 6.4 %collective-permute-start.1 = (f32[9,512]{1,0:T(8,128)}, f32[9,512]{1,0:T(8,128)S(1)}, u32[]{:S(2)}, u32[]{:S(2)}) collective-permute-start(f32[9,512]{1,0:T(8,128)} %get-tuple-element.21), channel_id=1, source_target_pairs={{0,480},{32,0},{64,32},{96,64},{128,96},{160,128},{192,160},{224,1... | collective-permute-start | bytes 55304 | tf_op jit(solution)/shard_map/ppermute | solution.py:24
  13.7 0.0 collective-permute-start.2
  13.8 7.9 %collective-permute-start.3 = (f32[9,512]{1,0:T(8,128)}, f32[9,512]{1,0:T(8,128)S(1)}, u32[]{:S(2)}, u32[]{:S(2)}) collective-permute-start(f32[9,512]{1,0:T(8,128)} %get-tuple-element.23), channel_id=1, source_target_pairs={{0,30},{2,0},{4,2},{6,4},{8,6},{10,8},{12,10},{14,12},{16,14},{18,... | collective-permute-start | bytes 55304 | tf_op jit(solution)/shard_map/ppermute | solution.py:24
  21.7 4.0 %shard_map.130 = (f32[8,8192]{1,0:T(8,128)}, f32[128,128]{1,0:T(8,128)}) custom-call(f32[8,8192]{1,0:T(8,128)} %bitcast.20, s32[1,8192]{1,0:T(1,128)} %bitcast.22, f32[1,8192]{1,0:T(1,128)} %bitcast.31, f32[128,128]{1,0:T(8,128)} %bitcast.25), custom_call_target="tpu_custom_call" | custom-call | flops 1610612736 | bytes 589824 | tf_op jit(solution)/shard_map/pallas_call | solution.py:232
  25.7 0.0 collective-permute-done.w_ref
  25.7 0.0 copy-start.1
  25.7 0.0 collective-permute-done.1.e_ref
  25.7 0.0 copy-start.2
  25.7 0.0 collective-permute-done.2.s_ref
  25.7 0.0 copy-start.3
  25.8 0.0 collective-permute-done.3.n_ref
  25.8 0.0 copy-start.4
  25.8 0.6 %copy-done.1 = f32[9,512]{1,0:T(8,128)} copy-done((f32[9,512]{1,0:T(8,128)}, f32[9,512]{1,0:T(8,128)S(1)}, u32[]{:S(2)}) %copy-start.1) | copy-done | bytes 18456
  26.3 0.0 copy-done.2
  26.3 0.0 copy-done.3
  26.3 0.0 copy-done.4
  26.4 3.4 %shard_map.131 = (f32[4,8,512]{2,1,0:T(8,128)}, f32[128,128]{1,0:T(8,128)}, f32[128,128]{1,0:T(8,128)}, f32[8,128]{1,0:T(8,128)}, f32[4,128,128]{2,1,0:T(8,128)}) custom-call(s32[1]{0:T(128)} %bitcast.11.off_ref, f32[4,128]{1,0:T(4,128)} %bi_ref.1, f32[4,128]{1,0:T(4,128)} %fm_ref.1, f32[4,128]{1,0:T(4,128)} %bm_ref.1, f32[9,512]{1,0:T(8,128)} %copy-done.1, ...), custom_call_target="tpu_custom_call" | custom-call | flops 269090816 | bytes 802816 | tf_op jit(solution)/shard_map/pallas_call | solution.py:381
  29.8 2.3 %collective-permute-start.4 = (f32[8,128]{1,0:T(8,128)}, f32[8,128]{1,0:T(8,128)S(1)}, u32[]{:S(2)}, u32[]{:S(2)}) collective-permute-start(f32[8,128]{1,0:T(8,128)} %get-tuple-element.27.own_ref), channel_id=1, source_target_pairs={{0,1},{1,0},{2,3},{3,2},{4,5},{5,4},{6,7},{7,6},{8,9},{9,8},{10,11... | collective-permute-start | bytes 12296 | tf_op jit(solution)/shard_map/ppermute | solution.py:402
  32.2 7.3 %collective-permute-done.4.recv_ref = f32[8,128]{1,0:T(8,128)S(1)} collective-permute-done((f32[8,128]{1,0:T(8,128)}, f32[8,128]{1,0:T(8,128)S(1)}, u32[]{:S(2)}, u32[]{:S(2)}) %collective-permute-start.4) | collective-permute-done | bytes 4128 | tf_op jit(solution)/shard_map/ppermute | solution.py:402
  39.4 0.0 copy-start
  39.4 0.6 %copy-done = f32[8,128]{1,0:T(8,128)} copy-done((f32[8,128]{1,0:T(8,128)}, f32[8,128]{1,0:T(8,128)S(1)}, u32[]{:S(2)}) %copy-start) | copy-done | bytes 4120
  40.0 1.7 %shard_map.132 = (f32[128,128]{1,0:T(8,128)}, f32[128,128]{1,0:T(8,128)}) custom-call(f32[4,128,128]{2,1,0:T(8,128)} %get-tuple-element.26.coef_ref, f32[8,128]{1,0:T(8,128)} %get-tuple-element.27.own_ref, f32[8,128]{1,0:T(8,128)} %copy-done, f32[128,128]{1,0:T(8,128)} %get-tuple-element.28.sv_ref, f32[128,128]{1,0:T(8,128)} %get-tuple-element.29.sp_ref), custom_call_target="tpu_custom_call" | custom-call | flops 131072 | bytes 524288 | tf_op jit(solution)/shard_map/pallas_call | solution.py:403
Async XLA Ops:
  4.0 21.7 %collective-permute-start = (f32[9,512]{1,0:T(8,128)}, f32[9,512]{1,0:T(8,128)S(1)}, u32[]{:S(2)}, u32[]{:S(2)}) collective-permute-start(f32[9,512]{1,0:T(8,128)} %get-tuple-element.20), channel_id=1, source_target_pairs={{0,32},{32,64},{64,96},{96,128},{128,160},{160,192},{192,224},{224... | collective-permute-start | bytes 55304 | tf_op jit(solution)/shard_map/ppermute | solution.py:24
  7.4 18.4 %collective-permute-start.1 = (f32[9,512]{1,0:T(8,128)}, f32[9,512]{1,0:T(8,128)S(1)}, u32[]{:S(2)}, u32[]{:S(2)}) collective-permute-start(f32[9,512]{1,0:T(8,128)} %get-tuple-element.21), channel_id=1, source_target_pairs={{0,480},{32,0},{64,32},{96,64},{128,96},{160,128},{192,160},{224,1... | collective-permute-start | bytes 55304 | tf_op jit(solution)/shard_map/ppermute | solution.py:24
  13.7 12.0 %collective-permute-start.2 = (f32[9,512]{1,0:T(8,128)}, f32[9,512]{1,0:T(8,128)S(1)}, u32[]{:S(2)}, u32[]{:S(2)}) collective-permute-start(f32[9,512]{1,0:T(8,128)} %get-tuple-element.22), channel_id=1, source_target_pairs={{0,2},{2,4},{4,6},{6,8},{8,10},{10,12},{12,14},{14,16},{16,18},{18... | collective-permute-start | bytes 55304 | tf_op jit(solution)/shard_map/ppermute | solution.py:24
  13.8 12.0 %collective-permute-start.3 = (f32[9,512]{1,0:T(8,128)}, f32[9,512]{1,0:T(8,128)S(1)}, u32[]{:S(2)}, u32[]{:S(2)}) collective-permute-start(f32[9,512]{1,0:T(8,128)} %get-tuple-element.23), channel_id=1, source_target_pairs={{0,30},{2,0},{4,2},{6,4},{8,6},{10,8},{12,10},{14,12},{16,14},{18,... | collective-permute-start | bytes 55304 | tf_op jit(solution)/shard_map/ppermute | solution.py:24
  25.7 0.6 %copy-start.1 = (f32[9,512]{1,0:T(8,128)}, f32[9,512]{1,0:T(8,128)S(1)}, u32[]{:S(2)}) copy-start(f32[9,512]{1,0:T(8,128)S(1)} %collective-permute-done.w_ref) | copy-start | bytes 55300
  25.7 0.6 %copy-start.2 = (f32[9,512]{1,0:T(8,128)}, f32[9,512]{1,0:T(8,128)S(1)}, u32[]{:S(2)}) copy-start(f32[9,512]{1,0:T(8,128)S(1)} %collective-permute-done.1.e_ref) | copy-start | bytes 55300
  25.7 0.6 %copy-start.3 = (f32[9,512]{1,0:T(8,128)}, f32[9,512]{1,0:T(8,128)S(1)}, u32[]{:S(2)}) copy-start(f32[9,512]{1,0:T(8,128)S(1)} %collective-permute-done.2.s_ref) | copy-start | bytes 55300
  25.8 0.6 %copy-start.4 = (f32[9,512]{1,0:T(8,128)}, f32[9,512]{1,0:T(8,128)S(1)}, u32[]{:S(2)}) copy-start(f32[9,512]{1,0:T(8,128)S(1)} %collective-permute-done.3.n_ref) | copy-start | bytes 55300
  29.8 9.6 %collective-permute-start.4 = (f32[8,128]{1,0:T(8,128)}, f32[8,128]{1,0:T(8,128)S(1)}, u32[]{:S(2)}, u32[]{:S(2)}) collective-permute-start(f32[8,128]{1,0:T(8,128)} %get-tuple-element.27.own_ref), channel_id=1, source_target_pairs={{0,1},{1,0},{2,3},{3,2},{4,5},{5,4},{6,7},{7,6},{8,9},{9,8},{10,11... | collective-permute-start | bytes 12296 | tf_op jit(solution)/shard_map/ppermute | solution.py:402
  39.4 0.6 %copy-start = (f32[8,128]{1,0:T(8,128)}, f32[8,128]{1,0:T(8,128)S(1)}, u32[]{:S(2)}) copy-start(f32[8,128]{1,0:T(8,128)S(1)} %collective-permute-done.4.recv_ref) | copy-start | bytes 12292

commit v10 on v9

--- a/solution.py
+++ b/solution.py
@@ -84,7 +84,7 @@
     slot_count = cross_ref.shape[1]
     shift = lanes.bit_length() - 1
     rec_stack = jnp.concatenate(split_pieces3(view_ref[...]), axis=1)
-    cell_stack = jnp.concatenate(split_pieces3(cells_ref[...].astype(jnp.float32)), axis=1)
+    cell_stack = jnp.concatenate(split_pieces(cells_ref[...].astype(jnp.float32)), axis=1)
     faces = len(face_refs)
     width = faces * slot_count
     index = jnp.concatenate([cross_ref[face : face + 1, :] for face in range(faces)], axis=1)
@@ -107,7 +107,9 @@
     got = jnp.dot(rec_stack, lane_hot3, preferred_element_type=jnp.float32)
     got = got.reshape(outer, record_width, width)
     picked = jnp.sum(jnp.where(high_mask[:, None, :], got, 0.0), axis=0)
-    got_cell = jnp.dot(cell_stack, lane_hot3, preferred_element_type=jnp.float32)
+    got_cell = jnp.dot(
+        cell_stack, jnp.concatenate([lane_hot, lane_hot], axis=0), preferred_element_type=jnp.float32
+    )
     source = (jnp.sum(jnp.where(high_mask, got_cell, 0.0), axis=0, keepdims=True) + 0.5).astype(jnp.int32)
     height = lax.shift_right_logical(source, (CX * CY).bit_length() - 1)
     cell_x = jnp.bitwise_and(lax.shift_right_logical(source, CY.bit_length() - 1), CX - 1)

time: 42 us -> 41.9 us (level)
  no operation moved by 1% of the time
where the time goes in v10:
time: 41.9 us; the launch traced here: 41.6 us
  starting transfers between devices  20 us (48%)
  Pallas kernels  12.4 us (30%)
  waiting for transfers between devices  7.26 us (17%)
  local copies, waits for them, and re-layouts  1.18 us (3%)
  between operations  0.71 us (2%)
    ppermute x4, starting transfers between devices, shifted(): return lax.ppermute(value, axis, pairs)  17.7 us
    ppermute x1, waiting for transfers between devices, settle_and_solve(): received = lax.ppermute(message, 'gz', [(0, 1), (1, 0)])  7.25 us
    pallas_call x1, Pallas kernels, settle_residents(): pl.pallas_call(resident_kernel, grid=(drop_count // chunk,), out_shape=(j...  4.02 us
    pallas_call x1, Pallas kernels, settle_and_solve(): pl.pallas_call(arrive_solve_kernel, out_shape=(jax.ShapeDtypeStruct((len(...  3.43 us
    pallas_call x1, Pallas kernels, emit_faces(): pl.pallas_call(emit_kernel, out_shape=tuple((jax.ShapeDtypeStruct((record...  3.25 us
    ppermute x1, starting transfers between devices, settle_and_solve(): received = lax.ppermute(message, 'gz', [(0, 1), (1, 0)])  2.35 us
    pallas_call x1, Pallas kernels, settle_and_solve(): pl.pallas_call(correct_kernel, out_shape=(jax.ShapeDtypeStruct((rows, lan...  1.68 us
    unnamed x10, local copies, waits for them, and re-layouts  1.18 us
  transfers between devices with their start and end apart: 5, of which 1 were waited for; matrix products, arithmetic and copies ran while one was open for 0% of the time, Pallas kernels for 10%

profile of v10, /device:TPU:32, one launch (start us, length us, event | category | flops | bytes accessed | tf_op | source)
XLA Modules:
  0.0 41.6 jit_solution(3617368375635320500)
XLA Ops:
  0.6 3.3 %shard_map.129 = (f32[9,512]{1,0:T(8,128)}, f32[9,512]{1,0:T(8,128)}, f32[9,512]{1,0:T(8,128)}, f32[9,512]{1,0:T(8,128)}, f32[64,128]{1,0:T(8,128)}) custom-call(s32[4]{0:T(128)} %bitcast.24, f32[512,128]{1,0:T(8,128)} %bitcast.19, s32[64,128]{1,0:T(8,128)} %bitcast.21, s32[4,512]{1,0:T(4,128)} %bitcast.23), custom_call_target="tpu_custom_call" | custom-call | flops 14155776 | bytes 442368 | tf_op jit(solution)/shard_map/pallas_call | solution.py:138
  3.9 3.4 %collective-permute-start = (f32[9,512]{1,0:T(8,128)}, f32[9,512]{1,0:T(8,128)S(1)}, u32[]{:S(2)}, u32[]{:S(2)}) collective-permute-start(f32[9,512]{1,0:T(8,128)} %get-tuple-element.20), channel_id=1, source_target_pairs={{0,32},{32,64},{64,96},{96,128},{128,160},{160,192},{192,224},{224... | collective-permute-start | bytes 55304 | tf_op jit(solution)/shard_map/ppermute | solution.py:24
  7.3 6.4 %collective-permute-start.1 = (f32[9,512]{1,0:T(8,128)}, f32[9,512]{1,0:T(8,128)S(1)}, u32[]{:S(2)}, u32[]{:S(2)}) collective-permute-start(f32[9,512]{1,0:T(8,128)} %get-tuple-element.21), channel_id=1, source_target_pairs={{0,480},{32,0},{64,32},{96,64},{128,96},{160,128},{192,160},{224,1... | collective-permute-start | bytes 55304 | tf_op jit(solution)/shard_map/ppermute | solution.py:24
  13.6 0.0 collective-permute-start.2
  13.7 7.9 %collective-permute-start.3 = (f32[9,512]{1,0:T(8,128)}, f32[9,512]{1,0:T(8,128)S(1)}, u32[]{:S(2)}, u32[]{:S(2)}) collective-permute-start(f32[9,512]{1,0:T(8,128)} %get-tuple-element.23), channel_id=1, source_target_pairs={{0,30},{2,0},{4,2},{6,4},{8,6},{10,8},{12,10},{14,12},{16,14},{18,... | collective-permute-start | bytes 55304 | tf_op jit(solution)/shard_map/ppermute | solution.py:24
  21.6 4.0 %shard_map.130 = (f32[8,8192]{1,0:T(8,128)}, f32[128,128]{1,0:T(8,128)}) custom-call(f32[8,8192]{1,0:T(8,128)} %bitcast.20, s32[1,8192]{1,0:T(1,128)} %bitcast.22, f32[1,8192]{1,0:T(1,128)} %bitcast.31, f32[128,128]{1,0:T(8,128)} %bitcast.25), custom_call_target="tpu_custom_call" | custom-call | flops 1610612736 | bytes 589824 | tf_op jit(solution)/shard_map/pallas_call | solution.py:234
  25.6 0.0 collective-permute-done.w_ref
  25.6 0.0 copy-start.1
  25.6 0.0 collective-permute-done.1.e_ref
  25.6 0.0 copy-start.2
  25.6 0.0 collective-permute-done.2.s_ref
  25.6 0.0 copy-start.3
  25.7 0.0 collective-permute-done.3.n_ref
  25.7 0.0 copy-start.4
  25.7 0.6 %copy-done.1 = f32[9,512]{1,0:T(8,128)} copy-done((f32[9,512]{1,0:T(8,128)}, f32[9,512]{1,0:T(8,128)S(1)}, u32[]{:S(2)}) %copy-start.1) | copy-done | bytes 18456
  26.2 0.0 copy-done.2
  26.2 0.0 copy-done.3
  26.2 0.0 copy-done.4
  26.3 3.4 %shard_map.131 = (f32[4,8,512]{2,1,0:T(8,128)}, f32[128,128]{1,0:T(8,128)}, f32[128,128]{1,0:T(8,128)}, f32[8,128]{1,0:T(8,128)}, f32[4,128,128]{2,1,0:T(8,128)}) custom-call(s32[1]{0:T(128)} %bitcast.11.off_ref, f32[4,128]{1,0:T(4,128)} %bi_ref.1, f32[4,128]{1,0:T(4,128)} %fm_ref.1, f32[4,128]{1,0:T(4,128)} %bm_ref.1, f32[9,512]{1,0:T(8,128)} %copy-done.1, ...), custom_call_target="tpu_custom_call" | custom-call | flops 269090816 | bytes 802816 | tf_op jit(solution)/shard_map/pallas_call | solution.py:383
  29.7 2.4 %collective-permute-start.4 = (f32[8,128]{1,0:T(8,128)}, f32[8,128]{1,0:T(8,128)S(1)}, u32[]{:S(2)}, u32[]{:S(2)}) collective-permute-start(f32[8,128]{1,0:T(8,128)} %get-tuple-element.27.own_ref), channel_id=1, source_target_pairs={{0,1},{1,0},{2,3},{3,2},{4,5},{5,4},{6,7},{7,6},{8,9},{9,8},{10,11... | collective-permute-start | bytes 12296 | tf_op jit(solution)/shard_map/ppermute | solution.py:404
  32.1 7.2 %collective-permute-done.4.recv_ref = f32[8,128]{1,0:T(8,128)S(1)} collective-permute-done((f32[8,128]{1,0:T(8,128)}, f32[8,128]{1,0:T(8,128)S(1)}, u32[]{:S(2)}, u32[]{:S(2)}) %collective-permute-start.4) | collective-permute-done | bytes 4128 | tf_op jit(solution)/shard_map/ppermute | solution.py:404
  39.3 0.0 copy-start
  39.3 0.6 %copy-done = f32[8,128]{1,0:T(8,128)} copy-done((f32[8,128]{1,0:T(8,128)}, f32[8,128]{1,0:T(8,128)S(1)}, u32[]{:S(2)}) %copy-start) | copy-done | bytes 4120
  39.9 1.7 %shard_map.132 = (f32[128,128]{1,0:T(8,128)}, f32[128,128]{1,0:T(8,128)}) custom-call(f32[4,128,128]{2,1,0:T(8,128)} %get-tuple-element.26.coef_ref, f32[8,128]{1,0:T(8,128)} %get-tuple-element.27.own_ref, f32[8,128]{1,0:T(8,128)} %copy-done, f32[128,128]{1,0:T(8,128)} %get-tuple-element.28.sv_ref, f32[128,128]{1,0:T(8,128)} %get-tuple-element.29.sp_ref), custom_call_target="tpu_custom_call" | custom-call | flops 131072 | bytes 524288 | tf_op jit(solution)/shard_map/pallas_call | solution.py:405
Async XLA Ops:
  3.9 21.7 %collective-permute-start = (f32[9,512]{1,0:T(8,128)}, f32[9,512]{1,0:T(8,128)S(1)}, u32[]{:S(2)}, u32[]{:S(2)}) collective-permute-start(f32[9,512]{1,0:T(8,128)} %get-tuple-element.20), channel_id=1, source_target_pairs={{0,32},{32,64},{64,96},{96,128},{128,160},{160,192},{192,224},{224... | collective-permute-start | bytes 55304 | tf_op jit(solution)/shard_map/ppermute | solution.py:24
  7.3 18.3 %collective-permute-start.1 = (f32[9,512]{1,0:T(8,128)}, f32[9,512]{1,0:T(8,128)S(1)}, u32[]{:S(2)}, u32[]{:S(2)}) collective-permute-start(f32[9,512]{1,0:T(8,128)} %get-tuple-element.21), channel_id=1, source_target_pairs={{0,480},{32,0},{64,32},{96,64},{128,96},{160,128},{192,160},{224,1... | collective-permute-start | bytes 55304 | tf_op jit(solution)/shard_map/ppermute | solution.py:24
  13.6 12.0 %collective-permute-start.2 = (f32[9,512]{1,0:T(8,128)}, f32[9,512]{1,0:T(8,128)S(1)}, u32[]{:S(2)}, u32[]{:S(2)}) collective-permute-start(f32[9,512]{1,0:T(8,128)} %get-tuple-element.22), channel_id=1, source_target_pairs={{0,2},{2,4},{4,6},{6,8},{8,10},{10,12},{12,14},{14,16},{16,18},{18... | collective-permute-start | bytes 55304 | tf_op jit(solution)/shard_map/ppermute | solution.py:24
  13.7 12.0 %collective-permute-start.3 = (f32[9,512]{1,0:T(8,128)}, f32[9,512]{1,0:T(8,128)S(1)}, u32[]{:S(2)}, u32[]{:S(2)}) collective-permute-start(f32[9,512]{1,0:T(8,128)} %get-tuple-element.23), channel_id=1, source_target_pairs={{0,30},{2,0},{4,2},{6,4},{8,6},{10,8},{12,10},{14,12},{16,14},{18,... | collective-permute-start | bytes 55304 | tf_op jit(solution)/shard_map/ppermute | solution.py:24
  25.6 0.6 %copy-start.1 = (f32[9,512]{1,0:T(8,128)}, f32[9,512]{1,0:T(8,128)S(1)}, u32[]{:S(2)}) copy-start(f32[9,512]{1,0:T(8,128)S(1)} %collective-permute-done.w_ref) | copy-start | bytes 55300
  25.6 0.6 %copy-start.2 = (f32[9,512]{1,0:T(8,128)}, f32[9,512]{1,0:T(8,128)S(1)}, u32[]{:S(2)}) copy-start(f32[9,512]{1,0:T(8,128)S(1)} %collective-permute-done.1.e_ref) | copy-start | bytes 55300
  25.6 0.6 %copy-start.3 = (f32[9,512]{1,0:T(8,128)}, f32[9,512]{1,0:T(8,128)S(1)}, u32[]{:S(2)}) copy-start(f32[9,512]{1,0:T(8,128)S(1)} %collective-permute-done.2.s_ref) | copy-start | bytes 55300
  25.7 0.6 %copy-start.4 = (f32[9,512]{1,0:T(8,128)}, f32[9,512]{1,0:T(8,128)S(1)}, u32[]{:S(2)}) copy-start(f32[9,512]{1,0:T(8,128)S(1)} %collective-permute-done.3.n_ref) | copy-start | bytes 55300
  29.7 9.6 %collective-permute-start.4 = (f32[8,128]{1,0:T(8,128)}, f32[8,128]{1,0:T(8,128)S(1)}, u32[]{:S(2)}, u32[]{:S(2)}) collective-permute-start(f32[8,128]{1,0:T(8,128)} %get-tuple-element.27.own_ref), channel_id=1, source_target_pairs={{0,1},{1,0},{2,3},{3,2},{4,5},{5,4},{6,7},{7,6},{8,9},{9,8},{10,11... | collective-permute-start | bytes 12296 | tf_op jit(solution)/shard_map/ppermute | solution.py:404
  39.3 0.6 %copy-start = (f32[8,128]{1,0:T(8,128)}, f32[8,128]{1,0:T(8,128)S(1)}, u32[]{:S(2)}) copy-start(f32[8,128]{1,0:T(8,128)S(1)} %collective-permute-done.4.recv_ref) | copy-start | bytes 12292
